TPU v7x, 512 devices: a whole 4x4x16 slice. The times are simulated.
512 devices in a mesh: gx: 16 (over y_lo, x, core), gy: 32 (over y_hi, z).
Axes of the slice: x: 4, y: 4 (y_hi: 2, y_lo: 2; y = y_hi * 2 + y_lo), z: 16, core: 2. Of those that a mesh axis runs over, the one named last changes fastest.
Arguments:
- phase_field: float32 [16, 2048, 2048], P(None, 'gy', 'gx'), may hold values from -1 to 1
- mobility: float32 [16, 2048, 2048], P(None, 'gy', 'gx'), may hold values from 0.25 to 2.5
- x_inverse: bfloat16 [2048, 2048], P('gx'), may hold values from -2 to 2
- y_inverse: bfloat16 [2048, 2048], P('gy'), may hold values from -2 to 2
Outputs:
- new_phase: float32 [16, 2048, 2048], P(None, 'gy', 'gx')
All inputs are finite; a program needn't handle non-finite values.
Results may differ from a plain program's by a relative error of at most 0.0041.
Values may be sent and summed in bfloat16 or wider, within the bound.
No kernel may reach another device: no remote copies, remote signals or barrier semaphores. Data moves between devices by JAX's collectives and lax.ppermute only.
A program may use at most 64 MiB of HBM per device.

v0:
```python
import jax
import jax.numpy as jnp
from jax import lax
from jax.experimental import pallas as pl
from jax.experimental.pallas import tpu as pltpu
from jax.sharding import Mesh
from jax.sharding import PartitionSpec as P

GX = ("yl", "x", "c")
GY = ("yh", "z")

step_size = 0.15
F32 = jnp.float32
BF16 = jnp.bfloat16
NT = (((1,), (1,)), ((), ()))
VMEM = pl.BlockSpec(memory_space=pltpu.VMEM)
OFF = 8


def near(v):
    return pltpu.with_memory_space_constraint(v, pltpu.VMEM)


def away(v):
    return pltpu.with_memory_space_constraint(v, pltpu.HBM)


def kept(shape, dtype):
    return pltpu.VMEM(shape, dtype)


FAR = pl.BlockSpec(memory_space=pltpu.HBM)


def call(kernel, out_shape, args, scalar=None, scratch=(), far=(), far_out=()):
    scalars = [] if scalar is None else [scalar]
    many = isinstance(out_shape, tuple)
    return pl.pallas_call(
        kernel,
        out_shape=out_shape,
        in_specs=[pl.BlockSpec(memory_space=pltpu.SMEM)] * len(scalars) + [FAR if i in far else VMEM for i in range(len(args))],
        out_specs=tuple(FAR if i in far_out else VMEM for i in range(len(out_shape))) if many else VMEM,
        scratch_shapes=list(scratch),
        compiler_params=pltpu.CompilerParams(vmem_limit_bytes=16 << 20),
    )(*scalars, *[away(v) if i in far else near(v) for i, v in enumerate(args)])


def face_mob(p, q):
    return 2.0 * p * q / jnp.maximum(p + q, 0.25)


def turn(x, shift, axis):
    return pltpu.roll(x, shift % x.shape[axis], axis)


def places(shape, axis):
    return lax.broadcasted_iota(jnp.int32, shape, axis)


def pack_x_kernel(core_ref, p_hbm, m_hbm, x_hbm, y_hbm, left_ref, right_ref, p_ref, m_ref, part_hbm, first_ref, last_ref, sems):
    planes, _, cx = p_ref.shape
    pairs = planes // 2
    rows = part_hbm.shape[0]
    copies = (
        (y_hbm.at[pl.ds(pl.multiple_of(core_ref[0] * rows, rows), rows)], part_hbm),
        (p_hbm, p_ref),
        (m_hbm, m_ref),
        (x_hbm.at[pl.ds(0, 16)], first_ref),
        (x_hbm.at[pl.ds(x_hbm.shape[0] - 16, 16)], last_ref),
    )
    copies = [pltpu.make_async_copy(src, dst, sems.at[i]) for i, (src, dst) in enumerate(copies)]
    for copy in copies:
        copy.start()
    for a, ref in enumerate((p_ref, m_ref)):
        copies[1 + a].wait()
        for i in range(pairs):
            t = jnp.concatenate([ref[i], ref[i + pairs]], axis=0).T
            for j in range(2):
                k = (2 * a + j) * pairs + i
                left_ref[k : k + 1, :] = t[j : j + 1]
                right_ref[k : k + 1, :] = t[cx - 2 + j : cx - 1 + j]
    base = 4 * pairs
    copies[3].wait()
    copies[4].wait()
    first = first_ref[0:1, :].astype(F32)
    last = last_ref[15:16, :].astype(F32)
    for s in range(16):
        left_ref[base + s : base + s + 1, :] = first[:, s * cx : (s + 1) * cx]
        right_ref[base + s : base + s + 1, :] = last[:, s * cx : (s + 1) * cx]
    copies[0].wait()


def strip(x, cy):
    both = jnp.concatenate([turn(x, OFF, 1), turn(x, OFF - cy, 1)], axis=0)
    lane = places(both.shape, 1)
    return jnp.where((lane >= OFF) & (lane < OFF + cy), both, 0.0)


def received(left_ref, right_ref, a, pairs, cy):
    refs = ((left_ref, 2 * a), (left_ref, 2 * a + 1), (right_ref, 2 * a), (right_ref, 2 * a + 1))
    return [strip(ref[k * pairs : (k + 1) * pairs, :], cy) for ref, k in refs]


def pack_y_kernel(p_ref, m_ref, left_ref, right_ref, up_ref, down_ref):
    planes, cy, cx = p_ref.shape
    for a, ref in enumerate((p_ref, m_ref)):
        for r in range(3):
            up_ref[3 * a + r] = ref[:, cy - 3 + r, :]
            down_ref[3 * a + r] = ref[:, r, :]
    lane = places((planes, cx), 1)
    up = jnp.zeros((planes, cx), F32)
    down = up
    for a in range(2):
        for j, s in enumerate(received(left_ref, right_ref, a, planes // 2, cy)):
            at = 3 * (4 * a + j)
            here = (lane >= at) & (lane < at + 3)
            up = jnp.where(here, turn(s, at - (OFF + cy - 3), 1), up)
            down = jnp.where(here, turn(s, at - OFF, 1), down)
    up_ref[6] = up
    down_ref[6] = down


def explicit_kernel(
    p_ref, m_ref, own_l_ref, own_r_ref, left_ref, right_ref, up_ref, down_ref,
    send_ref, fz_ref, fy_ref, fx_ref, edge_ref,
    v_ref, c_ref, f_ref, side_ref, rim_ref,
):
    planes, cy, cx = p_ref.shape
    pairs = planes // 2
    tall = cy + 2 * OFF
    lane = places((planes, cx), 1)
    plane = places((planes, cx), 0)

    def strips(a):
        out = []
        for j, s in enumerate(received(left_ref, right_ref, a, pairs, cy)):
            at = 3 * (4 * a + j)
            s = jnp.where((lane >= OFF - 3) & (lane < OFF), turn(up_ref[6], OFF - 3 - at, 1), s)
            s = jnp.where((lane >= OFF + cy) & (lane < OFF + cy + 3), turn(down_ref[6], OFF + cy - at, 1), s)
            out.append(s)
        own = []
        for ref, j, at in ((own_l_ref, 0, 0), (own_l_ref, 1, 1), (own_r_ref, 0, cx - 2), (own_r_ref, 1, cx - 1)):
            k = 2 * a + j
            s = strip(ref[k * pairs : (k + 1) * pairs, :], cy)
            for r in (1, 2):
                s = jnp.where(lane == OFF - 3 + r, turn(up_ref[3 * a + r], OFF - 3 + r - at, 1), s)
            for r in (0, 1):
                s = jnp.where(lane == OFF + cy + r, turn(down_ref[3 * a + r], OFF + cy + r - at, 1), s)
            own.append(s)
        return out[:2] + own[:2], own[2:] + out[2:]

    def strip_first(v, m, vl, ml, vr, mr):
        above = jnp.where(plane == planes - 1, 0.0, turn(m, -1, 0))
        fz = face_mob(m, above)
        gz = fz * (turn(v, -1, 0) - v)
        fy = face_mob(m, turn(m, -1, 1))
        gy = fy * (turn(v, -1, 1) - v)
        lap = gz - jnp.where(plane == 0, 0.0, turn(gz, 1, 0)) + gy - turn(gy, 1, 1)
        lap = lap + face_mob(m, mr) * (vr - v) + face_mob(m, ml) * (vl - v)
        return v + step_size * lap

    columns = []
    for side, (v, m) in enumerate(zip(strips(0), strips(1), strict=True)):
        f = face_mob(m[1], m[2])
        a = strip_first(v[1], m[1], v[0], m[0], v[2], m[2])
        b = strip_first(v[2], m[2], v[1], m[1], v[3], m[3])
        columns += [f * (v[2] - v[1]), f * (b - a)]
        side_ref[...] = f
        even = turn(side_ref[pl.ds(0, pairs, stride=2), :], -OFF, 1)
        odd = turn(side_ref[pl.ds(1, pairs, stride=2), :], cy - OFF, 1)
        edge_ref[side * pairs : (side + 1) * pairs, :] = jnp.where(lane[:pairs] < cy, even, odd)
    stacked = jnp.concatenate(columns + [jnp.zeros((cx - 4 * planes, cx), F32)], axis=0)
    across = stacked.T[:tall]

    def column(k, z):
        at = k * planes + z
        return jnp.broadcast_to(across[:, at : at + 1], (tall, cx))

    blank = jnp.zeros((OFF, cx), F32)
    for ref in (v_ref, c_ref, f_ref):
        for z in (0, planes + 1):
            ref[z * tall : (z + 1) * tall, :] = jnp.zeros((tall, cx), F32)
    for ref, a, field in ((v_ref, 0, p_ref), (c_ref, 1, m_ref)):
        for z in range(planes):
            base = (z + 1) * tall
            ref[base : base + OFF, :] = blank
            ref[base + OFF : base + OFF + cy, :] = field[z]
            ref[base + OFF + cy : base + tall, :] = blank
        for r in range(3):
            ref[pl.ds(tall + OFF - 3 + r, planes, stride=tall), :] = up_ref[3 * a + r]
            ref[pl.ds(tall + OFF + cy + r, planes, stride=tall), :] = down_ref[3 * a + r]

    wide = places((tall, cx), 1)

    def step(v, above, fz, fy, fx, gz_before, gl, gr):
        gz = fz * (above - v)
        gy = fy * (turn(v, -1, 0) - v)
        gx = jnp.where(wide == 0, gl, fx * (v - turn(v, 1, 1)))
        lap = gz - gz_before + gy - turn(gy, 1, 0)
        lap = lap + jnp.where(wide == cx - 1, gr, turn(gx, -1, 1)) - gx
        return v + step_size * lap, gz

    fz_ref[:tall, :] = jnp.zeros((tall, cx), F32)
    before = jnp.zeros((tall, cx), F32)
    for z in range(planes):
        here, above = pl.ds((z + 1) * tall, tall), pl.ds((z + 2) * tall, tall)
        flat = pl.ds(z * tall, tall)
        m = c_ref[here, :]
        fz = face_mob(m, c_ref[above, :])
        fy = face_mob(m, turn(m, -1, 0))
        fx = face_mob(m, turn(m, 1, 1))
        fz_ref[here, :] = fz
        fy_ref[flat, :] = fy
        fx_ref[flat, :] = fx
        out, before = step(v_ref[here, :], v_ref[above, :], fz, fy, fx, before, column(0, z), column(2, z))
        f_ref[here, :] = out

    rim_ref[...] = jnp.zeros(rim_ref.shape, F32)
    before = jnp.zeros((tall, cx), F32)
    quarter = planes // 4
    for z in range(planes):
        here, above = pl.ds((z + 1) * tall, tall), pl.ds((z + 2) * tall, tall)
        flat = pl.ds(z * tall, tall)
        out, before = step(
            f_ref[here, :], f_ref[above, :], fz_ref[here, :], fy_ref[flat, :], fx_ref[flat, :],
            before, column(1, z), column(3, z),
        )
        q, at = z // quarter, z % quarter
        body = out[OFF : OFF + cy].astype(BF16)
        for x in range(4):
            send_ref[(q // 2) * 8 + x * 2 + q % 2, at * cy : (at + 1) * cy, :] = body
        rim_ref[q, 2 * at : 2 * at + 1, :] = out[OFF - 1 : OFF]
        rim_ref[q, 2 * at + 1 : 2 * at + 2, :] = out[OFF + cy : OFF + cy + 1]
    for q in range(4):
        rims = rim_ref[q].astype(BF16)
        for x in range(4):
            send_ref[(q // 2) * 8 + x * 2 + q % 2, quarter * cy :, :] = rims


def solve_x_kernel(block_ref, got_ref, x0_ref, x1_ref, x2_ref, x3_ref, out_ref):
    own = block_ref[0]
    parts, lines, cx = got_ref.shape
    main = lines - 16
    a = jnp.concatenate([got_ref[s] for s in range(parts)], axis=1)
    for other, x_ref in enumerate((x0_ref, x1_ref, x2_ref, x3_ref)):
        block = own ^ other
        m = lax.dot_general(a, x_ref[:cx], NT, preferred_element_type=F32)
        out_ref[block, : main + 8] = m[: main + 8]
        e = lax.dot_general(x_ref[cx:], a[:main], NT, preferred_element_type=F32)
        out_ref[block, main + 8 : main + 12] = e[:4, :cx]
        out_ref[block, main + 12 :] = e[:4, cx:]


def implicit_kernel(back_ref, fz_ref, fy_ref, fx_ref, edge_ref, out_ref, c_ref, e_ref):
    planes, cy, cx = out_ref.shape
    tall = cy + 2 * OFF
    quarter, pairs = planes // 4, planes // 2
    main = quarter * cy

    def chemical(s):
        return s * s * s - s

    for z in (0, planes + 1):
        c_ref[z * tall : (z + 1) * tall, :] = jnp.zeros((tall, cx), F32)
    for q in range(4):
        e_ref[q * 8 : (q + 1) * 8, :] = chemical(back_ref[q, main + 8 : main + 16])
        rims = chemical(back_ref[q, main : main + 8])
        for at in range(quarter):
            base = (q * quarter + at + 1) * tall
            c_ref[base + OFF : base + OFF + cy, :] = chemical(back_ref[q, at * cy : (at + 1) * cy])
            c_ref[base + OFF - 1 : base + OFF, :] = rims[2 * at : 2 * at + 1]
            c_ref[base + OFF + cy : base + OFF + cy + 1, :] = rims[2 * at + 1 : 2 * at + 2]
    ends = [e_ref[pl.ds(j, pairs, stride=4), :] for j in range(4)]
    left = edge_ref[:pairs, :] * (ends[1] - ends[0])
    right = edge_ref[pairs:, :] * (ends[3] - ends[2])
    across = jnp.concatenate([left, right, jnp.zeros((cx - planes, cx), F32)], axis=0).T
    lane = places((cy, cx), 1)
    before = jnp.zeros((cy, cx), F32)
    for z in range(planes):
        base = (z + 1) * tall + OFF
        flat = z * tall + OFF
        c = c_ref[base : base + cy, :]
        gz = fz_ref[base : base + cy, :] * (c_ref[base + tall : base + tall + cy, :] - c)
        gy = fy_ref[flat : flat + cy, :] * (c_ref[base + 1 : base + 1 + cy, :] - c)
        gu = fy_ref[flat - 1 : flat - 1 + cy, :] * (c - c_ref[base - 1 : base - 1 + cy, :])
        rows = slice((z % 2) * cy, (z % 2 + 1) * cy)
        gl = jnp.broadcast_to(across[rows, z // 2 : z // 2 + 1], (cy, cx))
        gr = jnp.broadcast_to(across[rows, pairs + z // 2 : pairs + z // 2 + 1], (cy, cx))
        gx = jnp.where(lane == 0, gl, fx_ref[flat : flat + cy, :] * (c - turn(c, 1, 1)))
        lap = gz - before + gy - gu + jnp.where(lane == cx - 1, gr, turn(gx, -1, 1)) - gx
        s = back_ref[z // quarter, (z % quarter) * cy : (z % quarter + 1) * cy]
        out_ref[z] = (s + step_size * lap).astype(BF16)
        before = gz


def solve_y_near_kernel(side_ref, y_hbm, u_ref, sum_ref, y_ref, sem):
    high = side_ref[0]
    half, _ = u_ref.shape
    copy = pltpu.make_async_copy(y_hbm, y_ref, sem)
    copy.start()
    copy.wait()
    y0 = y_ref[:, pl.ds(pl.multiple_of(high * half, half), half)]
    sum_ref[...] = jnp.dot(y0, u_ref[...], preferred_element_type=F32)


def solve_y_far_kernel(side_ref, sum_ref, y_ref, o_ref, u0_ref, u1_ref, out_ref):
    high, core = side_ref[0], side_ref[1]
    half, cx = u0_ref.shape
    k0 = pl.ds(pl.multiple_of(high * half, half), half)
    k1 = pl.ds(pl.multiple_of((1 - high) * half, half), half)
    mine = sum_ref[...] + jnp.dot(y_ref[:, k1], u1_ref[...], preferred_element_type=F32)
    other = jnp.dot(o_ref[:, k0], u0_ref[...], preferred_element_type=F32)
    other = other + jnp.dot(o_ref[:, k1], u1_ref[...], preferred_element_type=F32)
    parts, cy, _ = out_ref.shape
    rows = cy // 2
    out_ref[:, pl.ds(pl.multiple_of(core * rows, rows), rows), :] = mine.astype(BF16).reshape(parts, rows, cx)
    out_ref[:, pl.ds(pl.multiple_of((1 - core) * rows, rows), rows), :] = other.astype(BF16).reshape(parts, rows, cx)


def pack_x(core, p, m, x_inverse, y_inverse):
    cx = p.shape[2]
    shape = (2 * p.shape[0] + 16, cx)
    cy, order = y_inverse.shape
    out = (kept(shape, F32),) * 2 + (kept(p.shape, F32),) * 2 + (jax.ShapeDtypeStruct((cy // 2, order), BF16),)
    rows = pltpu.VMEM((16, order), BF16)
    scratch = (rows, rows, pltpu.SemaphoreType.DMA((5,)))
    return call(pack_x_kernel, out, (p, m, x_inverse, y_inverse), core, scratch, range(4), (4,))


def pack_y(p, m, left, right):
    shape = (7, p.shape[0], p.shape[2])
    return call(pack_y_kernel, (kept(shape, F32),) * 2, (p, m, left, right))


def explicit(*args):
    planes, cy, cx = args[0].shape
    tall = cy + 2 * OFF
    lines = planes // 4 * cy + 16
    field = pltpu.VMEM(((planes + 2) * tall, cx), F32)
    out = (
        kept((16, lines, cx), BF16),
        kept(((planes + 1) * tall, cx), F32),
        kept((planes * tall, cx), F32),
        kept((planes * tall, cx), F32),
        kept((planes, cx), F32),
    )
    scratch = (field, field, field, pltpu.VMEM((planes, cx), F32), pltpu.VMEM((4, 16, cx), F32))
    return call(explicit_kernel, out, args, scratch=scratch)


def solve_x(block, got, x_blocks):
    _, lines, cx = got.shape
    return call(solve_x_kernel, kept((4, lines, cx), F32), (got, *x_blocks), scalar=block)


def implicit(back, faces, planes, cy):
    cx = back.shape[2]
    scratch = (pltpu.VMEM(((planes + 2) * (cy + 2 * OFF), cx), F32), pltpu.VMEM((32, cx), F32))
    return call(implicit_kernel, kept((planes, cy, cx), BF16), (back, *faces), scratch=scratch)


def solve_y_near(side, y, u):
    out = (kept((y.shape[0], u.shape[1]), F32), kept(y.shape, BF16))
    return call(solve_y_near_kernel, out, (y, u), side, (pltpu.SemaphoreType.DMA(()),), (0,))


def solve_y_far(side, *parts):
    half, cx = parts[-1].shape
    return call(solve_y_far_kernel, kept((16, half // 16, cx), BF16), parts, side)


def both_ways(to_before, to_after, axis):
    size = lax.axis_size(axis)
    up = [(i, i + 1) for i in range(size - 1)]
    return lax.ppermute(to_after, axis, up), lax.ppermute(to_before, axis, [(j, i) for i, j in up])


def local(phase_field, mobility, x_inverse, y_inverse):
    planes, cy, cx = phase_field.shape
    order = y_inverse.shape[1]
    half = order // 2
    core, low, high = lax.axis_index("c"), lax.axis_index("yl"), lax.axis_index("yh")
    swap = [(0, 1), (1, 0)]

    one = lambda v: v.reshape(1).astype(jnp.int32)

    own_l, own_r, phase_field, mobility, y_part = pack_x(one(core), phase_field, mobility, x_inverse, y_inverse)
    y_mine = lax.all_gather(y_part, "z", axis=0, tiled=True)
    left, right = both_ways(own_l, own_r, GX)
    to_up, to_down = pack_y(phase_field, mobility, left, right)

    row_before = left[-16:].reshape(1, order).astype(BF16)
    row_after = right[-16:].reshape(1, order).astype(BF16)
    row_before, row_after, to_up = lax.optimization_barrier((row_before, row_after, to_up))
    ends = [x_inverse, row_before, x_inverse[:1], x_inverse[-1:], row_after, jnp.zeros((12, order), BF16)]
    up, down = both_ways(to_down, to_up, GY)
    rows = jnp.concatenate(ends, axis=0)
    rows_yl = lax.ppermute(rows, "yl", swap)
    x_blocks = (rows, lax.ppermute(rows, "c", swap), rows_yl, lax.ppermute(rows_yl, "c", swap))

    send, *faces = explicit(phase_field, mobility, own_l, own_r, left, right, up, down)
    got = lax.all_to_all(send, GX, 0, 0, tiled=True)
    back = solve_x(one(low * 2 + core), got, x_blocks)
    back = lax.all_to_all(back, ("yl", "c"), 0, 0, tiled=True)
    updated = implicit(back, faces, planes, cy)

    mine = lax.all_to_all(updated, "z", 0, 0, tiled=True).reshape(half, cx)
    y_mine, mine = lax.optimization_barrier((y_mine, mine))
    theirs = lax.ppermute(mine, "yh", swap)
    side = jnp.concatenate([one(high), one(core)])
    part, y_mine = solve_y_near(side, y_mine, mine)
    y_other = lax.ppermute(y_mine, "c", swap)
    out = solve_y_far(side, part, y_mine, y_other, mine, theirs)
    out = lax.all_to_all(out, "z", 0, 0, tiled=True)
    return out.astype(F32)


def solution(mesh):
    shape = (2, mesh.shape["gx"] // 4, 2, 2, mesh.shape["gy"] // 2)
    torus = Mesh(mesh.devices.reshape(shape), ("yl", "x", "c", "yh", "z"))
    in_specs = (P(None, GY, GX), P(None, GY, GX), P(GX, None), P(GY, None))
    return jax.shard_map(local, mesh=torus, in_specs=in_specs, out_specs=P(None, GY, GX), check_vma=False)
```

profile of v0, /device:TPU:16, one launch (start us, length us, event | category | flops | bytes accessed | tf_op | source)
XLA Modules:
  0.0 163.7 jit_solution(566873113803081870)
XLA Ops:
  6.5 5.1 %shard_map.46 = (f32[48,128]{1,0:T(8,128)S(1)}, f32[48,128]{1,0:T(8,128)S(1)}, f32[16,64,128]{2,1,0:T(8,128)S(1)}, f32[16,64,128]{2,1,0:T(8,128)S(1)}, bf16[32,2048]{1,0:T(8,128)(2,1)}) custom-call(s32[1]{0:T(128)} %bitcast.1.core_ref, f32[16,64,128]{2,1,0:T(8,128)} %p_hbm.1, f32[16,64,128]{2,1,0:T(8,128)} %m_hbm.1, bf16[128,2048]{1,0:T(8,128)(2,1)} %x_hbm.1, ...), custom_call_target="tpu_custom_call" | custom-call | tf_op jit(solution)/shard_map/pallas_call | solution.py:38
  11.7 0.0 all-gather.2.cloned.1.call-update
  11.7 1.7 %collective-permute-start = (f32[48,128]{1,0:T(8,128)S(1)}, f32[48,128]{1,0:T(8,128)S(1)}, u32[]{:S(2)}, u32[]{:S(2)}) collective-permute-start(f32[48,128]{1,0:T(8,128)S(1)} %get-tuple-element.28.own_r_ref), channel_id=1, source_target_pairs={{0,32},{32,64},{64,96},{96,128},{128,160},{160,192},{192,224},{224... | collective-permute-start | bytes 73736 | tf_op jit(solution)/shard_map/ppermute | solution.py:375
  13.4 1.3 collective-permute-start.1
  14.7 0.8 fusion.2
  15.5 2.3 %collective-permute-done.1.right_ref = f32[48,128]{1,0:T(8,128)S(1)} collective-permute-done((f32[48,128]{1,0:T(8,128)S(1)}, f32[48,128]{1,0:T(8,128)S(1)}, u32[]{:S(2)}, u32[]{:S(2)}) %collective-permute-start.1) | collective-permute-done | bytes 24608 | tf_op jit(solution)/shard_map/ppermute | solution.py:375
  17.9 0.2 shard_map.47
  18.0 0.4 concatenate.7.x0_ref
  18.5 6.3 %collective-permute-start.5 = (bf16[144,2048]{1,0:T(8,128)(2,1)S(1)}, bf16[144,2048]{1,0:T(8,128)(2,1)}, u32[]{:S(2)}, u32[]{:S(2)}) collective-permute-start(bf16[144,2048]{1,0:T(8,128)(2,1)S(1)} %concatenate.7.x0_ref), channel_id=1, source_target_pairs={{0,256},{256,0},{1,257},{257,1},{2,258},{258,2},{3,259},{259,3},{4... | collective-permute-start | bytes 1769480 | tf_op jit(solution)/shard_map/ppermute | solution.py:398
  24.7 3.8 %collective-permute-start.2 = (f32[7,16,128]{2,1,0:T(8,128)S(1)}, f32[7,16,128]{2,1,0:T(8,128)S(1)}, u32[]{:S(2)}, u32[]{:S(2)}) collective-permute-start(f32[7,16,128]{2,1,0:T(8,128)S(1)} %get-tuple-element.30), channel_id=1, source_target_pairs={{0,1},{1,2},{2,3},{3,4},{4,5},{5,6},{6,7},{7,8},{8,9},{9,10},{10,1... | collective-permute-start | bytes 172040 | tf_op jit(solution)/shard_map/ppermute | solution.py:375
  28.6 9.6 %collective-permute-start.3 = (f32[7,16,128]{2,1,0:T(8,128)S(1)}, f32[7,16,128]{2,1,0:T(8,128)S(1)}, u32[]{:S(2)}, u32[]{:S(2)}) collective-permute-start(f32[7,16,128]{2,1,0:T(8,128)S(1)} %get-tuple-element.31), channel_id=1, source_target_pairs={{1,0},{2,1},{3,2},{4,3},{5,4},{6,5},{7,6},{8,7},{9,8},{10,9},{11,1... | collective-permute-start | bytes 172040 | tf_op jit(solution)/shard_map/ppermute | solution.py:375
  38.1 0.7 collective-permute-done.2.up_ref
  38.9 1.5 collective-permute-done.3.down_ref
  40.3 5.0 %shard_map.48 = (bf16[16,272,128]{2,1,0:T(8,128)(2,1)}, f32[1360,128]{1,0:T(8,128)S(1)}, f32[1280,128]{1,0:T(8,128)S(1)}, f32[1280,128]{1,0:T(8,128)S(1)}, f32[16,128]{1,0:T(8,128)S(1)}) custom-call(f32[16,64,128]{2,1,0:T(8,128)S(1)} %get-tuple-element.25.p_ref, f32[16,64,128]{2,1,0:T(8,128)S(1)} %get-tuple-element.26.m_ref, ...), custom_call_target="tpu_custom_call" | custom-call | tf_op jit(solution)/shard_map/pallas_call | solution.py:38
  45.3 0.8 copy-done
  46.2 4.5 %all-to-all-start = ((bf16[16,272,128]{2,1,0:T(8,128)(2,1)}), bf16[16,272,128]{2,1,0:T(8,128)(2,1)S(1)}, u32[]{:S(2)}, u32[]{:S(2)}) async-start(bf16[16,272,128]{2,1,0:T(8,128)(2,1)} %get-tuple-element.32), calls=%async_computation | async-start | bytes 2228224 | tf_op jit(solution)/shard_map/all_to_all | solution.py:402
  50.7 2.3 %collective-permute-start.4 = (bf16[144,2048]{1,0:T(8,128)(2,1)S(1)}, bf16[144,2048]{1,0:T(8,128)(2,1)}, u32[]{:S(2)}, u32[]{:S(2)}) collective-permute-start(bf16[144,2048]{1,0:T(8,128)(2,1)S(1)} %concatenate.7.x0_ref), channel_id=1, source_target_pairs={{0,32},{32,0},{1,33},{33,1},{2,34},{34,2},{3,35},{35,3},{4,36},{36... | collective-permute-start | bytes 1769480 | tf_op jit(solution)/shard_map/ppermute | solution.py:399
  53.0 2.0 %collective-permute-start.6 = (bf16[144,2048]{1,0:T(8,128)(2,1)}, bf16[144,2048]{1,0:T(8,128)(2,1)}, u32[]{:S(2)}, u32[]{:S(2)}) collective-permute-start(bf16[144,2048]{1,0:T(8,128)(2,1)} %collective-permute-done.5.x2_ref), channel_id=1, source_target_pairs={{0,32},{32,0},{1,33},{33,1},{2,34},{34,2},{3,35},{35,3},{4,36},{36... | collective-permute-start | bytes 1769480 | tf_op jit(solution)/shard_map/ppermute | solution.py:399
  55.1 12.8 %all-to-all-done.got_ref = bf16[16,272,128]{2,1,0:T(8,128)(2,1)S(1)} async-done(((bf16[16,272,128]{2,1,0:T(8,128)(2,1)}), bf16[16,272,128]{2,1,0:T(8,128)(2,1)S(1)}, u32[]{:S(2)}, u32[]{:S(2)}) %all-to-all-start) | async-done | bytes 1114144 | tf_op jit(solution)/shard_map/all_to_all | solution.py:402
  67.9 3.8 %shard_map.49 = f32[4,272,128]{2,1,0:T(8,128)S(1)} custom-call(s32[1]{0:T(128)} %bitcast.2.block_ref, bf16[16,272,128]{2,1,0:T(8,128)(2,1)S(1)} %all-to-all-done.got_ref, bf16[144,2048]{1,0:T(8,128)(2,1)S(1)} %concatenate.7.x0_ref, bf16[144,2048]{1,0:T(8,128)(2,1)} %collective-permute-done.4.x1_ref, bf16[144,2048]{1,0:T(8,128)(2,1)} %collective-permute-done.5.x2_ref, ...), custom_call_target="tpu_custom_call" | custom-call | tf_op jit(solution)/shard_map/pallas_call | solution.py:38
  71.7 11.5 %all_to_all.20.back_ref = f32[4,272,128]{2,1,0:T(8,128)S(1)} all-to-all(f32[4,272,128]{2,1,0:T(8,128)S(1)} %shard_map.49), channel_id=1, replica_groups=mesh['yl'=2,'x'=4,'c'=2,'yh'=2,'z'=16] {'yl','c'}, dimensions={0} | all-to-all | bytes 1114112 | tf_op jit(solution)/shard_map/all_to_all | solution.py:404
  83.2 2.3 %shard_map.50 = bf16[16,64,128]{2,1,0:T(8,128)(2,1)} custom-call(f32[4,272,128]{2,1,0:T(8,128)S(1)} %all_to_all.20.back_ref, f32[1360,128]{1,0:T(8,128)S(1)} %get-tuple-element.35.fz_ref, f32[1280,128]{1,0:T(8,128)S(1)} %get-tuple-element.36.fy_ref, f32[1280,128]{1,0:T(8,128)S(1)} %copy-done.1, f32[16,128]{1,0:T(8,128)S(1)} %get-tuple-element.38.edge_ref), custom_call_target="tpu_custom_call" | custom-call | tf_op jit(solution)/shard_map/pallas_call | solution.py:38
  85.5 9.6 %all-to-all-start.2 = ((bf16[16,64,128]{2,1,0:T(8,128)(2,1)}), bf16[16,64,128]{2,1,0:T(8,128)(2,1)S(1)}, u32[]{:S(2)}, u32[]{:S(2)}) async-start(bf16[16,64,128]{2,1,0:T(8,128)(2,1)} %shard_map.50), calls=%async_computation.2 | async-start | bytes 524288 | tf_op jit(solution)/shard_map/all_to_all | solution.py:407
  95.2 0.1 pad_add_fusion.side_ref
  95.2 18.4 %all-to-all-done.2 = bf16[16,64,128]{2,1,0:T(8,128)(2,1)S(1)} async-done(((bf16[16,64,128]{2,1,0:T(8,128)(2,1)}), bf16[16,64,128]{2,1,0:T(8,128)(2,1)S(1)}, u32[]{:S(2)}, u32[]{:S(2)}) %all-to-all-start.2) | async-done | bytes 262176 | tf_op jit(solution)/shard_map/all_to_all | solution.py:407
  113.7 2.6 %shard_map.51 = (f32[512,128]{1,0:T(8,128)S(1)}, bf16[512,2048]{1,0:T(8,128)(2,1)S(1)}) custom-call(s32[2]{0:T(128)S(1)} %pad_add_fusion.side_ref, bf16[512,2048]{1,0:T(8,128)(2,1)} %all-gather.2.cloned.1.call-done.y_hbm, bf16[1024,128]{1,0:T(8,128)(2,1)S(1)} %bitcast.16), custom_call_target="tpu_custom_call" | custom-call | tf_op jit(solution)/shard_map/pallas_call | solution.py:38
  116.2 1.9 %collective-permute-start.7 = (bf16[512,2048]{1,0:T(8,128)(2,1)S(1)}, bf16[512,2048]{1,0:T(8,128)(2,1)S(1)}, u32[]{:S(2)}, u32[]{:S(2)}) collective-permute-start(bf16[512,2048]{1,0:T(8,128)(2,1)S(1)} %get-tuple-element.42.y_ref), channel_id=1, source_target_pairs={{0,32},{32,0},{1,33},{33,1},{2,34},{34,2},{3,35},{35,3},{4,36},{36... | collective-permute-start | bytes 6291464 | tf_op jit(solution)/shard_map/ppermute | solution.py:412
  118.2 2.5 %collective-permute-start.8 = (bf16[1024,128]{1,0:T(8,128)(2,1)S(1)}, bf16[1024,128]{1,0:T(8,128)(2,1)S(1)}, u32[]{:S(2)}, u32[]{:S(2)}) collective-permute-start(bf16[1024,128]{1,0:T(8,128)(2,1)S(1)} %bitcast.17), channel_id=1, source_target_pairs={{0,16},{16,0},{1,17},{17,1},{2,18},{18,2},{3,19},{19,3},{4,20},{20... | collective-permute-start | bytes 786440 | tf_op jit(solution)/shard_map/ppermute | solution.py:409
  120.7 9.6 %collective-permute-done.8.u1_ref = bf16[1024,128]{1,0:T(8,128)(2,1)S(1)} collective-permute-done((bf16[1024,128]{1,0:T(8,128)(2,1)S(1)}, bf16[1024,128]{1,0:T(8,128)(2,1)S(1)}, u32[]{:S(2)}, u32[]{:S(2)}) %collective-permute-start.8) | collective-permute-done | bytes 262176 | tf_op jit(solution)/shard_map/ppermute | solution.py:409
  130.3 1.5 shard_map.52
  131.8 24.2 %all_to_all.21 = bf16[16,64,128]{2,1,0:T(8,128)(2,1)S(1)} all-to-all(bf16[16,64,128]{2,1,0:T(8,128)(2,1)S(1)} %shard_map.52), channel_id=1, replica_groups=mesh['yl'=2,'x'=4,'c'=2,'yh'=2,'z'=16] {'z'}, dimensions={0} | all-to-all | bytes 524288 | tf_op jit(solution)/shard_map/all_to_all | solution.py:414
  156.0 0.8 convert_element_type.29
  (17 shorter events, 0.1 us)
Async XLA Ops:
  6.5 11.5 %copy-start.2 = (bf16[128,2048]{1,0:T(8,128)(2,1)S(1)}, bf16[128,2048]{1,0:T(8,128)(2,1)}, u32[]{:S(2)}) copy-start(bf16[128,2048]{1,0:T(8,128)(2,1)} %x_hbm.1) | copy-start | bytes 1572868
  6.5 107.1 %all-gather.2.cloned.1.call-start = ((), (), s32[]{:S(2)}) async-start(), calls=%async_computation.4 | async-start | bytes 2228224 | tf_op jit(solution)/shard_map/all_gather | solution.py:388
  11.7 6.1 %collective-permute-start = (f32[48,128]{1,0:T(8,128)S(1)}, f32[48,128]{1,0:T(8,128)S(1)}, u32[]{:S(2)}, u32[]{:S(2)}) collective-permute-start(f32[48,128]{1,0:T(8,128)S(1)} %get-tuple-element.28.own_r_ref), channel_id=1, source_target_pairs={{0,32},{32,64},{64,96},{96,128},{128,160},{160,192},{192,224},{224... | collective-permute-start | bytes 73736 | tf_op jit(solution)/shard_map/ppermute | solution.py:375
  13.4 4.4 %collective-permute-start.1 = (f32[48,128]{1,0:T(8,128)S(1)}, f32[48,128]{1,0:T(8,128)S(1)}, u32[]{:S(2)}, u32[]{:S(2)}) collective-permute-start(f32[48,128]{1,0:T(8,128)S(1)} %get-tuple-element.27.own_l_ref), channel_id=1, source_target_pairs={{32,0},{64,32},{96,64},{128,96},{160,128},{192,160},{224,192},{256... | collective-permute-start | bytes 73736 | tf_op jit(solution)/shard_map/ppermute | solution.py:375
  18.5 34.6 %collective-permute-start.5 = (bf16[144,2048]{1,0:T(8,128)(2,1)S(1)}, bf16[144,2048]{1,0:T(8,128)(2,1)}, u32[]{:S(2)}, u32[]{:S(2)}) collective-permute-start(bf16[144,2048]{1,0:T(8,128)(2,1)S(1)} %concatenate.7.x0_ref), channel_id=1, source_target_pairs={{0,256},{256,0},{1,257},{257,1},{2,258},{258,2},{3,259},{259,3},{4... | collective-permute-start | bytes 1769480 | tf_op jit(solution)/shard_map/ppermute | solution.py:398
  24.7 14.2 %collective-permute-start.2 = (f32[7,16,128]{2,1,0:T(8,128)S(1)}, f32[7,16,128]{2,1,0:T(8,128)S(1)}, u32[]{:S(2)}, u32[]{:S(2)}) collective-permute-start(f32[7,16,128]{2,1,0:T(8,128)S(1)} %get-tuple-element.30), channel_id=1, source_target_pairs={{0,1},{1,2},{2,3},{3,4},{4,5},{5,6},{6,7},{7,8},{8,9},{9,10},{10,1... | collective-permute-start | bytes 172040 | tf_op jit(solution)/shard_map/ppermute | solution.py:375
  28.6 11.8 %collective-permute-start.3 = (f32[7,16,128]{2,1,0:T(8,128)S(1)}, f32[7,16,128]{2,1,0:T(8,128)S(1)}, u32[]{:S(2)}, u32[]{:S(2)}) collective-permute-start(f32[7,16,128]{2,1,0:T(8,128)S(1)} %get-tuple-element.31), channel_id=1, source_target_pairs={{1,0},{2,1},{3,2},{4,3},{5,4},{6,5},{7,6},{8,7},{9,8},{10,9},{11,1... | collective-permute-start | bytes 172040 | tf_op jit(solution)/shard_map/ppermute | solution.py:375
  45.3 0.8 copy-start
  46.2 21.7 %all-to-all-start = ((bf16[16,272,128]{2,1,0:T(8,128)(2,1)}), bf16[16,272,128]{2,1,0:T(8,128)(2,1)S(1)}, u32[]{:S(2)}, u32[]{:S(2)}) async-start(bf16[16,272,128]{2,1,0:T(8,128)(2,1)} %get-tuple-element.32), calls=%async_computation | async-start | bytes 2228224 | tf_op jit(solution)/shard_map/all_to_all | solution.py:402
  50.7 4.4 %collective-permute-start.4 = (bf16[144,2048]{1,0:T(8,128)(2,1)S(1)}, bf16[144,2048]{1,0:T(8,128)(2,1)}, u32[]{:S(2)}, u32[]{:S(2)}) collective-permute-start(bf16[144,2048]{1,0:T(8,128)(2,1)S(1)} %concatenate.7.x0_ref), channel_id=1, source_target_pairs={{0,32},{32,0},{1,33},{33,1},{2,34},{34,2},{3,35},{35,3},{4,36},{36... | collective-permute-start | bytes 1769480 | tf_op jit(solution)/shard_map/ppermute | solution.py:399
  53.0 14.8 %collective-permute-start.6 = (bf16[144,2048]{1,0:T(8,128)(2,1)}, bf16[144,2048]{1,0:T(8,128)(2,1)}, u32[]{:S(2)}, u32[]{:S(2)}) collective-permute-start(bf16[144,2048]{1,0:T(8,128)(2,1)} %collective-permute-done.5.x2_ref), channel_id=1, source_target_pairs={{0,32},{32,0},{1,33},{33,1},{2,34},{34,2},{3,35},{35,3},{4,36},{36... | collective-permute-start | bytes 1769480 | tf_op jit(solution)/shard_map/ppermute | solution.py:399
  67.9 15.4 %copy-start.1 = (f32[1280,128]{1,0:T(8,128)S(1)}, f32[1280,128]{1,0:T(8,128)}, u32[]{:S(2)}) copy-start(f32[1280,128]{1,0:T(8,128)} %copy-done) | copy-start | bytes 1966084
  85.5 28.1 %all-to-all-start.2 = ((bf16[16,64,128]{2,1,0:T(8,128)(2,1)}), bf16[16,64,128]{2,1,0:T(8,128)(2,1)S(1)}, u32[]{:S(2)}, u32[]{:S(2)}) async-start(bf16[16,64,128]{2,1,0:T(8,128)(2,1)} %shard_map.50), calls=%async_computation.2 | async-start | bytes 524288 | tf_op jit(solution)/shard_map/all_to_all | solution.py:407
  116.2 14.0 %collective-permute-start.7 = (bf16[512,2048]{1,0:T(8,128)(2,1)S(1)}, bf16[512,2048]{1,0:T(8,128)(2,1)S(1)}, u32[]{:S(2)}, u32[]{:S(2)}) collective-permute-start(bf16[512,2048]{1,0:T(8,128)(2,1)S(1)} %get-tuple-element.42.y_ref), channel_id=1, source_target_pairs={{0,32},{32,0},{1,33},{33,1},{2,34},{34,2},{3,35},{35,3},{4,36},{36... | collective-permute-start | bytes 6291464 | tf_op jit(solution)/shard_map/ppermute | solution.py:412
  118.2 12.1 %collective-permute-start.8 = (bf16[1024,128]{1,0:T(8,128)(2,1)S(1)}, bf16[1024,128]{1,0:T(8,128)(2,1)S(1)}, u32[]{:S(2)}, u32[]{:S(2)}) collective-permute-start(bf16[1024,128]{1,0:T(8,128)(2,1)S(1)} %bitcast.17), channel_id=1, source_target_pairs={{0,16},{16,0},{1,17},{17,1},{2,18},{18,2},{3,19},{19,3},{4,20},{20... | collective-permute-start | bytes 786440 | tf_op jit(solution)/shard_map/ppermute | solution.py:409
Sparse Core Ops, SparseCore 0:
  11.8 77.6 all-gather.1
where the time goes:
time: 164 us
  starting transfers between devices  45.6 us (28%)
  waiting for transfers between devices  45.2 us (28%)
  blocking collectives  35.7 us (22%)
  Pallas kernels  20.5 us (12%)
  between operations  13.6 us (8%)
  local copies, waits for them, and re-layouts  2.08 us (1%)
    all_to_all x1, blocking collectives, local(): out = lax.all_to_all(out, 'z', 0, 0, tiled=True)  24.2 us
    pallas_call x7, Pallas kernels, call(): pl.pallas_call(kernel, out_shape=out_shape, in_specs=[pl.BlockSpec(memory...  20.5 us
    all_to_all x1, waiting for transfers between devices, local(): mine = lax.all_to_all(updated, 'z', 0, 0, tiled=True).reshape(half, cx)  18.4 us
    all_to_all x1, waiting for transfers between devices, local(): got = lax.all_to_all(send, GX, 0, 0, tiled=True)  12.8 us
    all_to_all x1, blocking collectives, local(): back = lax.all_to_all(back, ('yl', 'c'), 0, 0, tiled=True)  11.5 us
    ppermute x2, starting transfers between devices, both_ways(): lax.ppermute(to_before, axis, [(j, i) for i, j in up])  10.9 us
    all_to_all x1, starting transfers between devices, local(): mine = lax.all_to_all(updated, 'z', 0, 0, tiled=True).reshape(half, cx)  9.62 us
    ppermute x1, waiting for transfers between devices, local(): theirs = lax.ppermute(mine, 'yh', swap)  9.56 us
  transfers between devices with their start and end apart: 12, of which 6 were waited for; matrix products, arithmetic and copies ran while one was open for 1% of the time, Pallas kernels for 7%

commit v1 on v0

--- a/solution.py
+++ b/solution.py
@@ -57,12 +57,11 @@
     return lax.broadcasted_iota(jnp.int32, shape, axis)
 
 
-def pack_x_kernel(core_ref, p_hbm, m_hbm, x_hbm, y_hbm, left_ref, right_ref, p_ref, m_ref, part_hbm, first_ref, last_ref, sems):
+def pack_x_kernel(part_ref, p_hbm, m_hbm, x_hbm, y_hbm, left_ref, right_ref, p_ref, m_ref, y_ref, first_ref, last_ref, sems):
     planes, _, cx = p_ref.shape
     pairs = planes // 2
-    rows = part_hbm.shape[0]
     copies = (
-        (y_hbm.at[pl.ds(pl.multiple_of(core_ref[0] * rows, rows), rows)], part_hbm),
+        (y_hbm.at[:, pl.ds(pl.multiple_of(part_ref[0] * cx, cx), cx)], y_ref),
         (p_hbm, p_ref),
         (m_hbm, m_ref),
         (x_hbm.at[pl.ds(0, 16)], first_ref),
@@ -293,38 +292,37 @@
         before = gz
 
 
-def solve_y_near_kernel(side_ref, y_hbm, u_ref, sum_ref, y_ref, sem):
-    high = side_ref[0]
-    half, _ = u_ref.shape
-    copy = pltpu.make_async_copy(y_hbm, y_ref, sem)
-    copy.start()
-    copy.wait()
-    y0 = y_ref[:, pl.ds(pl.multiple_of(high * half, half), half)]
-    sum_ref[...] = jnp.dot(y0, u_ref[...], preferred_element_type=F32)
-
-
-def solve_y_far_kernel(side_ref, sum_ref, y_ref, o_ref, u0_ref, u1_ref, out_ref):
-    high, core = side_ref[0], side_ref[1]
-    half, cx = u0_ref.shape
-    k0 = pl.ds(pl.multiple_of(high * half, half), half)
-    k1 = pl.ds(pl.multiple_of((1 - high) * half, half), half)
-    mine = sum_ref[...] + jnp.dot(y_ref[:, k1], u1_ref[...], preferred_element_type=F32)
-    other = jnp.dot(o_ref[:, k0], u0_ref[...], preferred_element_type=F32)
-    other = other + jnp.dot(o_ref[:, k1], u1_ref[...], preferred_element_type=F32)
-    parts, cy, _ = out_ref.shape
-    rows = cy // 2
-    out_ref[:, pl.ds(pl.multiple_of(core * rows, rows), rows), :] = mine.astype(BF16).reshape(parts, rows, cx)
-    out_ref[:, pl.ds(pl.multiple_of((1 - core) * rows, rows), rows), :] = other.astype(BF16).reshape(parts, rows, cx)
-
-
-def pack_x(core, p, m, x_inverse, y_inverse):
+def solve_y_kernel(place_ref, d_ref, l_ref, r_ref, s0_ref, s1_ref, near_ref, far_ref, mine_ref, theirs_ref, out_ref, u_ref):
+    high, low, x, core, z = (place_ref[i] for i in range(5))
+    parts, cy, cx = out_ref.shape
+    u_ref[high] = mine_ref[...]
+    u_ref[1 - high] = theirs_ref[...]
+
+    def product(turned, at, mine, other):
+        half = low ^ turned
+        base = (x + at) % 4 * 2
+        ua = u_ref[half, pl.ds(pl.multiple_of((base + core) * cx, cx), cx)]
+        ub = u_ref[half, pl.ds(pl.multiple_of((base + 1 - core) * cx, cx), cx)]
+        y = jnp.concatenate([mine, other], axis=1)
+        return jnp.dot(y, jnp.concatenate([ua, ub], axis=0), preferred_element_type=F32)
+
+    total = product(0, 2, s0_ref[...], far_ref[0]) + product(1, 2, s1_ref[...], far_ref[1])
+    for i, (ref, at) in enumerate(((d_ref, 0), (l_ref, 3), (r_ref, 1))):
+        for turned in range(2):
+            total = total + product(turned, at, ref[turned], near_ref[2 * i + turned])
+    for i in range(parts):
+        back = 8 * (i & 1) + 4 * (i >> 1 & 1) + 2 * (i >> 2 & 1) + (i >> 3 & 1)
+        out_ref[(z + parts - back) % parts] = total[i * cy : (i + 1) * cy].astype(BF16)
+
+
+def pack_x(part, p, m, x_inverse, y_inverse):
     cx = p.shape[2]
     shape = (2 * p.shape[0] + 16, cx)
     cy, order = y_inverse.shape
-    out = (kept(shape, F32),) * 2 + (kept(p.shape, F32),) * 2 + (jax.ShapeDtypeStruct((cy // 2, order), BF16),)
+    out = (kept(shape, F32),) * 2 + (kept(p.shape, F32),) * 2 + (kept((cy, cx), BF16),)
     rows = pltpu.VMEM((16, order), BF16)
     scratch = (rows, rows, pltpu.SemaphoreType.DMA((5,)))
-    return call(pack_x_kernel, out, (p, m, x_inverse, y_inverse), core, scratch, range(4), (4,))
+    return call(pack_x_kernel, out, (p, m, x_inverse, y_inverse), part, scratch, range(4))
 
 
 def pack_y(p, m, left, right):
@@ -359,14 +357,10 @@
     return call(implicit_kernel, kept((planes, cy, cx), BF16), (back, *faces), scratch=scratch)
 
 
-def solve_y_near(side, y, u):
-    out = (kept((y.shape[0], u.shape[1]), F32), kept(y.shape, BF16))
-    return call(solve_y_near_kernel, out, (y, u), side, (pltpu.SemaphoreType.DMA(()),), (0,))
-
-
-def solve_y_far(side, *parts):
+def solve_y(place, *parts):
     half, cx = parts[-1].shape
-    return call(solve_y_far_kernel, kept((16, half // 16, cx), BF16), parts, side)
+    scratch = (pltpu.VMEM((2, half, cx), BF16),)
+    return call(solve_y_kernel, kept((16, half // 16, cx), BF16), parts, place, scratch)
 
 
 def both_ways(to_before, to_after, axis):
@@ -375,44 +369,59 @@
     return lax.ppermute(to_after, axis, up), lax.ppermute(to_before, axis, [(j, i) for i, j in up])
 
 
+def moved(v, axis, distance):
+    size = lax.axis_size(axis)
+    return lax.ppermute(v, axis, [(i, (i + distance) % size) for i in range(size)])
+
+
+def exchanged(v, axes):
+    return lax.all_to_all(v, axes, 0, 0, tiled=True)
+
+
 def local(phase_field, mobility, x_inverse, y_inverse):
     planes, cy, cx = phase_field.shape
     order = y_inverse.shape[1]
     half = order // 2
-    core, low, high = lax.axis_index("c"), lax.axis_index("yl"), lax.axis_index("yh")
-    swap = [(0, 1), (1, 0)]
-
+    high, low, x, core, z = (lax.axis_index(a) for a in ("yh", "yl", "x", "c", "z"))
+    place = jnp.stack((high, low, x, core, z)).astype(jnp.int32)
     one = lambda v: v.reshape(1).astype(jnp.int32)
 
-    own_l, own_r, phase_field, mobility, y_part = pack_x(one(core), phase_field, mobility, x_inverse, y_inverse)
-    y_mine = lax.all_gather(y_part, "z", axis=0, tiled=True)
+    own_l, own_r, phase_field, mobility, part = pack_x(
+        one(low * 8 + x * 2 + core), phase_field, mobility, x_inverse, y_inverse
+    )
     left, right = both_ways(own_l, own_r, GX)
     to_up, to_down = pack_y(phase_field, mobility, left, right)
-
     row_before = left[-16:].reshape(1, order).astype(BF16)
     row_after = right[-16:].reshape(1, order).astype(BF16)
     row_before, row_after, to_up = lax.optimization_barrier((row_before, row_after, to_up))
+    up, down = both_ways(to_down, to_up, GY)
+
     ends = [x_inverse, row_before, x_inverse[:1], x_inverse[-1:], row_after, jnp.zeros((12, order), BF16)]
-    up, down = both_ways(to_down, to_up, GY)
     rows = jnp.concatenate(ends, axis=0)
-    rows_yl = lax.ppermute(rows, "yl", swap)
-    x_blocks = (rows, lax.ppermute(rows, "c", swap), rows_yl, lax.ppermute(rows_yl, "c", swap))
+    rows_yl = moved(rows, "yl", 1)
+    x_blocks = (rows, moved(rows, "c", 1), rows_yl, moved(rows_yl, "c", 1))
+
+    ys = part[None]
+    for d in (8, 4, 2, 1):
+        ys = jnp.concatenate([ys, moved(ys, "z", d)], axis=0)
+    ys = ys.reshape(1, half, cx)
+    ys = jnp.concatenate([ys, moved(ys, "yl", 1)], axis=0)
+    y_left = moved(ys, "x", 1)
+    y_right = moved(ys, "x", -1)
+    y_near = moved(jnp.concatenate([ys, y_left, y_right], axis=0), "c", 1)
+    y_s0 = moved(y_left[0], "x", 1)
+    y_s1 = moved(y_right[1], "x", -1)
+    y_far = moved(jnp.stack((y_s0, y_s1)), "c", 1)
 
     send, *faces = explicit(phase_field, mobility, own_l, own_r, left, right, up, down)
-    got = lax.all_to_all(send, GX, 0, 0, tiled=True)
+    got = exchanged(send, GX)
     back = solve_x(one(low * 2 + core), got, x_blocks)
-    back = lax.all_to_all(back, ("yl", "c"), 0, 0, tiled=True)
+    back = exchanged(back, ("yl", "c"))
     updated = implicit(back, faces, planes, cy)
-
-    mine = lax.all_to_all(updated, "z", 0, 0, tiled=True).reshape(half, cx)
-    y_mine, mine = lax.optimization_barrier((y_mine, mine))
-    theirs = lax.ppermute(mine, "yh", swap)
-    side = jnp.concatenate([one(high), one(core)])
-    part, y_mine = solve_y_near(side, y_mine, mine)
-    y_other = lax.ppermute(y_mine, "c", swap)
-    out = solve_y_far(side, part, y_mine, y_other, mine, theirs)
-    out = lax.all_to_all(out, "z", 0, 0, tiled=True)
-    return out.astype(F32)
+    mine = exchanged(updated, "z").reshape(half, cx)
+    theirs = moved(mine, "yh", 1)
+    out = solve_y(place, ys, y_left, y_right, y_s0, y_s1, y_near, y_far, mine, theirs)
+    return exchanged(out, "z").astype(F32)
 
 
 def solution(mesh):

time: 164 us -> 190 us (1.16)
  the two profiles are of different devices: /device:TPU:16 before, /device:TPU:6 now
where the time goes in v1:
time: 190 us; the launch traced here: 189 us
  starting transfers between devices  92.4 us (49%)
  waiting for transfers between devices  37.7 us (20%)
  blocking collectives  29.9 us (16%)
  Pallas kernels  15.3 us (8%)
  local copies, waits for them, and re-layouts  8.02 us (4%)
  other arithmetic  5.11 us (3%)
    ppermute x15, starting transfers between devices, moved(): lax.ppermute(v, axis, [(i, (i + distance) % size) for i in range(size)])  61.2 us
    ppermute x15, waiting for transfers between devices, moved(): lax.ppermute(v, axis, [(i, (i + distance) % size) for i in range(size)])  35.5 us
    all_to_all x1, blocking collectives, exchanged(): return lax.all_to_all(v, axes, 0, 0, tiled=True)  29.9 us
    all_to_all x3, starting transfers between devices, exchanged(): return lax.all_to_all(v, axes, 0, 0, tiled=True)  21.4 us
    pallas_call x6, Pallas kernels, call(): pl.pallas_call(kernel, out_shape=out_shape, in_specs=[pl.BlockSpec(memory...  15.3 us
    unnamed x28, local copies, waits for them, and re-layouts  6.55 us
    ppermute x2, starting transfers between devices, both_ways(): lax.ppermute(to_before, axis, [(j, i) for i, j in up])  4.93 us
    ppermute x2, starting transfers between devices, both_ways(): lax.ppermute(to_after, axis, up)  4.85 us
  transfers between devices with their start and end apart: 22, of which 10 were waited for; matrix products, arithmetic and copies ran while one was open for 4% of the time, Pallas kernels for 6%

profile of v1, /device:TPU:6, one launch (start us, length us, event | category | flops | bytes accessed | tf_op | source)
XLA Modules:
  0.0 188.8 jit_solution(14313428964546713784)
XLA Ops:
  1.6 1.9 %collective-permute-start.11 = (f32[48,128]{1,0:T(8,128)S(1)}, f32[48,128]{1,0:T(8,128)S(1)}, u32[]{:S(2)}, u32[]{:S(2)}) collective-permute-start(f32[48,128]{1,0:T(8,128)S(1)} %get-tuple-element.24.own_r_ref), channel_id=1, source_target_pairs={{0,32},{32,64},{64,96},{96,128},{128,160},{160,192},{192,224},{224... | collective-permute-start | bytes 73736 | tf_op jit(solution)/shard_map/ppermute | solution.py:369
  3.5 3.6 %collective-permute-start.12 = (f32[48,128]{1,0:T(8,128)S(1)}, f32[48,128]{1,0:T(8,128)S(1)}, u32[]{:S(2)}, u32[]{:S(2)}) collective-permute-start(f32[48,128]{1,0:T(8,128)S(1)} %get-tuple-element.23.own_l_ref), channel_id=1, source_target_pairs={{32,0},{64,32},{96,64},{128,96},{160,128},{192,160},{224,192},{256... | collective-permute-start | bytes 73736 | tf_op jit(solution)/shard_map/ppermute | solution.py:369
  7.2 15.7 %collective-permute-start = (bf16[1,64,128]{2,1,0:T(8,128)(2,1)S(1)}, bf16[1,64,128]{2,1,0:T(8,128)(2,1)S(1)}, u32[]{:S(2)}, u32[]{:S(2)}) collective-permute-start(bf16[1,64,128]{2,1,0:T(8,128)(2,1)S(1)} %bitcast.33), channel_id=1, source_target_pairs={{0,8},{1,9},{2,10},{3,11},{4,12},{5,13},{6,14},{7,15},{8,0},{9,1},... | collective-permute-start | bytes 49160 | tf_op jit(solution)/shard_map/ppermute | solution.py:374
  24.6 6.0 %collective-permute-start.1 = (bf16[2,64,128]{2,1,0:T(8,128)(2,1)S(1)}, bf16[2,64,128]{2,1,0:T(8,128)(2,1)S(1)}, u32[]{:S(2)}, u32[]{:S(2)}) collective-permute-start(bf16[2,64,128]{2,1,0:T(8,128)(2,1)S(1)} %pad_maximum_fusion.5), channel_id=1, source_target_pairs={{0,4},{1,5},{2,6},{3,7},{4,8},{5,9},{6,10},{7,11},{8,12},{9,13},{1... | collective-permute-start | bytes 98312 | tf_op jit(solution)/shard_map/ppermute | solution.py:374
  31.3 4.9 %collective-permute-done.1 = bf16[2,64,128]{2,1,0:T(8,128)(2,1)S(1)} collective-permute-done((bf16[2,64,128]{2,1,0:T(8,128)(2,1)S(1)}, bf16[2,64,128]{2,1,0:T(8,128)(2,1)S(1)}, u32[]{:S(2)}, u32[]{:S(2)}) %collective-permute-start.1) | collective-permute-done | bytes 32800 | tf_op jit(solution)/shard_map/ppermute | solution.py:374
  36.1 3.5 %collective-permute-start.2 = (bf16[4,64,128]{2,1,0:T(8,128)(2,1)S(1)}, bf16[4,64,128]{2,1,0:T(8,128)(2,1)S(1)}, u32[]{:S(2)}, u32[]{:S(2)}) collective-permute-start(bf16[4,64,128]{2,1,0:T(8,128)(2,1)S(1)} %pad_maximum_fusion.4), channel_id=1, source_target_pairs={{0,2},{1,3},{2,4},{3,5},{4,6},{5,7},{6,8},{7,9},{8,10},{9,11},{10,... | collective-permute-start | bytes 196616 | tf_op jit(solution)/shard_map/ppermute | solution.py:374
  40.3 3.4 %collective-permute-start.16 = (bf16[144,2048]{1,0:T(8,128)(2,1)S(1)}, bf16[144,2048]{1,0:T(8,128)(2,1)}, u32[]{:S(2)}, u32[]{:S(2)}) collective-permute-start(bf16[144,2048]{1,0:T(8,128)(2,1)S(1)} %concatenate.31.x0_ref), channel_id=1, source_target_pairs={{0,256},{256,0},{1,257},{257,1},{2,258},{258,2},{3,259},{259,3},{4... | collective-permute-start | bytes 1769480 | tf_op jit(solution)/shard_map/ppermute | solution.py:374
  43.7 2.9 %collective-permute-start.13 = (f32[7,16,128]{2,1,0:T(8,128)S(1)}, f32[7,16,128]{2,1,0:T(8,128)S(1)}, u32[]{:S(2)}, u32[]{:S(2)}) collective-permute-start(f32[7,16,128]{2,1,0:T(8,128)S(1)} %get-tuple-element.26), channel_id=1, source_target_pairs={{0,1},{1,2},{2,3},{3,4},{4,5},{5,6},{6,7},{7,8},{8,9},{9,10},{10,1... | collective-permute-start | bytes 172040 | tf_op jit(solution)/shard_map/ppermute | solution.py:369
  47.9 4.6 %collective-permute-start.3 = (bf16[8,64,128]{2,1,0:T(8,128)(2,1)S(1)}, bf16[8,64,128]{2,1,0:T(8,128)(2,1)}, u32[]{:S(2)}, u32[]{:S(2)}) collective-permute-start(bf16[8,64,128]{2,1,0:T(8,128)(2,1)S(1)} %pad_maximum_fusion.3), channel_id=1, source_target_pairs={{0,1},{1,2},{2,3},{3,4},{4,5},{5,6},{6,7},{7,8},{8,9},{9,10},{10,1... | collective-permute-start | bytes 393224 | tf_op jit(solution)/shard_map/ppermute | solution.py:374
  53.1 4.0 %shard_map.48 = (bf16[16,272,128]{2,1,0:T(8,128)(2,1)S(1)}, f32[1360,128]{1,0:T(8,128)S(1)}, f32[1280,128]{1,0:T(8,128)S(1)}, f32[1280,128]{1,0:T(8,128)S(1)}, f32[16,128]{1,0:T(8,128)S(1)}) custom-call(f32[16,64,128]{2,1,0:T(8,128)S(1)} %get-tuple-element.21.p_ref, f32[16,64,128]{2,1,0:T(8,128)S(1)} %get-tuple-element.22.m_ref, ...), custom_call_target="tpu_custom_call" | custom-call | tf_op jit(solution)/shard_map/pallas_call | solution.py:38
  60.7 6.2 %all-to-all-start = ((bf16[16,272,128]{2,1,0:T(8,128)(2,1)}), bf16[16,272,128]{2,1,0:T(8,128)(2,1)S(1)}, u32[]{:S(2)}, u32[]{:S(2)}) async-start(bf16[16,272,128]{2,1,0:T(8,128)(2,1)} %copy-done), calls=%async_computation | async-start | bytes 2228224 | tf_op jit(solution)/shard_map/all_to_all | solution.py:378
  67.9 3.4 %collective-permute-start.4 = (bf16[1,1024,128]{2,1,0:T(8,128)(2,1)S(1)}, bf16[1,1024,128]{2,1,0:T(8,128)(2,1)}, u32[]{:S(2)}, u32[]{:S(2)}) collective-permute-start(bf16[1,1024,128]{2,1,0:T(8,128)(2,1)S(1)} %bitcast.37), channel_id=1, source_target_pairs={{0,256},{256,0},{1,257},{257,1},{2,258},{258,2},{3,259},{259,3},{4... | collective-permute-start | bytes 786440 | tf_op jit(solution)/shard_map/ppermute | solution.py:374
  71.4 1.9 %collective-permute-start.15 = (bf16[144,2048]{1,0:T(8,128)(2,1)S(1)}, bf16[144,2048]{1,0:T(8,128)(2,1)}, u32[]{:S(2)}, u32[]{:S(2)}) collective-permute-start(bf16[144,2048]{1,0:T(8,128)(2,1)S(1)} %concatenate.31.x0_ref), channel_id=1, source_target_pairs={{0,32},{32,0},{1,33},{33,1},{2,34},{34,2},{3,35},{35,3},{4,36},{36... | collective-permute-start | bytes 1769480 | tf_op jit(solution)/shard_map/ppermute | solution.py:374
  73.3 2.4 %collective-permute-start.17 = (bf16[144,2048]{1,0:T(8,128)(2,1)}, bf16[144,2048]{1,0:T(8,128)(2,1)}, u32[]{:S(2)}, u32[]{:S(2)}) collective-permute-start(bf16[144,2048]{1,0:T(8,128)(2,1)} %collective-permute-done.16.x2_ref), channel_id=1, source_target_pairs={{0,32},{32,0},{1,33},{33,1},{2,34},{34,2},{3,35},{35,3},{4,36},{36... | collective-permute-start | bytes 1769480 | tf_op jit(solution)/shard_map/ppermute | solution.py:374
  75.7 11.6 %collective-permute-done.4 = bf16[1,1024,128]{2,1,0:T(8,128)(2,1)} collective-permute-done((bf16[1,1024,128]{2,1,0:T(8,128)(2,1)S(1)}, bf16[1,1024,128]{2,1,0:T(8,128)(2,1)}, u32[]{:S(2)}, u32[]{:S(2)}) %collective-permute-start.4) | collective-permute-done | bytes 262176 | tf_op jit(solution)/shard_map/ppermute | solution.py:374
  88.3 2.4 %collective-permute-start.5 = (bf16[2,1024,128]{2,1,0:T(8,128)(2,1)S(1)}, bf16[2,1024,128]{2,1,0:T(8,128)(2,1)S(1)}, u32[]{:S(2)}, u32[]{:S(2)}) collective-permute-start(bf16[2,1024,128]{2,1,0:T(8,128)(2,1)S(1)} %pad_maximum_fusion.1.d_ref), channel_id=1, source_target_pairs={{0,64},{64,128},{128,192},{192,0},{1,65},{65,129},{129,193},{193,1... | collective-permute-start | bytes 1572872 | tf_op jit(solution)/shard_map/ppermute | solution.py:374
  90.8 3.4 %collective-permute-start.6 = (bf16[2,1024,128]{2,1,0:T(8,128)(2,1)S(1)}, bf16[2,1024,128]{2,1,0:T(8,128)(2,1)S(1)}, u32[]{:S(2)}, u32[]{:S(2)}) collective-permute-start(bf16[2,1024,128]{2,1,0:T(8,128)(2,1)S(1)} %pad_maximum_fusion.1.d_ref), channel_id=1, source_target_pairs={{0,192},{64,0},{128,64},{192,128},{1,193},{65,1},{129,65},{193,129... | collective-permute-start | bytes 1572872 | tf_op jit(solution)/shard_map/ppermute | solution.py:374
  94.2 4.6 %shard_map.49 = f32[4,272,128]{2,1,0:T(8,128)} custom-call(s32[1]{0:T(128)} %bitcast.12.block_ref, bf16[16,272,128]{2,1,0:T(8,128)(2,1)S(1)} %all-to-all-done.got_ref, bf16[144,2048]{1,0:T(8,128)(2,1)S(1)} %concatenate.31.x0_ref, bf16[144,2048]{1,0:T(8,128)(2,1)} %collective-permute-done.15.x1_ref, bf16[144,2048]{1,0:T(8,128)(2,1)} %collective-permute-done.16.x2_ref, ...), custom_call_target="tpu_custom_call" | custom-call | tf_op jit(solution)/shard_map/pallas_call | solution.py:38
  98.8 3.5 %all-to-all-start.1 = ((f32[4,272,128]{2,1,0:T(8,128)}), f32[4,272,128]{2,1,0:T(8,128)S(1)}, u32[]{:S(2)}, u32[]{:S(2)}) async-start(f32[4,272,128]{2,1,0:T(8,128)} %shard_map.49), calls=%async_computation.1 | async-start | bytes 1114112 | tf_op jit(solution)/shard_map/all_to_all | solution.py:378
  103.6 3.4 %collective-permute-done.6.r_ref = bf16[2,1024,128]{2,1,0:T(8,128)(2,1)S(1)} collective-permute-done((bf16[2,1024,128]{2,1,0:T(8,128)(2,1)S(1)}, bf16[2,1024,128]{2,1,0:T(8,128)(2,1)S(1)}, u32[]{:S(2)}, u32[]{:S(2)}) %collective-permute-start.6) | collective-permute-done | bytes 524320 | tf_op jit(solution)/shard_map/ppermute | solution.py:374
  107.0 2.4 %pad_maximum_fusion = bf16[6,1024,128]{2,1,0:T(8,128)(2,1)} fusion(bf16[2,1024,128]{2,1,0:T(8,128)(2,1)S(1)} %collective-permute-done.6.r_ref, bf16[2,1024,128]{2,1,0:T(8,128)(2,1)S(1)} %collective-permute-done.5.l_ref, bf16[1,1024,128]{2,1,0:T(8,128)(2,1)} %collective-permute-done.4, bf16[1,1024,128]{2,1,0:T(8,128)(2,1)} %bitcast.39), kind=kLoop, calls=%fused_computation | loop fusion | flops 2359296 | bytes 3145728 | tf_op jit(solution)/shard_map/concatenate | solution.py:411
  112.5 2.3 %shard_map.50 = bf16[16,64,128]{2,1,0:T(8,128)(2,1)} custom-call(f32[4,272,128]{2,1,0:T(8,128)S(1)} %all-to-all-done.1.back_ref, f32[1360,128]{1,0:T(8,128)S(1)} %copy-done.2, f32[1280,128]{1,0:T(8,128)S(1)} %copy-done.4, f32[1280,128]{1,0:T(8,128)S(1)} %copy-done.6, f32[16,128]{1,0:T(8,128)S(1)} %get-tuple-element.34.edge_ref), custom_call_target="tpu_custom_call" | custom-call | tf_op jit(solution)/shard_map/pallas_call | solution.py:38
  114.8 11.7 %all-to-all-start.2 = ((bf16[16,64,128]{2,1,0:T(8,128)(2,1)}), bf16[16,64,128]{2,1,0:T(8,128)(2,1)S(1)}, u32[]{:S(2)}, u32[]{:S(2)}) async-start(bf16[16,64,128]{2,1,0:T(8,128)(2,1)} %shard_map.50), calls=%async_computation.2 | async-start | bytes 524288 | tf_op jit(solution)/shard_map/all_to_all | solution.py:378
  126.5 3.6 %collective-permute-start.7 = (bf16[1024,128]{1,0:T(8,128)(2,1)S(1)}, bf16[1024,128]{1,0:T(8,128)(2,1)S(1)}, u32[]{:S(2)}, u32[]{:S(2)}) collective-permute-start(bf16[1024,128]{1,0:T(8,128)(2,1)S(1)} %slice_bitcast_fusion.1), channel_id=1, source_target_pairs={{0,64},{64,128},{128,192},{192,0},{1,65},{65,129},{129,193},{193,1... | collective-permute-start | bytes 786440 | tf_op jit(solution)/shard_map/ppermute | solution.py:374
  130.2 2.2 %collective-permute-start.8 = (bf16[1024,128]{1,0:T(8,128)(2,1)S(1)}, bf16[1024,128]{1,0:T(8,128)(2,1)S(1)}, u32[]{:S(2)}, u32[]{:S(2)}) collective-permute-start(bf16[1024,128]{1,0:T(8,128)(2,1)S(1)} %slice_bitcast_fusion), channel_id=1, source_target_pairs={{0,192},{64,0},{128,64},{192,128},{1,193},{65,1},{129,65},{193,129... | collective-permute-start | bytes 786440 | tf_op jit(solution)/shard_map/ppermute | solution.py:374
  132.4 4.3 %collective-permute-done.7.s0_ref = bf16[1024,128]{1,0:T(8,128)(2,1)S(1)} collective-permute-done((bf16[1024,128]{1,0:T(8,128)(2,1)S(1)}, bf16[1024,128]{1,0:T(8,128)(2,1)S(1)}, u32[]{:S(2)}, u32[]{:S(2)}) %collective-permute-start.7) | collective-permute-done | bytes 262176 | tf_op jit(solution)/shard_map/ppermute | solution.py:374
  136.7 3.8 %collective-permute-done.8.s1_ref = bf16[1024,128]{1,0:T(8,128)(2,1)S(1)} collective-permute-done((bf16[1024,128]{1,0:T(8,128)(2,1)S(1)}, bf16[1024,128]{1,0:T(8,128)(2,1)S(1)}, u32[]{:S(2)}, u32[]{:S(2)}) %collective-permute-start.8) | collective-permute-done | bytes 262176 | tf_op jit(solution)/shard_map/ppermute | solution.py:374
  143.2 2.0 %all-to-all-done.2 = bf16[16,64,128]{2,1,0:T(8,128)(2,1)S(1)} async-done(((bf16[16,64,128]{2,1,0:T(8,128)(2,1)}), bf16[16,64,128]{2,1,0:T(8,128)(2,1)S(1)}, u32[]{:S(2)}, u32[]{:S(2)}) %all-to-all-start.2) | async-done | bytes 262176 | tf_op jit(solution)/shard_map/all_to_all | solution.py:378
  145.2 4.8 %collective-permute-start.18 = (bf16[1024,128]{1,0:T(8,128)(2,1)S(1)}, bf16[1024,128]{1,0:T(8,128)(2,1)S(1)}, u32[]{:S(2)}, u32[]{:S(2)}) collective-permute-start(bf16[1024,128]{1,0:T(8,128)(2,1)S(1)} %bitcast.29), channel_id=1, source_target_pairs={{0,16},{16,0},{1,17},{17,1},{2,18},{18,2},{3,19},{19,3},{4,20},{20... | collective-permute-start | bytes 786440 | tf_op jit(solution)/shard_map/ppermute | solution.py:374
  150.1 5.2 %collective-permute-done.18.theirs_ref = bf16[1024,128]{1,0:T(8,128)(2,1)S(1)} collective-permute-done((bf16[1024,128]{1,0:T(8,128)(2,1)S(1)}, bf16[1024,128]{1,0:T(8,128)(2,1)S(1)}, u32[]{:S(2)}, u32[]{:S(2)}) %collective-permute-start.18) | collective-permute-done | bytes 262176 | tf_op jit(solution)/shard_map/ppermute | solution.py:374
  155.3 2.7 %shard_map.51 = bf16[16,64,128]{2,1,0:T(8,128)(2,1)S(1)} custom-call(s32[5]{0:T(128)S(1)} %stack.32.place_ref, bf16[2,1024,128]{2,1,0:T(8,128)(2,1)S(1)} %pad_maximum_fusion.1.d_ref, bf16[2,1024,128]{2,1,0:T(8,128)(2,1)S(1)} %collective-permute-done.5.l_ref, bf16[2,1024,128]{2,1,0:T(8,128)(2,1)S(1)} %collective-permute-done.6.r_ref, ...), custom_call_target="tpu_custom_call" | custom-call | tf_op jit(solution)/shard_map/pallas_call | solution.py:38
  158.0 29.9 %all_to_all.20 = bf16[16,64,128]{2,1,0:T(8,128)(2,1)S(1)} all-to-all(bf16[16,64,128]{2,1,0:T(8,128)(2,1)S(1)} %shard_map.51), channel_id=1, replica_groups=mesh['yl'=2,'x'=4,'c'=2,'yh'=2,'z'=16] {'z'}, dimensions={0} | all-to-all | bytes 524288 | tf_op jit(solution)/shard_map/all_to_all | solution.py:378
  (61 shorter events, 20.1 us)
Async XLA Ops:
  0.0 22.9 %copy-start.7 = (bf16[128,2048]{1,0:T(8,128)(2,1)S(1)}, bf16[128,2048]{1,0:T(8,128)(2,1)}, u32[]{:S(2)}) copy-start(bf16[128,2048]{1,0:T(8,128)(2,1)} %x_hbm.1) | copy-start | bytes 1572868
  1.6 38.0 %collective-permute-start.11 = (f32[48,128]{1,0:T(8,128)S(1)}, f32[48,128]{1,0:T(8,128)S(1)}, u32[]{:S(2)}, u32[]{:S(2)}) collective-permute-start(f32[48,128]{1,0:T(8,128)S(1)} %get-tuple-element.24.own_r_ref), channel_id=1, source_target_pairs={{0,32},{32,64},{64,96},{96,128},{128,160},{160,192},{192,224},{224... | collective-permute-start | bytes 73736 | tf_op jit(solution)/shard_map/ppermute | solution.py:369
  3.5 27.7 %collective-permute-start.12 = (f32[48,128]{1,0:T(8,128)S(1)}, f32[48,128]{1,0:T(8,128)S(1)}, u32[]{:S(2)}, u32[]{:S(2)}) collective-permute-start(f32[48,128]{1,0:T(8,128)S(1)} %get-tuple-element.23.own_l_ref), channel_id=1, source_target_pairs={{32,0},{64,32},{96,64},{128,96},{160,128},{192,160},{224,192},{256... | collective-permute-start | bytes 73736 | tf_op jit(solution)/shard_map/ppermute | solution.py:369
  7.2 17.4 %collective-permute-start = (bf16[1,64,128]{2,1,0:T(8,128)(2,1)S(1)}, bf16[1,64,128]{2,1,0:T(8,128)(2,1)S(1)}, u32[]{:S(2)}, u32[]{:S(2)}) collective-permute-start(bf16[1,64,128]{2,1,0:T(8,128)(2,1)S(1)} %bitcast.33), channel_id=1, source_target_pairs={{0,8},{1,9},{2,10},{3,11},{4,12},{5,13},{6,14},{7,15},{8,0},{9,1},... | collective-permute-start | bytes 49160 | tf_op jit(solution)/shard_map/ppermute | solution.py:374
  24.6 11.5 %collective-permute-start.1 = (bf16[2,64,128]{2,1,0:T(8,128)(2,1)S(1)}, bf16[2,64,128]{2,1,0:T(8,128)(2,1)S(1)}, u32[]{:S(2)}, u32[]{:S(2)}) collective-permute-start(bf16[2,64,128]{2,1,0:T(8,128)(2,1)S(1)} %pad_maximum_fusion.5), channel_id=1, source_target_pairs={{0,4},{1,5},{2,6},{3,7},{4,8},{5,9},{6,10},{7,11},{8,12},{9,13},{1... | collective-permute-start | bytes 98312 | tf_op jit(solution)/shard_map/ppermute | solution.py:374
  36.1 11.8 %collective-permute-start.2 = (bf16[4,64,128]{2,1,0:T(8,128)(2,1)S(1)}, bf16[4,64,128]{2,1,0:T(8,128)(2,1)S(1)}, u32[]{:S(2)}, u32[]{:S(2)}) collective-permute-start(bf16[4,64,128]{2,1,0:T(8,128)(2,1)S(1)} %pad_maximum_fusion.4), channel_id=1, source_target_pairs={{0,2},{1,3},{2,4},{3,5},{4,6},{5,7},{6,8},{7,9},{8,10},{9,11},{10,... | collective-permute-start | bytes 196616 | tf_op jit(solution)/shard_map/ppermute | solution.py:374
  40.3 33.0 %collective-permute-start.16 = (bf16[144,2048]{1,0:T(8,128)(2,1)S(1)}, bf16[144,2048]{1,0:T(8,128)(2,1)}, u32[]{:S(2)}, u32[]{:S(2)}) collective-permute-start(bf16[144,2048]{1,0:T(8,128)(2,1)S(1)} %concatenate.31.x0_ref), channel_id=1, source_target_pairs={{0,256},{256,0},{1,257},{257,1},{2,258},{258,2},{3,259},{259,3},{4... | collective-permute-start | bytes 1769480 | tf_op jit(solution)/shard_map/ppermute | solution.py:374
  43.7 9.5 %collective-permute-start.13 = (f32[7,16,128]{2,1,0:T(8,128)S(1)}, f32[7,16,128]{2,1,0:T(8,128)S(1)}, u32[]{:S(2)}, u32[]{:S(2)}) collective-permute-start(f32[7,16,128]{2,1,0:T(8,128)S(1)} %get-tuple-element.26), channel_id=1, source_target_pairs={{0,1},{1,2},{2,3},{3,4},{4,5},{5,6},{6,7},{7,8},{8,9},{9,10},{10,1... | collective-permute-start | bytes 172040 | tf_op jit(solution)/shard_map/ppermute | solution.py:369
  46.6 6.5 %collective-permute-start.14 = (f32[7,16,128]{2,1,0:T(8,128)S(1)}, f32[7,16,128]{2,1,0:T(8,128)S(1)}, u32[]{:S(2)}, u32[]{:S(2)}) collective-permute-start(f32[7,16,128]{2,1,0:T(8,128)S(1)} %get-tuple-element.27), channel_id=1, source_target_pairs={{1,0},{2,1},{3,2},{4,3},{5,4},{6,5},{7,6},{8,7},{9,8},{10,9},{11,1... | collective-permute-start | bytes 172040 | tf_op jit(solution)/shard_map/ppermute | solution.py:369
  47.9 19.1 %collective-permute-start.3 = (bf16[8,64,128]{2,1,0:T(8,128)(2,1)S(1)}, bf16[8,64,128]{2,1,0:T(8,128)(2,1)}, u32[]{:S(2)}, u32[]{:S(2)}) collective-permute-start(bf16[8,64,128]{2,1,0:T(8,128)(2,1)S(1)} %pad_maximum_fusion.3), channel_id=1, source_target_pairs={{0,1},{1,2},{2,3},{3,4},{4,5},{5,6},{6,7},{7,8},{8,9},{9,10},{10,1... | collective-permute-start | bytes 393224 | tf_op jit(solution)/shard_map/ppermute | solution.py:374
  57.2 1.0 copy-start
  58.2 0.9 copy-start.1
  59.0 0.8 copy-start.3
  59.9 0.9 copy-start.5
  60.7 6.2 %copy-start.8 = (bf16[16,64,128]{2,1,0:T(8,128)(2,1)S(1)}, bf16[16,64,128]{2,1,0:T(8,128)(2,1)}, u32[]{:S(2)}) copy-start(bf16[16,64,128]{2,1,0:T(8,128)(2,1)} %constant_dynamic-update-slice_fusion.2) | copy-start | bytes 786436
  60.7 33.5 %all-to-all-start = ((bf16[16,272,128]{2,1,0:T(8,128)(2,1)}), bf16[16,272,128]{2,1,0:T(8,128)(2,1)S(1)}, u32[]{:S(2)}, u32[]{:S(2)}) async-start(bf16[16,272,128]{2,1,0:T(8,128)(2,1)} %copy-done), calls=%async_computation | async-start | bytes 2228224 | tf_op jit(solution)/shard_map/all_to_all | solution.py:378
  67.9 19.4 %copy-start.9 = (bf16[16,64,128]{2,1,0:T(8,128)(2,1)}, bf16[16,64,128]{2,1,0:T(8,128)(2,1)S(1)}, u32[]{:S(2)}) copy-start(bf16[16,64,128]{2,1,0:T(8,128)(2,1)S(1)} %constant_dynamic-update-slice_fusion) | copy-start | bytes 786436
  67.9 19.4 %collective-permute-start.4 = (bf16[1,1024,128]{2,1,0:T(8,128)(2,1)S(1)}, bf16[1,1024,128]{2,1,0:T(8,128)(2,1)}, u32[]{:S(2)}, u32[]{:S(2)}) collective-permute-start(bf16[1,1024,128]{2,1,0:T(8,128)(2,1)S(1)} %bitcast.37), channel_id=1, source_target_pairs={{0,256},{256,0},{1,257},{257,1},{2,258},{258,2},{3,259},{259,3},{4... | collective-permute-start | bytes 786440 | tf_op jit(solution)/shard_map/ppermute | solution.py:374
  71.4 22.8 %collective-permute-start.15 = (bf16[144,2048]{1,0:T(8,128)(2,1)S(1)}, bf16[144,2048]{1,0:T(8,128)(2,1)}, u32[]{:S(2)}, u32[]{:S(2)}) collective-permute-start(bf16[144,2048]{1,0:T(8,128)(2,1)S(1)} %concatenate.31.x0_ref), channel_id=1, source_target_pairs={{0,32},{32,0},{1,33},{33,1},{2,34},{34,2},{3,35},{35,3},{4,36},{36... | collective-permute-start | bytes 1769480 | tf_op jit(solution)/shard_map/ppermute | solution.py:374
  73.3 20.9 %collective-permute-start.17 = (bf16[144,2048]{1,0:T(8,128)(2,1)}, bf16[144,2048]{1,0:T(8,128)(2,1)}, u32[]{:S(2)}, u32[]{:S(2)}) collective-permute-start(bf16[144,2048]{1,0:T(8,128)(2,1)} %collective-permute-done.16.x2_ref), channel_id=1, source_target_pairs={{0,32},{32,0},{1,33},{33,1},{2,34},{34,2},{3,35},{35,3},{4,36},{36... | collective-permute-start | bytes 1769480 | tf_op jit(solution)/shard_map/ppermute | solution.py:374
  88.3 15.3 %collective-permute-start.5 = (bf16[2,1024,128]{2,1,0:T(8,128)(2,1)S(1)}, bf16[2,1024,128]{2,1,0:T(8,128)(2,1)S(1)}, u32[]{:S(2)}, u32[]{:S(2)}) collective-permute-start(bf16[2,1024,128]{2,1,0:T(8,128)(2,1)S(1)} %pad_maximum_fusion.1.d_ref), channel_id=1, source_target_pairs={{0,64},{64,128},{128,192},{192,0},{1,65},{65,129},{129,193},{193,1... | collective-permute-start | bytes 1572872 | tf_op jit(solution)/shard_map/ppermute | solution.py:374
  90.8 16.2 %collective-permute-start.6 = (bf16[2,1024,128]{2,1,0:T(8,128)(2,1)S(1)}, bf16[2,1024,128]{2,1,0:T(8,128)(2,1)S(1)}, u32[]{:S(2)}, u32[]{:S(2)}) collective-permute-start(bf16[2,1024,128]{2,1,0:T(8,128)(2,1)S(1)} %pad_maximum_fusion.1.d_ref), channel_id=1, source_target_pairs={{0,192},{64,0},{128,64},{192,128},{1,193},{65,1},{129,65},{193,129... | collective-permute-start | bytes 1572872 | tf_op jit(solution)/shard_map/ppermute | solution.py:374
  98.8 12.6 %all-to-all-start.1 = ((f32[4,272,128]{2,1,0:T(8,128)}), f32[4,272,128]{2,1,0:T(8,128)S(1)}, u32[]{:S(2)}, u32[]{:S(2)}) async-start(f32[4,272,128]{2,1,0:T(8,128)} %shard_map.49), calls=%async_computation.1 | async-start | bytes 1114112 | tf_op jit(solution)/shard_map/all_to_all | solution.py:378
  102.3 9.1 %copy-start.2 = (f32[1360,128]{1,0:T(8,128)S(1)}, f32[1360,128]{1,0:T(8,128)}, u32[]{:S(2)}) copy-start(f32[1360,128]{1,0:T(8,128)} %copy-done.1) | copy-start | bytes 2088964
  102.3 9.1 %copy-start.4 = (f32[1280,128]{1,0:T(8,128)S(1)}, f32[1280,128]{1,0:T(8,128)}, u32[]{:S(2)}) copy-start(f32[1280,128]{1,0:T(8,128)} %copy-done.3) | copy-start | bytes 1966084
  109.4 40.8 %collective-permute-start.9 = (bf16[6,1024,128]{2,1,0:T(8,128)(2,1)}, bf16[6,1024,128]{2,1,0:T(8,128)(2,1)}, u32[]{:S(2)}, u32[]{:S(2)}) collective-permute-start(bf16[6,1024,128]{2,1,0:T(8,128)(2,1)} %pad_maximum_fusion), channel_id=1, source_target_pairs={{0,32},{32,0},{1,33},{33,1},{2,34},{34,2},{3,35},{35,3},{4,36},{36... | collective-permute-start | bytes 4718600 | tf_op jit(solution)/shard_map/ppermute | solution.py:374
  111.4 1.1 copy-start.6
  114.8 30.4 %all-to-all-start.2 = ((bf16[16,64,128]{2,1,0:T(8,128)(2,1)}), bf16[16,64,128]{2,1,0:T(8,128)(2,1)S(1)}, u32[]{:S(2)}, u32[]{:S(2)}) async-start(bf16[16,64,128]{2,1,0:T(8,128)(2,1)} %shard_map.50), calls=%async_computation.2 | async-start | bytes 524288 | tf_op jit(solution)/shard_map/all_to_all | solution.py:378
  126.5 10.2 %collective-permute-start.7 = (bf16[1024,128]{1,0:T(8,128)(2,1)S(1)}, bf16[1024,128]{1,0:T(8,128)(2,1)S(1)}, u32[]{:S(2)}, u32[]{:S(2)}) collective-permute-start(bf16[1024,128]{1,0:T(8,128)(2,1)S(1)} %slice_bitcast_fusion.1), channel_id=1, source_target_pairs={{0,64},{64,128},{128,192},{192,0},{1,65},{65,129},{129,193},{193,1... | collective-permute-start | bytes 786440 | tf_op jit(solution)/shard_map/ppermute | solution.py:374
  130.2 10.3 %collective-permute-start.8 = (bf16[1024,128]{1,0:T(8,128)(2,1)S(1)}, bf16[1024,128]{1,0:T(8,128)(2,1)S(1)}, u32[]{:S(2)}, u32[]{:S(2)}) collective-permute-start(bf16[1024,128]{1,0:T(8,128)(2,1)S(1)} %slice_bitcast_fusion), channel_id=1, source_target_pairs={{0,192},{64,0},{128,64},{192,128},{1,193},{65,1},{129,65},{193,129... | collective-permute-start | bytes 786440 | tf_op jit(solution)/shard_map/ppermute | solution.py:374
  141.3 8.8 %collective-permute-start.10 = (bf16[2,1024,128]{2,1,0:T(8,128)(2,1)}, bf16[2,1024,128]{2,1,0:T(8,128)(2,1)S(1)}, u32[]{:S(2)}, u32[]{:S(2)}) collective-permute-start(bf16[2,1024,128]{2,1,0:T(8,128)(2,1)} %pad_maximum_fusion.2), channel_id=1, source_target_pairs={{0,32},{32,0},{1,33},{33,1},{2,34},{34,2},{3,35},{35,3},{4,36},{36... | collective-permute-start | bytes 1572872 | tf_op jit(solution)/shard_map/ppermute | solution.py:374
  145.2 10.1 %collective-permute-start.18 = (bf16[1024,128]{1,0:T(8,128)(2,1)S(1)}, bf16[1024,128]{1,0:T(8,128)(2,1)S(1)}, u32[]{:S(2)}, u32[]{:S(2)}) collective-permute-start(bf16[1024,128]{1,0:T(8,128)(2,1)S(1)} %bitcast.29), channel_id=1, source_target_pairs={{0,16},{16,0},{1,17},{17,1},{2,18},{18,2},{3,19},{19,3},{4,20},{20... | collective-permute-start | bytes 786440 | tf_op jit(solution)/shard_map/ppermute | solution.py:374

commit v2 on v0

--- a/solution.py
+++ b/solution.py
@@ -57,12 +57,12 @@
     return lax.broadcasted_iota(jnp.int32, shape, axis)
 
 
-def pack_x_kernel(core_ref, p_hbm, m_hbm, x_hbm, y_hbm, left_ref, right_ref, p_ref, m_ref, part_hbm, first_ref, last_ref, sems):
+def pack_x_kernel(core_ref, p_hbm, m_hbm, x_hbm, y_hbm, left_ref, right_ref, p_ref, m_ref, part_hbm, first_ref, last_ref, part_ref, sems):
     planes, _, cx = p_ref.shape
     pairs = planes // 2
     rows = part_hbm.shape[0]
     copies = (
-        (y_hbm.at[pl.ds(pl.multiple_of(core_ref[0] * rows, rows), rows)], part_hbm),
+        (y_hbm.at[pl.ds(pl.multiple_of(core_ref[0] * rows, rows), rows)], part_ref),
         (p_hbm, p_ref),
         (m_hbm, m_ref),
         (x_hbm.at[pl.ds(0, 16)], first_ref),
@@ -71,6 +71,9 @@
     copies = [pltpu.make_async_copy(src, dst, sems.at[i]) for i, (src, dst) in enumerate(copies)]
     for copy in copies:
         copy.start()
+    copies[0].wait()
+    out = pltpu.make_async_copy(part_ref, part_hbm, sems.at[0])
+    out.start()
     for a, ref in enumerate((p_ref, m_ref)):
         copies[1 + a].wait()
         for i in range(pairs):
@@ -87,7 +90,7 @@
     for s in range(16):
         left_ref[base + s : base + s + 1, :] = first[:, s * cx : (s + 1) * cx]
         right_ref[base + s : base + s + 1, :] = last[:, s * cx : (s + 1) * cx]
-    copies[0].wait()
+    out.wait()
 
 
 def strip(x, cy):
@@ -293,28 +296,22 @@
         before = gz
 
 
-def solve_y_near_kernel(side_ref, y_hbm, u_ref, sum_ref, y_ref, sem):
+def solve_y_near_kernel(side_ref, y_hbm, u_ref, sum_ref, y_ref, near_ref, sems):
     high = side_ref[0]
     half, _ = u_ref.shape
-    copy = pltpu.make_async_copy(y_hbm, y_ref, sem)
-    copy.start()
-    copy.wait()
-    y0 = y_ref[:, pl.ds(pl.multiple_of(high * half, half), half)]
-    sum_ref[...] = jnp.dot(y0, u_ref[...], preferred_element_type=F32)
-
-
-def solve_y_far_kernel(side_ref, sum_ref, y_ref, o_ref, u0_ref, u1_ref, out_ref):
-    high, core = side_ref[0], side_ref[1]
-    half, cx = u0_ref.shape
-    k0 = pl.ds(pl.multiple_of(high * half, half), half)
-    k1 = pl.ds(pl.multiple_of((1 - high) * half, half), half)
-    mine = sum_ref[...] + jnp.dot(y_ref[:, k1], u1_ref[...], preferred_element_type=F32)
-    other = jnp.dot(o_ref[:, k0], u0_ref[...], preferred_element_type=F32)
-    other = other + jnp.dot(o_ref[:, k1], u1_ref[...], preferred_element_type=F32)
-    parts, cy, _ = out_ref.shape
-    rows = cy // 2
-    out_ref[:, pl.ds(pl.multiple_of(core * rows, rows), rows), :] = mine.astype(BF16).reshape(parts, rows, cx)
-    out_ref[:, pl.ds(pl.multiple_of((1 - core) * rows, rows), rows), :] = other.astype(BF16).reshape(parts, rows, cx)
+    halves = (high, 1 - high)
+    columns = [y_hbm.at[:, pl.ds(pl.multiple_of(h * half, half), half)] for h in halves]
+    copies = [pltpu.make_async_copy(c, ref, sems.at[i]) for i, (c, ref) in enumerate(zip(columns, (near_ref, y_ref), strict=True))]
+    for copy in copies:
+        copy.start()
+    copies[0].wait()
+    sum_ref[...] = jnp.dot(near_ref[...], u_ref[...], preferred_element_type=F32)
+    copies[1].wait()
+
+
+def solve_y_far_kernel(sum_ref, y_ref, u_ref, out_ref):
+    total = sum_ref[...] + jnp.dot(y_ref[...], u_ref[...], preferred_element_type=F32)
+    out_ref[...] = total.astype(BF16)
 
 
 def pack_x(core, p, m, x_inverse, y_inverse):
@@ -323,7 +320,7 @@
     cy, order = y_inverse.shape
     out = (kept(shape, F32),) * 2 + (kept(p.shape, F32),) * 2 + (jax.ShapeDtypeStruct((cy // 2, order), BF16),)
     rows = pltpu.VMEM((16, order), BF16)
-    scratch = (rows, rows, pltpu.SemaphoreType.DMA((5,)))
+    scratch = (rows, rows, pltpu.VMEM((cy // 2, order), BF16), pltpu.SemaphoreType.DMA((5,)))
     return call(pack_x_kernel, out, (p, m, x_inverse, y_inverse), core, scratch, range(4), (4,))
 
 
@@ -360,13 +357,14 @@
 
 
 def solve_y_near(side, y, u):
-    out = (kept((y.shape[0], u.shape[1]), F32), kept(y.shape, BF16))
-    return call(solve_y_near_kernel, out, (y, u), side, (pltpu.SemaphoreType.DMA(()),), (0,))
-
-
-def solve_y_far(side, *parts):
-    half, cx = parts[-1].shape
-    return call(solve_y_far_kernel, kept((16, half // 16, cx), BF16), parts, side)
+    half, cx = u.shape
+    out = (kept((half, cx), F32), kept((half, half), BF16))
+    scratch = (pltpu.VMEM((half, half), BF16), pltpu.SemaphoreType.DMA((2,)))
+    return call(solve_y_near_kernel, out, (y, u), side, scratch, (0,))
+
+
+def solve_y_far(*parts):
+    return call(solve_y_far_kernel, kept(parts[-1].shape, BF16), parts)
 
 
 def both_ways(to_before, to_after, axis):
@@ -385,7 +383,7 @@
     one = lambda v: v.reshape(1).astype(jnp.int32)
 
     own_l, own_r, phase_field, mobility, y_part = pack_x(one(core), phase_field, mobility, x_inverse, y_inverse)
-    y_mine = lax.all_gather(y_part, "z", axis=0, tiled=True)
+    y_rows = lax.all_gather(y_part, ("z", "c"), axis=0, tiled=True)
     left, right = both_ways(own_l, own_r, GX)
     to_up, to_down = pack_y(phase_field, mobility, left, right)
 
@@ -405,12 +403,10 @@
     updated = implicit(back, faces, planes, cy)
 
     mine = lax.all_to_all(updated, "z", 0, 0, tiled=True).reshape(half, cx)
-    y_mine, mine = lax.optimization_barrier((y_mine, mine))
+    y_rows, mine = lax.optimization_barrier((y_rows, mine))
     theirs = lax.ppermute(mine, "yh", swap)
-    side = jnp.concatenate([one(high), one(core)])
-    part, y_mine = solve_y_near(side, y_mine, mine)
-    y_other = lax.ppermute(y_mine, "c", swap)
-    out = solve_y_far(side, part, y_mine, y_other, mine, theirs)
+    part, y_far = solve_y_near(one(high), y_rows, mine)
+    out = solve_y_far(part, y_far, theirs).reshape(16, cy, cx)
     out = lax.all_to_all(out, "z", 0, 0, tiled=True)
     return out.astype(F32)
 

time: 164 us -> 153 us (0.933)
  blocking collectives: 35.7 us -> 63.6 us
  waiting for transfers between devices: 45.2 us -> 22 us
  starting transfers between devices: 45.6 us -> 34.6 us
  Pallas kernels: 20.5 us -> 15.3 us
    all_to_all x0 -> x1, blocking collectives: none -> 26.6 us  [local(): mine = lax.all_to_all(updated, 'z', 0, 0, tiled=True).reshape(half, cx)]
    all_to_all x1 -> x0, waiting for transfers between devices: 18.4 us -> none  [local(): mine = lax.all_to_all(updated, 'z', 0, 0, tiled=True).reshape(half, cx)]
    all_to_all x1 -> x0, starting transfers between devices: 9.62 us -> none  [local(): mine = lax.all_to_all(updated, 'z', 0, 0, tiled=True).reshape(half, cx)]
    pallas_call x7, Pallas kernels: 20.5 us -> 15.3 us  [call(): pl.pallas_call(kernel, out_shape=out_shape, in_specs=[pl.BlockSpec(memory...]
    ppermute x1, waiting for transfers between devices: 9.56 us -> 4.85 us  [local(): theirs = lax.ppermute(mine, 'yh', swap)]
    ppermute x1 -> x0, starting transfers between devices: 1.92 us -> none  [local(): y_other = lax.ppermute(y_mine, 'c', swap)]
  transfers between devices with their start and end apart: 12 -> 10, of which waited for: 6 -> 5; matrix products, arithmetic and copies ran while one was open for 1% -> 1% of each run, Pallas kernels for 7% -> 8%
where the time goes in v2:
time: 153 us; the launch traced here: 152 us
  blocking collectives  63.6 us (42%)
  starting transfers between devices  34.6 us (23%)
  waiting for transfers between devices  22 us (14%)
  Pallas kernels  15.3 us (10%)
  between operations  13.6 us (9%)
  local copies, waits for them, and re-layouts  2.09 us (1%)
    all_to_all x1, blocking collectives, local(): mine = lax.all_to_all(updated, 'z', 0, 0, tiled=True).reshape(half, cx)  26.6 us
    all_to_all x1, blocking collectives, local(): out = lax.all_to_all(out, 'z', 0, 0, tiled=True)  25.4 us
    pallas_call x7, Pallas kernels, call(): pl.pallas_call(kernel, out_shape=out_shape, in_specs=[pl.BlockSpec(memory...  15.3 us
    all_to_all x1, waiting for transfers between devices, local(): got = lax.all_to_all(send, GX, 0, 0, tiled=True)  12.8 us
    all_to_all x1, blocking collectives, local(): back = lax.all_to_all(back, ('yl', 'c'), 0, 0, tiled=True)  11.5 us
    ppermute x2, starting transfers between devices, both_ways(): lax.ppermute(to_before, axis, [(j, i) for i, j in up])  10.9 us
    ppermute x1, starting transfers between devices, local(): rows_yl = lax.ppermute(rows, 'yl', swap)  6.26 us
    ppermute x2, starting transfers between devices, both_ways(): lax.ppermute(to_after, axis, up)  5.57 us
  transfers between devices with their start and end apart: 10, of which 5 were waited for; matrix products, arithmetic and copies ran while one was open for 1% of the time, Pallas kernels for 8%

profile of v2, /device:TPU:16, one launch (start us, length us, event | category | flops | bytes accessed | tf_op | source)
XLA Modules:
  0.0 152.0 jit_solution(15356765704431883756)
XLA Ops:
  6.5 1.7 %shard_map.46 = (f32[48,128]{1,0:T(8,128)S(1)}, f32[48,128]{1,0:T(8,128)S(1)}, f32[16,64,128]{2,1,0:T(8,128)S(1)}, f32[16,64,128]{2,1,0:T(8,128)S(1)}, bf16[32,2048]{1,0:T(8,128)(2,1)}) custom-call(s32[1]{0:T(128)} %bitcast.1.core_ref, f32[16,64,128]{2,1,0:T(8,128)} %p_hbm.1, f32[16,64,128]{2,1,0:T(8,128)} %m_hbm.1, bf16[128,2048]{1,0:T(8,128)(2,1)} %x_hbm.1, ...), custom_call_target="tpu_custom_call" | custom-call | tf_op jit(solution)/shard_map/pallas_call | solution.py:38
  8.2 0.0 all-gather.2.cloned.1.call-update
  8.2 1.7 %collective-permute-start = (f32[48,128]{1,0:T(8,128)S(1)}, f32[48,128]{1,0:T(8,128)S(1)}, u32[]{:S(2)}, u32[]{:S(2)}) collective-permute-start(f32[48,128]{1,0:T(8,128)S(1)} %get-tuple-element.28.own_r_ref), channel_id=1, source_target_pairs={{0,32},{32,64},{64,96},{96,128},{128,160},{160,192},{192,224},{224... | collective-permute-start | bytes 73736 | tf_op jit(solution)/shard_map/ppermute | solution.py:373
  10.0 1.3 collective-permute-start.1
  11.3 0.8 fusion.2
  12.1 2.3 %collective-permute-done.1.right_ref = f32[48,128]{1,0:T(8,128)S(1)} collective-permute-done((f32[48,128]{1,0:T(8,128)S(1)}, f32[48,128]{1,0:T(8,128)S(1)}, u32[]{:S(2)}, u32[]{:S(2)}) %collective-permute-start.1) | collective-permute-done | bytes 24608 | tf_op jit(solution)/shard_map/ppermute | solution.py:373
  14.4 0.0 collective-permute-done.left_ref
  14.4 0.2 shard_map.47
  14.6 0.4 concatenate.3.x0_ref
  15.0 6.3 %collective-permute-start.5 = (bf16[144,2048]{1,0:T(8,128)(2,1)S(1)}, bf16[144,2048]{1,0:T(8,128)(2,1)}, u32[]{:S(2)}, u32[]{:S(2)}) collective-permute-start(bf16[144,2048]{1,0:T(8,128)(2,1)S(1)} %concatenate.3.x0_ref), channel_id=1, source_target_pairs={{0,256},{256,0},{1,257},{257,1},{2,258},{258,2},{3,259},{259,3},{4... | collective-permute-start | bytes 1769480 | tf_op jit(solution)/shard_map/ppermute | solution.py:396
  21.3 3.8 %collective-permute-start.2 = (f32[7,16,128]{2,1,0:T(8,128)S(1)}, f32[7,16,128]{2,1,0:T(8,128)S(1)}, u32[]{:S(2)}, u32[]{:S(2)}) collective-permute-start(f32[7,16,128]{2,1,0:T(8,128)S(1)} %get-tuple-element.30), channel_id=1, source_target_pairs={{0,1},{1,2},{2,3},{3,4},{4,5},{5,6},{6,7},{7,8},{8,9},{9,10},{10,1... | collective-permute-start | bytes 172040 | tf_op jit(solution)/shard_map/ppermute | solution.py:373
  25.1 9.6 %collective-permute-start.3 = (f32[7,16,128]{2,1,0:T(8,128)S(1)}, f32[7,16,128]{2,1,0:T(8,128)S(1)}, u32[]{:S(2)}, u32[]{:S(2)}) collective-permute-start(f32[7,16,128]{2,1,0:T(8,128)S(1)} %get-tuple-element.31), channel_id=1, source_target_pairs={{1,0},{2,1},{3,2},{4,3},{5,4},{6,5},{7,6},{8,7},{9,8},{10,9},{11,1... | collective-permute-start | bytes 172040 | tf_op jit(solution)/shard_map/ppermute | solution.py:373
  34.7 1.0 collective-permute-done.2.up_ref
  35.7 1.1 collective-permute-done.3.down_ref
  36.8 5.0 %shard_map.48 = (bf16[16,272,128]{2,1,0:T(8,128)(2,1)}, f32[1360,128]{1,0:T(8,128)S(1)}, f32[1280,128]{1,0:T(8,128)S(1)}, f32[1280,128]{1,0:T(8,128)S(1)}, f32[16,128]{1,0:T(8,128)S(1)}) custom-call(f32[16,64,128]{2,1,0:T(8,128)S(1)} %get-tuple-element.25.p_ref, f32[16,64,128]{2,1,0:T(8,128)S(1)} %get-tuple-element.26.m_ref, ...), custom_call_target="tpu_custom_call" | custom-call | tf_op jit(solution)/shard_map/pallas_call | solution.py:38
  41.8 0.9 copy-done
  42.7 5.0 %all-to-all-start = ((bf16[16,272,128]{2,1,0:T(8,128)(2,1)}), bf16[16,272,128]{2,1,0:T(8,128)(2,1)S(1)}, u32[]{:S(2)}, u32[]{:S(2)}) async-start(bf16[16,272,128]{2,1,0:T(8,128)(2,1)} %get-tuple-element.32), calls=%async_computation | async-start | bytes 2228224 | tf_op jit(solution)/shard_map/all_to_all | solution.py:400
  47.7 2.3 %collective-permute-start.4 = (bf16[144,2048]{1,0:T(8,128)(2,1)S(1)}, bf16[144,2048]{1,0:T(8,128)(2,1)}, u32[]{:S(2)}, u32[]{:S(2)}) collective-permute-start(bf16[144,2048]{1,0:T(8,128)(2,1)S(1)} %concatenate.3.x0_ref), channel_id=1, source_target_pairs={{0,32},{32,0},{1,33},{33,1},{2,34},{34,2},{3,35},{35,3},{4,36},{36... | collective-permute-start | bytes 1769480 | tf_op jit(solution)/shard_map/ppermute | solution.py:397
  50.0 0.0 collective-permute-done.5.x2_ref
  50.0 2.0 %collective-permute-start.6 = (bf16[144,2048]{1,0:T(8,128)(2,1)}, bf16[144,2048]{1,0:T(8,128)(2,1)}, u32[]{:S(2)}, u32[]{:S(2)}) collective-permute-start(bf16[144,2048]{1,0:T(8,128)(2,1)} %collective-permute-done.5.x2_ref), channel_id=1, source_target_pairs={{0,32},{32,0},{1,33},{33,1},{2,34},{34,2},{3,35},{35,3},{4,36},{36... | collective-permute-start | bytes 1769480 | tf_op jit(solution)/shard_map/ppermute | solution.py:397
  52.0 0.0 collective-permute-done.4.x1_ref
  52.1 12.8 %all-to-all-done.got_ref = bf16[16,272,128]{2,1,0:T(8,128)(2,1)S(1)} async-done(((bf16[16,272,128]{2,1,0:T(8,128)(2,1)}), bf16[16,272,128]{2,1,0:T(8,128)(2,1)S(1)}, u32[]{:S(2)}, u32[]{:S(2)}) %all-to-all-start) | async-done | bytes 1114144 | tf_op jit(solution)/shard_map/all_to_all | solution.py:400
  64.8 3.8 %shard_map.49 = f32[4,272,128]{2,1,0:T(8,128)S(1)} custom-call(s32[1]{0:T(128)} %bitcast.2.block_ref, bf16[16,272,128]{2,1,0:T(8,128)(2,1)S(1)} %all-to-all-done.got_ref, bf16[144,2048]{1,0:T(8,128)(2,1)S(1)} %concatenate.3.x0_ref, bf16[144,2048]{1,0:T(8,128)(2,1)} %collective-permute-done.4.x1_ref, bf16[144,2048]{1,0:T(8,128)(2,1)} %collective-permute-done.5.x2_ref, ...), custom_call_target="tpu_custom_call" | custom-call | tf_op jit(solution)/shard_map/pallas_call | solution.py:38
  68.7 11.5 %all_to_all.20.back_ref = f32[4,272,128]{2,1,0:T(8,128)S(1)} all-to-all(f32[4,272,128]{2,1,0:T(8,128)S(1)} %shard_map.49), channel_id=1, replica_groups=mesh['yl'=2,'x'=4,'c'=2,'yh'=2,'z'=16] {'yl','c'}, dimensions={0} | all-to-all | bytes 1114112 | tf_op jit(solution)/shard_map/all_to_all | solution.py:402
  80.2 1.6 %shard_map.50 = bf16[16,64,128]{2,1,0:T(8,128)(2,1)S(1)} custom-call(f32[4,272,128]{2,1,0:T(8,128)S(1)} %all_to_all.20.back_ref, f32[1360,128]{1,0:T(8,128)S(1)} %get-tuple-element.35.fz_ref, f32[1280,128]{1,0:T(8,128)S(1)} %get-tuple-element.36.fy_ref, f32[1280,128]{1,0:T(8,128)S(1)} %copy-done.1, f32[16,128]{1,0:T(8,128)S(1)} %get-tuple-element.38.edge_ref), custom_call_target="tpu_custom_call" | custom-call | tf_op jit(solution)/shard_map/pallas_call | solution.py:38
  81.8 26.6 %all_to_all.21 = bf16[16,64,128]{2,1,0:T(8,128)(2,1)S(1)} all-to-all(bf16[16,64,128]{2,1,0:T(8,128)(2,1)S(1)} %shard_map.50), channel_id=1, replica_groups=mesh['yl'=2,'x'=4,'c'=2,'yh'=2,'z'=16] {'z'}, dimensions={0} | all-to-all | bytes 524288 | tf_op jit(solution)/shard_map/all_to_all | solution.py:405
  108.4 2.6 %collective-permute-start.7 = (bf16[1024,128]{1,0:T(8,128)(2,1)S(1)}, bf16[1024,128]{1,0:T(8,128)(2,1)S(1)}, u32[]{:S(2)}, u32[]{:S(2)}) collective-permute-start(bf16[1024,128]{1,0:T(8,128)(2,1)S(1)} %bitcast.17), channel_id=1, source_target_pairs={{0,16},{16,0},{1,17},{17,1},{2,18},{18,2},{3,19},{19,3},{4,20},{20... | collective-permute-start | bytes 786440 | tf_op jit(solution)/shard_map/ppermute | solution.py:407
  111.0 2.3 %shard_map.51 = (f32[1024,128]{1,0:T(8,128)S(1)}, bf16[1024,1024]{1,0:T(8,128)(2,1)S(1)}) custom-call(s32[1]{0:T(128)} %bitcast.side_ref, bf16[1024,2048]{1,0:T(8,128)(2,1)} %all-gather.2.cloned.1.call-done.y_hbm, bf16[1024,128]{1,0:T(8,128)(2,1)S(1)} %bitcast.18), custom_call_target="tpu_custom_call" | custom-call | tf_op jit(solution)/shard_map/pallas_call | solution.py:38
  113.3 4.9 %collective-permute-done.7.u_ref = bf16[1024,128]{1,0:T(8,128)(2,1)S(1)} collective-permute-done((bf16[1024,128]{1,0:T(8,128)(2,1)S(1)}, bf16[1024,128]{1,0:T(8,128)(2,1)S(1)}, u32[]{:S(2)}, u32[]{:S(2)}) %collective-permute-start.7) | collective-permute-done | bytes 262176 | tf_op jit(solution)/shard_map/ppermute | solution.py:407
  118.2 0.7 shard_map.52
  118.9 25.4 %all_to_all.22 = bf16[16,64,128]{2,1,0:T(8,128)(2,1)S(1)} all-to-all(bf16[16,64,128]{2,1,0:T(8,128)(2,1)S(1)} %bitcast.19), channel_id=1, replica_groups=mesh['yl'=2,'x'=4,'c'=2,'yh'=2,'z'=16] {'z'}, dimensions={0} | all-to-all | bytes 524288 | tf_op jit(solution)/shard_map/all_to_all | solution.py:410
  144.3 0.8 convert_element_type.29
  (13 shorter events, 0.0 us)
Async XLA Ops:
  6.5 8.1 %copy-start.2 = (bf16[128,2048]{1,0:T(8,128)(2,1)S(1)}, bf16[128,2048]{1,0:T(8,128)(2,1)}, u32[]{:S(2)}) copy-start(bf16[128,2048]{1,0:T(8,128)(2,1)} %x_hbm.1) | copy-start | bytes 1572868
  6.5 101.9 %all-gather.2.cloned.1.call-start = ((), (), s32[]{:S(2)}) async-start(), calls=%async_computation.4 | async-start | bytes 4325376 | tf_op jit(solution)/shard_map/all_gather | solution.py:386
  8.2 6.1 %collective-permute-start = (f32[48,128]{1,0:T(8,128)S(1)}, f32[48,128]{1,0:T(8,128)S(1)}, u32[]{:S(2)}, u32[]{:S(2)}) collective-permute-start(f32[48,128]{1,0:T(8,128)S(1)} %get-tuple-element.28.own_r_ref), channel_id=1, source_target_pairs={{0,32},{32,64},{64,96},{96,128},{128,160},{160,192},{192,224},{224... | collective-permute-start | bytes 73736 | tf_op jit(solution)/shard_map/ppermute | solution.py:373
  10.0 4.4 %collective-permute-start.1 = (f32[48,128]{1,0:T(8,128)S(1)}, f32[48,128]{1,0:T(8,128)S(1)}, u32[]{:S(2)}, u32[]{:S(2)}) collective-permute-start(f32[48,128]{1,0:T(8,128)S(1)} %get-tuple-element.27.own_l_ref), channel_id=1, source_target_pairs={{32,0},{64,32},{96,64},{128,96},{160,128},{192,160},{224,192},{256... | collective-permute-start | bytes 73736 | tf_op jit(solution)/shard_map/ppermute | solution.py:373
  15.0 35.0 %collective-permute-start.5 = (bf16[144,2048]{1,0:T(8,128)(2,1)S(1)}, bf16[144,2048]{1,0:T(8,128)(2,1)}, u32[]{:S(2)}, u32[]{:S(2)}) collective-permute-start(bf16[144,2048]{1,0:T(8,128)(2,1)S(1)} %concatenate.3.x0_ref), channel_id=1, source_target_pairs={{0,256},{256,0},{1,257},{257,1},{2,258},{258,2},{3,259},{259,3},{4... | collective-permute-start | bytes 1769480 | tf_op jit(solution)/shard_map/ppermute | solution.py:396
  21.3 14.4 %collective-permute-start.2 = (f32[7,16,128]{2,1,0:T(8,128)S(1)}, f32[7,16,128]{2,1,0:T(8,128)S(1)}, u32[]{:S(2)}, u32[]{:S(2)}) collective-permute-start(f32[7,16,128]{2,1,0:T(8,128)S(1)} %get-tuple-element.30), channel_id=1, source_target_pairs={{0,1},{1,2},{2,3},{3,4},{4,5},{5,6},{6,7},{7,8},{8,9},{9,10},{10,1... | collective-permute-start | bytes 172040 | tf_op jit(solution)/shard_map/ppermute | solution.py:373
  25.1 11.7 %collective-permute-start.3 = (f32[7,16,128]{2,1,0:T(8,128)S(1)}, f32[7,16,128]{2,1,0:T(8,128)S(1)}, u32[]{:S(2)}, u32[]{:S(2)}) collective-permute-start(f32[7,16,128]{2,1,0:T(8,128)S(1)} %get-tuple-element.31), channel_id=1, source_target_pairs={{1,0},{2,1},{3,2},{4,3},{5,4},{6,5},{7,6},{8,7},{9,8},{10,9},{11,1... | collective-permute-start | bytes 172040 | tf_op jit(solution)/shard_map/ppermute | solution.py:373
  41.8 0.9 copy-start
  42.7 22.2 %all-to-all-start = ((bf16[16,272,128]{2,1,0:T(8,128)(2,1)}), bf16[16,272,128]{2,1,0:T(8,128)(2,1)S(1)}, u32[]{:S(2)}, u32[]{:S(2)}) async-start(bf16[16,272,128]{2,1,0:T(8,128)(2,1)} %get-tuple-element.32), calls=%async_computation | async-start | bytes 2228224 | tf_op jit(solution)/shard_map/all_to_all | solution.py:400
  47.7 4.4 %collective-permute-start.4 = (bf16[144,2048]{1,0:T(8,128)(2,1)S(1)}, bf16[144,2048]{1,0:T(8,128)(2,1)}, u32[]{:S(2)}, u32[]{:S(2)}) collective-permute-start(bf16[144,2048]{1,0:T(8,128)(2,1)S(1)} %concatenate.3.x0_ref), channel_id=1, source_target_pairs={{0,32},{32,0},{1,33},{33,1},{2,34},{34,2},{3,35},{35,3},{4,36},{36... | collective-permute-start | bytes 1769480 | tf_op jit(solution)/shard_map/ppermute | solution.py:397
  50.0 14.8 %collective-permute-start.6 = (bf16[144,2048]{1,0:T(8,128)(2,1)}, bf16[144,2048]{1,0:T(8,128)(2,1)}, u32[]{:S(2)}, u32[]{:S(2)}) collective-permute-start(bf16[144,2048]{1,0:T(8,128)(2,1)} %collective-permute-done.5.x2_ref), channel_id=1, source_target_pairs={{0,32},{32,0},{1,33},{33,1},{2,34},{34,2},{3,35},{35,3},{4,36},{36... | collective-permute-start | bytes 1769480 | tf_op jit(solution)/shard_map/ppermute | solution.py:397
  64.8 15.4 %copy-start.1 = (f32[1280,128]{1,0:T(8,128)S(1)}, f32[1280,128]{1,0:T(8,128)}, u32[]{:S(2)}) copy-start(f32[1280,128]{1,0:T(8,128)} %copy-done) | copy-start | bytes 1966084
  108.4 9.8 %collective-permute-start.7 = (bf16[1024,128]{1,0:T(8,128)(2,1)S(1)}, bf16[1024,128]{1,0:T(8,128)(2,1)S(1)}, u32[]{:S(2)}, u32[]{:S(2)}) collective-permute-start(bf16[1024,128]{1,0:T(8,128)(2,1)S(1)} %bitcast.17), channel_id=1, source_target_pairs={{0,16},{16,0},{1,17},{17,1},{2,18},{18,2},{3,19},{19,3},{4,20},{20... | collective-permute-start | bytes 786440 | tf_op jit(solution)/shard_map/ppermute | solution.py:407
Sparse Core Ops, SparseCore 0:
  9.5 77.9 all-gather.1

commit v3 on v2

--- a/solution.py
+++ b/solution.py
@@ -57,7 +57,7 @@
     return lax.broadcasted_iota(jnp.int32, shape, axis)
 
 
-def pack_x_kernel(core_ref, p_hbm, m_hbm, x_hbm, y_hbm, left_ref, right_ref, p_ref, m_ref, part_hbm, first_ref, last_ref, part_ref, sems):
+def pack_x_kernel(core_ref, p_hbm, m_hbm, x_hbm, y_hbm, left_ref, right_ref, p_ref, m_ref, x_ref, part_hbm, part_ref, sems):
     planes, _, cx = p_ref.shape
     pairs = planes // 2
     rows = part_hbm.shape[0]
@@ -65,8 +65,7 @@
         (y_hbm.at[pl.ds(pl.multiple_of(core_ref[0] * rows, rows), rows)], part_ref),
         (p_hbm, p_ref),
         (m_hbm, m_ref),
-        (x_hbm.at[pl.ds(0, 16)], first_ref),
-        (x_hbm.at[pl.ds(x_hbm.shape[0] - 16, 16)], last_ref),
+        (x_hbm, x_ref),
     )
     copies = [pltpu.make_async_copy(src, dst, sems.at[i]) for i, (src, dst) in enumerate(copies)]
     for copy in copies:
@@ -84,9 +83,8 @@
                 right_ref[k : k + 1, :] = t[cx - 2 + j : cx - 1 + j]
     base = 4 * pairs
     copies[3].wait()
-    copies[4].wait()
-    first = first_ref[0:1, :].astype(F32)
-    last = last_ref[15:16, :].astype(F32)
+    first = x_ref[0:16, :][0:1].astype(F32)
+    last = x_ref[cx - 16 : cx, :][15:16].astype(F32)
     for s in range(16):
         left_ref[base + s : base + s + 1, :] = first[:, s * cx : (s + 1) * cx]
         right_ref[base + s : base + s + 1, :] = last[:, s * cx : (s + 1) * cx]
@@ -104,7 +102,7 @@
     return [strip(ref[k * pairs : (k + 1) * pairs, :], cy) for ref, k in refs]
 
 
-def pack_y_kernel(p_ref, m_ref, left_ref, right_ref, up_ref, down_ref):
+def pack_y_kernel(p_ref, m_ref, x_ref, left_ref, right_ref, up_ref, down_ref, rows_ref, row_ref):
     planes, cy, cx = p_ref.shape
     for a, ref in enumerate((p_ref, m_ref)):
         for r in range(3):
@@ -121,12 +119,21 @@
             down = jnp.where(here, turn(s, at - OFF, 1), down)
     up_ref[6] = up
     down_ref[6] = down
+    rows_ref[:cx] = x_ref[...]
+    row_ref[...] = jnp.zeros(row_ref.shape, F32)
+    base = left_ref.shape[0] - 16
+    for s in range(16):
+        row_ref[0:1, s * cx : (s + 1) * cx] = left_ref[base + s : base + s + 1, :]
+        row_ref[3:4, s * cx : (s + 1) * cx] = right_ref[base + s : base + s + 1, :]
+    row_ref[1:2, :] = x_ref[0:16, :][0:1].astype(F32)
+    row_ref[2:3, :] = x_ref[cx - 16 : cx, :][15:16].astype(F32)
+    rows_ref[cx:] = row_ref[...].astype(BF16)
 
 
 def explicit_kernel(
     p_ref, m_ref, own_l_ref, own_r_ref, left_ref, right_ref, up_ref, down_ref,
-    send_ref, fz_ref, fy_ref, fx_ref, edge_ref,
-    v_ref, c_ref, f_ref, side_ref, rim_ref,
+    send_ref, fz_ref, fy_ref, fx_hbm, edge_ref,
+    v_ref, c_ref, f_ref, fx_ref, side_ref, rim_ref, sem,
 ):
     planes, cy, cx = p_ref.shape
     pairs = planes // 2
@@ -175,9 +182,11 @@
     stacked = jnp.concatenate(columns + [jnp.zeros((cx - 4 * planes, cx), F32)], axis=0)
     across = stacked.T[:tall]
 
-    def column(k, z):
+    part = tall // 2
+
+    def column(k, z, h):
         at = k * planes + z
-        return jnp.broadcast_to(across[:, at : at + 1], (tall, cx))
+        return jnp.broadcast_to(across[h * part : (h + 1) * part, at : at + 1], (part, cx))
 
     blank = jnp.zeros((OFF, cx), F32)
     for ref in (v_ref, c_ref, f_ref):
@@ -193,41 +202,52 @@
             ref[pl.ds(tall + OFF - 3 + r, planes, stride=tall), :] = up_ref[3 * a + r]
             ref[pl.ds(tall + OFF + cy + r, planes, stride=tall), :] = down_ref[3 * a + r]
 
-    wide = places((tall, cx), 1)
-
-    def step(v, above, fz, fy, fx, gz_before, gl, gr):
-        gz = fz * (above - v)
-        gy = fy * (turn(v, -1, 0) - v)
+    wide = places((part, cx), 1)
+
+    def step(ref, z, h, fz, fy, fx, gz_before, gl, gr):
+        at = (z + 1) * tall + h * part
+        v = ref[at : at + part, :]
+        gz = fz * (ref[at + tall : at + tall + part, :] - v)
+        gy = fy * (ref[at + 1 : at + 1 + part, :] - v)
+        flat = OFF + z * tall + h * part - 1
+        gu = fy_ref[flat : flat + part, :] * (v - ref[at - 1 : at - 1 + part, :])
         gx = jnp.where(wide == 0, gl, fx * (v - turn(v, 1, 1)))
-        lap = gz - gz_before + gy - turn(gy, 1, 0)
-        lap = lap + jnp.where(wide == cx - 1, gr, turn(gx, -1, 1)) - gx
+        lap = gz - gz_before + gy - gu + jnp.where(wide == cx - 1, gr, turn(gx, -1, 1)) - gx
         return v + step_size * lap, gz
 
     fz_ref[:tall, :] = jnp.zeros((tall, cx), F32)
-    before = jnp.zeros((tall, cx), F32)
+    fy_ref[:OFF, :] = jnp.zeros((OFF, cx), F32)
+    for h in range(2):
+        before = jnp.zeros((part, cx), F32)
+        for z in range(planes):
+            at = (z + 1) * tall + h * part
+            flat = z * tall + h * part
+            m = c_ref[at : at + part, :]
+            fz = face_mob(m, c_ref[at + tall : at + tall + part, :])
+            fy = face_mob(m, c_ref[at + 1 : at + 1 + part, :])
+            fx = face_mob(m, turn(m, 1, 1))
+            fz_ref[at : at + part, :] = fz
+            fy_ref[OFF + flat : OFF + flat + part, :] = fy
+            fx_ref[flat : flat + part, :] = fx
+            out, before = step(v_ref, z, h, fz, fy, fx, before, column(0, z, h), column(2, z, h))
+            f_ref[at : at + part, :] = out
+    leave = pltpu.make_async_copy(fx_ref, fx_hbm, sem)
+    leave.start()
+
+    rim_ref[...] = jnp.zeros(rim_ref.shape, F32)
+    quarter = planes // 4
+    for h in range(2):
+        before = jnp.zeros((part, cx), F32)
+        for z in range(planes):
+            at = (z + 1) * tall + h * part
+            flat = z * tall + h * part
+            out, before = step(
+                f_ref, z, h, fz_ref[at : at + part, :], fy_ref[OFF + flat : OFF + flat + part, :],
+                fx_ref[flat : flat + part, :], before, column(1, z, h), column(3, z, h),
+            )
+            v_ref[at : at + part, :] = out
     for z in range(planes):
-        here, above = pl.ds((z + 1) * tall, tall), pl.ds((z + 2) * tall, tall)
-        flat = pl.ds(z * tall, tall)
-        m = c_ref[here, :]
-        fz = face_mob(m, c_ref[above, :])
-        fy = face_mob(m, turn(m, -1, 0))
-        fx = face_mob(m, turn(m, 1, 1))
-        fz_ref[here, :] = fz
-        fy_ref[flat, :] = fy
-        fx_ref[flat, :] = fx
-        out, before = step(v_ref[here, :], v_ref[above, :], fz, fy, fx, before, column(0, z), column(2, z))
-        f_ref[here, :] = out
-
-    rim_ref[...] = jnp.zeros(rim_ref.shape, F32)
-    before = jnp.zeros((tall, cx), F32)
-    quarter = planes // 4
-    for z in range(planes):
-        here, above = pl.ds((z + 1) * tall, tall), pl.ds((z + 2) * tall, tall)
-        flat = pl.ds(z * tall, tall)
-        out, before = step(
-            f_ref[here, :], f_ref[above, :], fz_ref[here, :], fy_ref[flat, :], fx_ref[flat, :],
-            before, column(1, z), column(3, z),
-        )
+        out = v_ref[(z + 1) * tall : (z + 2) * tall, :]
         q, at = z // quarter, z % quarter
         body = out[OFF : OFF + cy].astype(BF16)
         for x in range(4):
@@ -238,14 +258,21 @@
         rims = rim_ref[q].astype(BF16)
         for x in range(4):
             send_ref[(q // 2) * 8 + x * 2 + q % 2, quarter * cy :, :] = rims
-
-
-def solve_x_kernel(block_ref, got_ref, x0_ref, x1_ref, x2_ref, x3_ref, out_ref):
+    leave.wait()
+
+
+def solve_x_kernel(block_ref, got_ref, x0_ref, x1_hbm, x2_hbm, x3_hbm, out_ref, x1_ref, x2_ref, x3_ref, sems):
     own = block_ref[0]
     parts, lines, cx = got_ref.shape
     main = lines - 16
+    moves = ((x1_hbm, x1_ref), (x2_hbm, x2_ref), (x3_hbm, x3_ref))
+    copies = [pltpu.make_async_copy(src, dst, sems.at[i]) for i, (src, dst) in enumerate(moves)]
+    for copy in copies:
+        copy.start()
     a = jnp.concatenate([got_ref[s] for s in range(parts)], axis=1)
     for other, x_ref in enumerate((x0_ref, x1_ref, x2_ref, x3_ref)):
+        if other:
+            copies[other - 1].wait()
         block = own ^ other
         m = lax.dot_general(a, x_ref[:cx], NT, preferred_element_type=F32)
         out_ref[block, : main + 8] = m[: main + 8]
@@ -254,11 +281,14 @@
         out_ref[block, main + 12 :] = e[:4, cx:]
 
 
-def implicit_kernel(back_ref, fz_ref, fy_ref, fx_ref, edge_ref, out_ref, c_ref, e_ref):
+def implicit_kernel(back_ref, fz_ref, fy_ref, fx_hbm, edge_ref, out_ref, c_ref, e_ref, fx_ref, sem):
     planes, cy, cx = out_ref.shape
     tall = cy + 2 * OFF
     quarter, pairs = planes // 4, planes // 2
     main = quarter * cy
+
+    come = pltpu.make_async_copy(fx_hbm, fx_ref, sem)
+    come.start()
 
     def chemical(s):
         return s * s * s - s
@@ -279,13 +309,14 @@
     across = jnp.concatenate([left, right, jnp.zeros((cx - planes, cx), F32)], axis=0).T
     lane = places((cy, cx), 1)
     before = jnp.zeros((cy, cx), F32)
+    come.wait()
     for z in range(planes):
         base = (z + 1) * tall + OFF
         flat = z * tall + OFF
         c = c_ref[base : base + cy, :]
         gz = fz_ref[base : base + cy, :] * (c_ref[base + tall : base + tall + cy, :] - c)
-        gy = fy_ref[flat : flat + cy, :] * (c_ref[base + 1 : base + 1 + cy, :] - c)
-        gu = fy_ref[flat - 1 : flat - 1 + cy, :] * (c - c_ref[base - 1 : base - 1 + cy, :])
+        gy = fy_ref[flat + OFF : flat + OFF + cy, :] * (c_ref[base + 1 : base + 1 + cy, :] - c)
+        gu = fy_ref[flat + OFF - 1 : flat + OFF - 1 + cy, :] * (c - c_ref[base - 1 : base - 1 + cy, :])
         rows = slice((z % 2) * cy, (z % 2 + 1) * cy)
         gl = jnp.broadcast_to(across[rows, z // 2 : z // 2 + 1], (cy, cx))
         gr = jnp.broadcast_to(across[rows, pairs + z // 2 : pairs + z // 2 + 1], (cy, cx))
@@ -318,15 +349,16 @@
     cx = p.shape[2]
     shape = (2 * p.shape[0] + 16, cx)
     cy, order = y_inverse.shape
-    out = (kept(shape, F32),) * 2 + (kept(p.shape, F32),) * 2 + (jax.ShapeDtypeStruct((cy // 2, order), BF16),)
-    rows = pltpu.VMEM((16, order), BF16)
-    scratch = (rows, rows, pltpu.VMEM((cy // 2, order), BF16), pltpu.SemaphoreType.DMA((5,)))
-    return call(pack_x_kernel, out, (p, m, x_inverse, y_inverse), core, scratch, range(4), (4,))
-
-
-def pack_y(p, m, left, right):
-    shape = (7, p.shape[0], p.shape[2])
-    return call(pack_y_kernel, (kept(shape, F32),) * 2, (p, m, left, right))
+    out = (kept(shape, F32),) * 2 + (kept(p.shape, F32),) * 2 + (kept(x_inverse.shape, BF16),)
+    out += (jax.ShapeDtypeStruct((cy // 2, order), BF16),)
+    scratch = (pltpu.VMEM((cy // 2, order), BF16), pltpu.SemaphoreType.DMA((4,)))
+    return call(pack_x_kernel, out, (p, m, x_inverse, y_inverse), core, scratch, range(4), (5,))
+
+
+def pack_y(p, m, x_inverse, left, right):
+    cx, order = x_inverse.shape
+    out = (kept((7, p.shape[0], cx), F32),) * 2 + (kept((cx + 16, order), BF16),)
+    return call(pack_y_kernel, out, (p, m, x_inverse, left, right), scratch=(pltpu.VMEM((16, order), F32),))
 
 
 def explicit(*args):
@@ -337,23 +369,28 @@
     out = (
         kept((16, lines, cx), BF16),
         kept(((planes + 1) * tall, cx), F32),
-        kept((planes * tall, cx), F32),
-        kept((planes * tall, cx), F32),
+        kept((planes * tall + OFF, cx), F32),
+        jax.ShapeDtypeStruct((planes * tall, cx), F32),
         kept((planes, cx), F32),
     )
-    scratch = (field, field, field, pltpu.VMEM((planes, cx), F32), pltpu.VMEM((4, 16, cx), F32))
-    return call(explicit_kernel, out, args, scratch=scratch)
+    scratch = (field, field, field, pltpu.VMEM((planes * tall, cx), F32), pltpu.VMEM((planes, cx), F32))
+    scratch += (pltpu.VMEM((4, 16, cx), F32), pltpu.SemaphoreType.DMA(()))
+    return call(explicit_kernel, out, args, scratch=scratch, far_out=(3,))
 
 
 def solve_x(block, got, x_blocks):
     _, lines, cx = got.shape
-    return call(solve_x_kernel, kept((4, lines, cx), F32), (got, *x_blocks), scalar=block)
+    blocks = pltpu.VMEM(x_blocks[0].shape, BF16)
+    scratch = (blocks, blocks, blocks, pltpu.SemaphoreType.DMA((3,)))
+    return call(solve_x_kernel, kept((4, lines, cx), F32), (got, *x_blocks), block, scratch, (2, 3, 4))
 
 
 def implicit(back, faces, planes, cy):
     cx = back.shape[2]
-    scratch = (pltpu.VMEM(((planes + 2) * (cy + 2 * OFF), cx), F32), pltpu.VMEM((32, cx), F32))
-    return call(implicit_kernel, kept((planes, cy, cx), BF16), (back, *faces), scratch=scratch)
+    tall = cy + 2 * OFF
+    scratch = (pltpu.VMEM(((planes + 2) * tall, cx), F32), pltpu.VMEM((32, cx), F32))
+    scratch += (pltpu.VMEM((planes * tall, cx), F32), pltpu.SemaphoreType.DMA(()))
+    return call(implicit_kernel, kept((planes, cy, cx), BF16), (back, *faces), None, scratch, (3,))
 
 
 def solve_y_near(side, y, u):
@@ -382,17 +419,11 @@
 
     one = lambda v: v.reshape(1).astype(jnp.int32)
 
-    own_l, own_r, phase_field, mobility, y_part = pack_x(one(core), phase_field, mobility, x_inverse, y_inverse)
+    own_l, own_r, phase_field, mobility, x_own, y_part = pack_x(one(core), phase_field, mobility, x_inverse, y_inverse)
     y_rows = lax.all_gather(y_part, ("z", "c"), axis=0, tiled=True)
     left, right = both_ways(own_l, own_r, GX)
-    to_up, to_down = pack_y(phase_field, mobility, left, right)
-
-    row_before = left[-16:].reshape(1, order).astype(BF16)
-    row_after = right[-16:].reshape(1, order).astype(BF16)
-    row_before, row_after, to_up = lax.optimization_barrier((row_before, row_after, to_up))
-    ends = [x_inverse, row_before, x_inverse[:1], x_inverse[-1:], row_after, jnp.zeros((12, order), BF16)]
+    to_up, to_down, rows = pack_y(phase_field, mobility, x_own, left, right)
     up, down = both_ways(to_down, to_up, GY)
-    rows = jnp.concatenate(ends, axis=0)
     rows_yl = lax.ppermute(rows, "yl", swap)
     x_blocks = (rows, lax.ppermute(rows, "c", swap), rows_yl, lax.ppermute(rows_yl, "c", swap))
 

time: 153 us -> 155 us (1.013)
  the two profiles are of different devices: /device:TPU:16 before, /device:TPU:32 now
where the time goes in v3:
time: 155 us; the launch traced here: 154 us
  blocking collectives  69 us (45%)
  starting transfers between devices  28.6 us (18%)
  waiting for transfers between devices  23.7 us (15%)
  Pallas kernels  17.7 us (11%)
  between operations  13.6 us (9%)
    all_to_all x1, blocking collectives, local(): mine = lax.all_to_all(updated, 'z', 0, 0, tiled=True).reshape(half, cx)  33.3 us
    all_to_all x1, blocking collectives, local(): out = lax.all_to_all(out, 'z', 0, 0, tiled=True)  24.1 us
    pallas_call x7, Pallas kernels, call(): pl.pallas_call(kernel, out_shape=out_shape, in_specs=[pl.BlockSpec(memory...  17.7 us
    all_to_all x1, waiting for transfers between devices, local(): got = lax.all_to_all(send, GX, 0, 0, tiled=True)  12.8 us
    all_to_all x1, blocking collectives, local(): back = lax.all_to_all(back, ('yl', 'c'), 0, 0, tiled=True)  11.5 us
    ppermute x2, waiting for transfers between devices, both_ways(): lax.ppermute(to_before, axis, [(j, i) for i, j in up])  6.89 us
    ppermute x1, starting transfers between devices, local(): rows_yl = lax.ppermute(rows, 'yl', swap)  6.56 us
    ppermute x2, starting transfers between devices, both_ways(): lax.ppermute(to_after, axis, up)  5.57 us
  transfers between devices with their start and end apart: 10, of which 5 were waited for; matrix products, arithmetic and copies ran while one was open for 0% of the time, Pallas kernels for 10%

profile of v3, /device:TPU:32, one launch (start us, length us, event | category | flops | bytes accessed | tf_op | source)
XLA Modules:
  0.0 154.2 jit_solution(12912093787719447503)
XLA Ops:
  6.5 0.0 all-gather.2.cloned.1.call-start
  6.5 1.6 %shard_map.46 = (f32[48,128]{1,0:T(8,128)S(1)}, f32[48,128]{1,0:T(8,128)S(1)}, f32[16,64,128]{2,1,0:T(8,128)S(1)}, f32[16,64,128]{2,1,0:T(8,128)S(1)}, bf16[128,...) custom-call(s32[1]{0:T(128)} %bitcast.1.core_ref, f32[16,64,128]{2,1,0:T(8,128)} %p_hbm.1, f32[16,64,128]{2,1,0:T(8,128)} %m_hbm.1, ...), custom_call_target="tpu_custom_call" | custom-call | tf_op jit(solution)/shard_map/pallas_call | solution.py:38
  8.1 0.0 all-gather.2.cloned.1.call-update
  8.2 1.7 %collective-permute-start = (f32[48,128]{1,0:T(8,128)S(1)}, f32[48,128]{1,0:T(8,128)S(1)}, u32[]{:S(2)}, u32[]{:S(2)}) collective-permute-start(f32[48,128]{1,0:T(8,128)S(1)} %get-tuple-element.27.own_r_ref), channel_id=1, source_target_pairs={{0,32},{32,64},{64,96},{96,128},{128,160},{160,192},{192,224},{224... | collective-permute-start | bytes 73736 | tf_op jit(solution)/shard_map/ppermute | solution.py:410
  9.9 1.3 collective-permute-start.1
  11.2 0.0 collective-permute-done.left_ref
  11.2 3.1 %collective-permute-done.1.right_ref = f32[48,128]{1,0:T(8,128)S(1)} collective-permute-done((f32[48,128]{1,0:T(8,128)S(1)}, f32[48,128]{1,0:T(8,128)S(1)}, u32[]{:S(2)}, u32[]{:S(2)}) %collective-permute-start.1) | collective-permute-done | bytes 24608 | tf_op jit(solution)/shard_map/ppermute | solution.py:410
  14.3 0.2 shard_map.47
  14.5 6.6 %collective-permute-start.5 = (bf16[144,2048]{1,0:T(8,128)(2,1)S(1)}, bf16[144,2048]{1,0:T(8,128)(2,1)}, u32[]{:S(2)}, u32[]{:S(2)}) collective-permute-start(bf16[144,2048]{1,0:T(8,128)(2,1)S(1)} %get-tuple-element.32.x0_ref), channel_id=1, source_target_pairs={{0,256},{256,0},{1,257},{257,1},{2,258},{258,2},{3,259},{259,3},{4... | collective-permute-start | bytes 1769480 | tf_op jit(solution)/shard_map/ppermute | solution.py:427
  21.1 3.8 %collective-permute-start.2 = (f32[7,16,128]{2,1,0:T(8,128)S(1)}, f32[7,16,128]{2,1,0:T(8,128)S(1)}, u32[]{:S(2)}, u32[]{:S(2)}) collective-permute-start(f32[7,16,128]{2,1,0:T(8,128)S(1)} %get-tuple-element.29), channel_id=1, source_target_pairs={{0,1},{1,2},{2,3},{3,4},{4,5},{5,6},{6,7},{7,8},{8,9},{9,10},{10,1... | collective-permute-start | bytes 172040 | tf_op jit(solution)/shard_map/ppermute | solution.py:410
  24.9 2.0 %collective-permute-start.3 = (f32[7,16,128]{2,1,0:T(8,128)S(1)}, f32[7,16,128]{2,1,0:T(8,128)S(1)}, u32[]{:S(2)}, u32[]{:S(2)}) collective-permute-start(f32[7,16,128]{2,1,0:T(8,128)S(1)} %get-tuple-element.30), channel_id=1, source_target_pairs={{1,0},{2,1},{3,2},{4,3},{5,4},{6,5},{7,6},{8,7},{9,8},{10,9},{11,1... | collective-permute-start | bytes 172040 | tf_op jit(solution)/shard_map/ppermute | solution.py:410
  26.9 0.2 collective-permute-done.2.up_ref
  27.1 3.8 %collective-permute-done.3.down_ref = f32[7,16,128]{2,1,0:T(8,128)S(1)} collective-permute-done((f32[7,16,128]{2,1,0:T(8,128)S(1)}, f32[7,16,128]{2,1,0:T(8,128)S(1)}, u32[]{:S(2)}, u32[]{:S(2)}) %collective-permute-start.3) | collective-permute-done | bytes 57376 | tf_op jit(solution)/shard_map/ppermute | solution.py:410
  31.0 7.0 %shard_map.48 = (bf16[16,272,128]{2,1,0:T(8,128)(2,1)}, f32[1360,128]{1,0:T(8,128)S(1)}, f32[1288,128]{1,0:T(8,128)S(1)}, f32[1280,128]{1,0:T(8,128)S(1)}, f32[16,128]{1,0:T(8,128)S(1)}) custom-call(f32[16,64,128]{2,1,0:T(8,128)S(1)} %get-tuple-element.24.p_ref, f32[16,64,128]{2,1,0:T(8,128)S(1)} %get-tuple-element.25.m_ref, ...), custom_call_target="tpu_custom_call" | custom-call | tf_op jit(solution)/shard_map/pallas_call | solution.py:38
  38.0 0.8 copy-done
  38.8 4.1 %all-to-all-start = ((bf16[16,272,128]{2,1,0:T(8,128)(2,1)}), bf16[16,272,128]{2,1,0:T(8,128)(2,1)S(1)}, u32[]{:S(2)}, u32[]{:S(2)}) async-start(bf16[16,272,128]{2,1,0:T(8,128)(2,1)} %get-tuple-element.31), calls=%async_computation | async-start | bytes 2228224 | tf_op jit(solution)/shard_map/all_to_all | solution.py:431
  42.9 2.3 %collective-permute-start.4 = (bf16[144,2048]{1,0:T(8,128)(2,1)S(1)}, bf16[144,2048]{1,0:T(8,128)(2,1)}, u32[]{:S(2)}, u32[]{:S(2)}) collective-permute-start(bf16[144,2048]{1,0:T(8,128)(2,1)S(1)} %get-tuple-element.32.x0_ref), channel_id=1, source_target_pairs={{0,32},{32,0},{1,33},{33,1},{2,34},{34,2},{3,35},{35,3},{4,36},{36... | collective-permute-start | bytes 1769480 | tf_op jit(solution)/shard_map/ppermute | solution.py:428
  45.3 0.0 collective-permute-done.5.x2_hbm
  45.3 2.0 %collective-permute-start.6 = (bf16[144,2048]{1,0:T(8,128)(2,1)}, bf16[144,2048]{1,0:T(8,128)(2,1)}, u32[]{:S(2)}, u32[]{:S(2)}) collective-permute-start(bf16[144,2048]{1,0:T(8,128)(2,1)} %collective-permute-done.5.x2_hbm), channel_id=1, source_target_pairs={{0,32},{32,0},{1,33},{33,1},{2,34},{34,2},{3,35},{35,3},{4,36},{36... | collective-permute-start | bytes 1769480 | tf_op jit(solution)/shard_map/ppermute | solution.py:428
  47.3 0.0 collective-permute-done.4.x1_hbm
  47.3 12.8 %all-to-all-done.got_ref = bf16[16,272,128]{2,1,0:T(8,128)(2,1)S(1)} async-done(((bf16[16,272,128]{2,1,0:T(8,128)(2,1)}), bf16[16,272,128]{2,1,0:T(8,128)(2,1)S(1)}, u32[]{:S(2)}, u32[]{:S(2)}) %all-to-all-start) | async-done | bytes 1114144 | tf_op jit(solution)/shard_map/all_to_all | solution.py:431
  60.1 0.0 collective-permute-done.6.x3_hbm
  60.1 3.3 %shard_map.49 = f32[4,272,128]{2,1,0:T(8,128)S(1)} custom-call(s32[1]{0:T(128)} %bitcast.2.block_ref, bf16[16,272,128]{2,1,0:T(8,128)(2,1)S(1)} %all-to-all-done.got_ref, bf16[144,2048]{1,0:T(8,128)(2,1)S(1)} %get-tuple-element.32.x0_ref, bf16[144,2048]{1,0:T(8,128)(2,1)} %collective-permute-done.4.x1_hbm, bf16[144,2048]{1,0:T(8,128)(2,1)} %collective-permute-done.5.x2_hbm, ...), custom_call_target="tpu_custom_call" | custom-call | tf_op jit(solution)/shard_map/pallas_call | solution.py:38
  63.4 11.5 %all_to_all.20.back_ref = f32[4,272,128]{2,1,0:T(8,128)S(1)} all-to-all(f32[4,272,128]{2,1,0:T(8,128)S(1)} %shard_map.49), channel_id=1, replica_groups=mesh['yl'=2,'x'=4,'c'=2,'yh'=2,'z'=16] {'yl','c'}, dimensions={0} | all-to-all | bytes 1114112 | tf_op jit(solution)/shard_map/all_to_all | solution.py:433
  74.9 2.6 %shard_map.50 = bf16[16,64,128]{2,1,0:T(8,128)(2,1)S(1)} custom-call(f32[4,272,128]{2,1,0:T(8,128)S(1)} %all_to_all.20.back_ref, f32[1360,128]{1,0:T(8,128)S(1)} %get-tuple-element.33.fz_ref, f32[1288,128]{1,0:T(8,128)S(1)} %get-tuple-element.34.fy_ref, f32[1280,128]{1,0:T(8,128)} %copy-done, f32[16,128]{1,0:T(8,128)S(1)} %get-tuple-element.36.edge_ref), custom_call_target="tpu_custom_call" | custom-call | tf_op jit(solution)/shard_map/pallas_call | solution.py:38
  77.5 33.3 %all_to_all.21 = bf16[16,64,128]{2,1,0:T(8,128)(2,1)S(1)} all-to-all(bf16[16,64,128]{2,1,0:T(8,128)(2,1)S(1)} %shard_map.50), channel_id=1, replica_groups=mesh['yl'=2,'x'=4,'c'=2,'yh'=2,'z'=16] {'z'}, dimensions={0} | all-to-all | bytes 524288 | tf_op jit(solution)/shard_map/all_to_all | solution.py:436
  110.9 4.7 %collective-permute-start.7 = (bf16[1024,128]{1,0:T(8,128)(2,1)S(1)}, bf16[1024,128]{1,0:T(8,128)(2,1)S(1)}, u32[]{:S(2)}, u32[]{:S(2)}) collective-permute-start(bf16[1024,128]{1,0:T(8,128)(2,1)S(1)} %bitcast.5), channel_id=1, source_target_pairs={{0,16},{16,0},{1,17},{17,1},{2,18},{18,2},{3,19},{19,3},{4,20},{20... | collective-permute-start | bytes 786440 | tf_op jit(solution)/shard_map/ppermute | solution.py:438
  115.6 2.3 %shard_map.51 = (f32[1024,128]{1,0:T(8,128)S(1)}, bf16[1024,1024]{1,0:T(8,128)(2,1)S(1)}) custom-call(s32[1]{0:T(128)} %bitcast.side_ref, bf16[1024,2048]{1,0:T(8,128)(2,1)} %all-gather.2.cloned.1.call-done.y_hbm, bf16[1024,128]{1,0:T(8,128)(2,1)S(1)} %bitcast.6), custom_call_target="tpu_custom_call" | custom-call | tf_op jit(solution)/shard_map/pallas_call | solution.py:38
  117.9 3.7 %collective-permute-done.7.u_ref = bf16[1024,128]{1,0:T(8,128)(2,1)S(1)} collective-permute-done((bf16[1024,128]{1,0:T(8,128)(2,1)S(1)}, bf16[1024,128]{1,0:T(8,128)(2,1)S(1)}, u32[]{:S(2)}, u32[]{:S(2)}) %collective-permute-start.7) | collective-permute-done | bytes 262176 | tf_op jit(solution)/shard_map/ppermute | solution.py:438
  121.6 0.7 shard_map.52
  122.4 24.1 %all_to_all.22 = bf16[16,64,128]{2,1,0:T(8,128)(2,1)S(1)} all-to-all(bf16[16,64,128]{2,1,0:T(8,128)(2,1)S(1)} %bitcast.7), channel_id=1, replica_groups=mesh['yl'=2,'x'=4,'c'=2,'yh'=2,'z'=16] {'z'}, dimensions={0} | all-to-all | bytes 524288 | tf_op jit(solution)/shard_map/all_to_all | solution.py:441
  146.5 0.8 convert_element_type.3
  (2 shorter events, 0.0 us)
Async XLA Ops:
  6.5 104.3 %all-gather.2.cloned.1.call-start = ((), (), s32[]{:S(2)}) async-start(), calls=%async_computation.4 | async-start | bytes 4325376 | tf_op jit(solution)/shard_map/all_gather | solution.py:423
  8.2 3.1 %collective-permute-start = (f32[48,128]{1,0:T(8,128)S(1)}, f32[48,128]{1,0:T(8,128)S(1)}, u32[]{:S(2)}, u32[]{:S(2)}) collective-permute-start(f32[48,128]{1,0:T(8,128)S(1)} %get-tuple-element.27.own_r_ref), channel_id=1, source_target_pairs={{0,32},{32,64},{64,96},{96,128},{128,160},{160,192},{192,224},{224... | collective-permute-start | bytes 73736 | tf_op jit(solution)/shard_map/ppermute | solution.py:410
  9.9 4.4 %collective-permute-start.1 = (f32[48,128]{1,0:T(8,128)S(1)}, f32[48,128]{1,0:T(8,128)S(1)}, u32[]{:S(2)}, u32[]{:S(2)}) collective-permute-start(f32[48,128]{1,0:T(8,128)S(1)} %get-tuple-element.26.own_l_ref), channel_id=1, source_target_pairs={{32,0},{64,32},{96,64},{128,96},{160,128},{192,160},{224,192},{256... | collective-permute-start | bytes 73736 | tf_op jit(solution)/shard_map/ppermute | solution.py:410
  14.5 30.8 %collective-permute-start.5 = (bf16[144,2048]{1,0:T(8,128)(2,1)S(1)}, bf16[144,2048]{1,0:T(8,128)(2,1)}, u32[]{:S(2)}, u32[]{:S(2)}) collective-permute-start(bf16[144,2048]{1,0:T(8,128)(2,1)S(1)} %get-tuple-element.32.x0_ref), channel_id=1, source_target_pairs={{0,256},{256,0},{1,257},{257,1},{2,258},{258,2},{3,259},{259,3},{4... | collective-permute-start | bytes 1769480 | tf_op jit(solution)/shard_map/ppermute | solution.py:427
  21.1 6.1 %collective-permute-start.2 = (f32[7,16,128]{2,1,0:T(8,128)S(1)}, f32[7,16,128]{2,1,0:T(8,128)S(1)}, u32[]{:S(2)}, u32[]{:S(2)}) collective-permute-start(f32[7,16,128]{2,1,0:T(8,128)S(1)} %get-tuple-element.29), channel_id=1, source_target_pairs={{0,1},{1,2},{2,3},{3,4},{4,5},{5,6},{6,7},{7,8},{8,9},{9,10},{10,1... | collective-permute-start | bytes 172040 | tf_op jit(solution)/shard_map/ppermute | solution.py:410
  24.9 6.1 %collective-permute-start.3 = (f32[7,16,128]{2,1,0:T(8,128)S(1)}, f32[7,16,128]{2,1,0:T(8,128)S(1)}, u32[]{:S(2)}, u32[]{:S(2)}) collective-permute-start(f32[7,16,128]{2,1,0:T(8,128)S(1)} %get-tuple-element.30), channel_id=1, source_target_pairs={{1,0},{2,1},{3,2},{4,3},{5,4},{6,5},{7,6},{8,7},{9,8},{10,9},{11,1... | collective-permute-start | bytes 172040 | tf_op jit(solution)/shard_map/ppermute | solution.py:410
  38.0 0.9 copy-start
  38.8 21.3 %all-to-all-start = ((bf16[16,272,128]{2,1,0:T(8,128)(2,1)}), bf16[16,272,128]{2,1,0:T(8,128)(2,1)S(1)}, u32[]{:S(2)}, u32[]{:S(2)}) async-start(bf16[16,272,128]{2,1,0:T(8,128)(2,1)} %get-tuple-element.31), calls=%async_computation | async-start | bytes 2228224 | tf_op jit(solution)/shard_map/all_to_all | solution.py:431
  42.9 4.4 %collective-permute-start.4 = (bf16[144,2048]{1,0:T(8,128)(2,1)S(1)}, bf16[144,2048]{1,0:T(8,128)(2,1)}, u32[]{:S(2)}, u32[]{:S(2)}) collective-permute-start(bf16[144,2048]{1,0:T(8,128)(2,1)S(1)} %get-tuple-element.32.x0_ref), channel_id=1, source_target_pairs={{0,32},{32,0},{1,33},{33,1},{2,34},{34,2},{3,35},{35,3},{4,36},{36... | collective-permute-start | bytes 1769480 | tf_op jit(solution)/shard_map/ppermute | solution.py:428
  45.3 14.8 %collective-permute-start.6 = (bf16[144,2048]{1,0:T(8,128)(2,1)}, bf16[144,2048]{1,0:T(8,128)(2,1)}, u32[]{:S(2)}, u32[]{:S(2)}) collective-permute-start(bf16[144,2048]{1,0:T(8,128)(2,1)} %collective-permute-done.5.x2_hbm), channel_id=1, source_target_pairs={{0,32},{32,0},{1,33},{33,1},{2,34},{34,2},{3,35},{35,3},{4,36},{36... | collective-permute-start | bytes 1769480 | tf_op jit(solution)/shard_map/ppermute | solution.py:428
  110.9 10.8 %collective-permute-start.7 = (bf16[1024,128]{1,0:T(8,128)(2,1)S(1)}, bf16[1024,128]{1,0:T(8,128)(2,1)S(1)}, u32[]{:S(2)}, u32[]{:S(2)}) collective-permute-start(bf16[1024,128]{1,0:T(8,128)(2,1)S(1)} %bitcast.5), channel_id=1, source_target_pairs={{0,16},{16,0},{1,17},{17,1},{2,18},{18,2},{3,19},{19,3},{4,20},{20... | collective-permute-start | bytes 786440 | tf_op jit(solution)/shard_map/ppermute | solution.py:438
Sparse Core Ops, SparseCore 0:
  9.4 77.7 all-gather.1

commit v4 on v3

--- a/solution.py
+++ b/solution.py
@@ -30,6 +30,10 @@
 
 
 FAR = pl.BlockSpec(memory_space=pltpu.HBM)
+
+
+def away_kept(shape, dtype):
+    return pltpu.HBM(shape, dtype)
 
 
 def call(kernel, out_shape, args, scalar=None, scratch=(), far=(), far_out=()):
@@ -132,8 +136,8 @@
 
 def explicit_kernel(
     p_ref, m_ref, own_l_ref, own_r_ref, left_ref, right_ref, up_ref, down_ref,
-    send_ref, fz_ref, fy_ref, fx_hbm, edge_ref,
-    v_ref, c_ref, f_ref, fx_ref, side_ref, rim_ref, sem,
+    send_ref, fz_ref, fy_ref, fx_ref, edge_ref,
+    v_ref, c_ref, f_ref, side_ref, rim_ref, turned_ref, gy_ref,
 ):
     planes, cy, cx = p_ref.shape
     pairs = planes // 2
@@ -169,24 +173,22 @@
         lap = lap + face_mob(m, mr) * (vr - v) + face_mob(m, ml) * (vl - v)
         return v + step_size * lap
 
-    columns = []
+    turned_ref[...] = jnp.zeros(turned_ref.shape, F32)
     for side, (v, m) in enumerate(zip(strips(0), strips(1), strict=True)):
         f = face_mob(m[1], m[2])
         a = strip_first(v[1], m[1], v[0], m[0], v[2], m[2])
         b = strip_first(v[2], m[2], v[1], m[1], v[3], m[3])
-        columns += [f * (v[2] - v[1]), f * (b - a)]
+        turned_ref[pl.ds(2 - side, planes, stride=2), :] = f * (v[2] - v[1])
+        turned_ref[pl.ds(66 - side, planes, stride=2), :] = f * (b - a)
         side_ref[...] = f
         even = turn(side_ref[pl.ds(0, pairs, stride=2), :], -OFF, 1)
         odd = turn(side_ref[pl.ds(1, pairs, stride=2), :], cy - OFF, 1)
         edge_ref[side * pairs : (side + 1) * pairs, :] = jnp.where(lane[:pairs] < cy, even, odd)
-    stacked = jnp.concatenate(columns + [jnp.zeros((cx - 4 * planes, cx), F32)], axis=0)
-    across = stacked.T[:tall]
-
+    across = turned_ref[...].T
     part = tall // 2
 
-    def column(k, z, h):
-        at = k * planes + z
-        return jnp.broadcast_to(across[h * part : (h + 1) * part, at : at + 1], (part, cx))
+    def ends(k, z, h):
+        return turn(across[h * part : (h + 1) * part], -(64 * k + 2 * z + 2), 1)
 
     blank = jnp.zeros((OFF, cx), F32)
     for ref in (v_ref, c_ref, f_ref):
@@ -204,19 +206,21 @@
 
     wide = places((part, cx), 1)
 
-    def step(ref, z, h, fz, fy, fx, gz_before, gl, gr):
+    def step(ref, z, h, fz, fy, fx, gz_before, end):
         at = (z + 1) * tall + h * part
         v = ref[at : at + part, :]
         gz = fz * (ref[at + tall : at + tall + part, :] - v)
         gy = fy * (ref[at + 1 : at + 1 + part, :] - v)
-        flat = OFF + z * tall + h * part - 1
-        gu = fy_ref[flat : flat + part, :] * (v - ref[at - 1 : at - 1 + part, :])
-        gx = jnp.where(wide == 0, gl, fx * (v - turn(v, 1, 1)))
-        lap = gz - gz_before + gy - gu + jnp.where(wide == cx - 1, gr, turn(gx, -1, 1)) - gx
+        flat = OFF + z * tall + h * part
+        gy_ref[flat : flat + part, :] = gy
+        gu = gy_ref[flat - 1 : flat - 1 + part, :]
+        gx = jnp.where(wide == 0, end, fx * (v - turn(v, 1, 1)))
+        lap = gz - gz_before + gy - gu + jnp.where(wide == cx - 1, end, turn(gx, -1, 1)) - gx
         return v + step_size * lap, gz
 
     fz_ref[:tall, :] = jnp.zeros((tall, cx), F32)
     fy_ref[:OFF, :] = jnp.zeros((OFF, cx), F32)
+    gy_ref[:OFF, :] = jnp.zeros((OFF, cx), F32)
     for h in range(2):
         before = jnp.zeros((part, cx), F32)
         for z in range(planes):
@@ -229,10 +233,8 @@
             fz_ref[at : at + part, :] = fz
             fy_ref[OFF + flat : OFF + flat + part, :] = fy
             fx_ref[flat : flat + part, :] = fx
-            out, before = step(v_ref, z, h, fz, fy, fx, before, column(0, z, h), column(2, z, h))
+            out, before = step(v_ref, z, h, fz, fy, fx, before, ends(0, z, h))
             f_ref[at : at + part, :] = out
-    leave = pltpu.make_async_copy(fx_ref, fx_hbm, sem)
-    leave.start()
 
     rim_ref[...] = jnp.zeros(rim_ref.shape, F32)
     quarter = planes // 4
@@ -243,7 +245,7 @@
             flat = z * tall + h * part
             out, before = step(
                 f_ref, z, h, fz_ref[at : at + part, :], fy_ref[OFF + flat : OFF + flat + part, :],
-                fx_ref[flat : flat + part, :], before, column(1, z, h), column(3, z, h),
+                fx_ref[flat : flat + part, :], before, ends(1, z, h),
             )
             v_ref[at : at + part, :] = out
     for z in range(planes):
@@ -258,21 +260,19 @@
         rims = rim_ref[q].astype(BF16)
         for x in range(4):
             send_ref[(q // 2) * 8 + x * 2 + q % 2, quarter * cy :, :] = rims
-    leave.wait()
-
-
-def solve_x_kernel(block_ref, got_ref, x0_ref, x1_hbm, x2_hbm, x3_hbm, out_ref, x1_ref, x2_ref, x3_ref, sems):
+
+
+def solve_x_kernel(block_ref, got_ref, x0_hbm, x1_hbm, x2_hbm, x3_hbm, out_ref, x0_ref, x1_ref, x2_ref, x3_ref, sems):
     own = block_ref[0]
     parts, lines, cx = got_ref.shape
     main = lines - 16
-    moves = ((x1_hbm, x1_ref), (x2_hbm, x2_ref), (x3_hbm, x3_ref))
+    moves = ((x0_hbm, x0_ref), (x1_hbm, x1_ref), (x2_hbm, x2_ref), (x3_hbm, x3_ref))
     copies = [pltpu.make_async_copy(src, dst, sems.at[i]) for i, (src, dst) in enumerate(moves)]
     for copy in copies:
         copy.start()
     a = jnp.concatenate([got_ref[s] for s in range(parts)], axis=1)
     for other, x_ref in enumerate((x0_ref, x1_ref, x2_ref, x3_ref)):
-        if other:
-            copies[other - 1].wait()
+        copies[other].wait()
         block = own ^ other
         m = lax.dot_general(a, x_ref[:cx], NT, preferred_element_type=F32)
         out_ref[block, : main + 8] = m[: main + 8]
@@ -281,14 +281,11 @@
         out_ref[block, main + 12 :] = e[:4, cx:]
 
 
-def implicit_kernel(back_ref, fz_ref, fy_ref, fx_hbm, edge_ref, out_ref, c_ref, e_ref, fx_ref, sem):
+def implicit_kernel(back_ref, fz_ref, fy_ref, fx_ref, edge_ref, out_ref, c_ref, e_ref):
     planes, cy, cx = out_ref.shape
     tall = cy + 2 * OFF
     quarter, pairs = planes // 4, planes // 2
     main = quarter * cy
-
-    come = pltpu.make_async_copy(fx_hbm, fx_ref, sem)
-    come.start()
 
     def chemical(s):
         return s * s * s - s
@@ -309,7 +306,6 @@
     across = jnp.concatenate([left, right, jnp.zeros((cx - planes, cx), F32)], axis=0).T
     lane = places((cy, cx), 1)
     before = jnp.zeros((cy, cx), F32)
-    come.wait()
     for z in range(planes):
         base = (z + 1) * tall + OFF
         flat = z * tall + OFF
@@ -350,7 +346,7 @@
     shape = (2 * p.shape[0] + 16, cx)
     cy, order = y_inverse.shape
     out = (kept(shape, F32),) * 2 + (kept(p.shape, F32),) * 2 + (kept(x_inverse.shape, BF16),)
-    out += (jax.ShapeDtypeStruct((cy // 2, order), BF16),)
+    out += (away_kept((cy // 2, order), BF16),)
     scratch = (pltpu.VMEM((cy // 2, order), BF16), pltpu.SemaphoreType.DMA((4,)))
     return call(pack_x_kernel, out, (p, m, x_inverse, y_inverse), core, scratch, range(4), (5,))
 
@@ -370,27 +366,27 @@
         kept((16, lines, cx), BF16),
         kept(((planes + 1) * tall, cx), F32),
         kept((planes * tall + OFF, cx), F32),
-        jax.ShapeDtypeStruct((planes * tall, cx), F32),
+        kept((planes * tall, cx), F32),
         kept((planes, cx), F32),
     )
-    scratch = (field, field, field, pltpu.VMEM((planes * tall, cx), F32), pltpu.VMEM((planes, cx), F32))
-    scratch += (pltpu.VMEM((4, 16, cx), F32), pltpu.SemaphoreType.DMA(()))
-    return call(explicit_kernel, out, args, scratch=scratch, far_out=(3,))
+    scratch = (field, field, field, pltpu.VMEM((planes, cx), F32))
+    scratch += (pltpu.VMEM((4, 16, cx), F32), pltpu.VMEM((cx, cx), F32))
+    scratch += (pltpu.VMEM((planes * tall + OFF, cx), F32),)
+    return call(explicit_kernel, out, args, scratch=scratch)
 
 
 def solve_x(block, got, x_blocks):
     _, lines, cx = got.shape
     blocks = pltpu.VMEM(x_blocks[0].shape, BF16)
-    scratch = (blocks, blocks, blocks, pltpu.SemaphoreType.DMA((3,)))
-    return call(solve_x_kernel, kept((4, lines, cx), F32), (got, *x_blocks), block, scratch, (2, 3, 4))
+    scratch = (blocks,) * 4 + (pltpu.SemaphoreType.DMA((4,)),)
+    return call(solve_x_kernel, kept((4, lines, cx), F32), (got, *x_blocks), block, scratch, (1, 2, 3, 4))
 
 
 def implicit(back, faces, planes, cy):
     cx = back.shape[2]
     tall = cy + 2 * OFF
     scratch = (pltpu.VMEM(((planes + 2) * tall, cx), F32), pltpu.VMEM((32, cx), F32))
-    scratch += (pltpu.VMEM((planes * tall, cx), F32), pltpu.SemaphoreType.DMA(()))
-    return call(implicit_kernel, kept((planes, cy, cx), BF16), (back, *faces), None, scratch, (3,))
+    return call(implicit_kernel, kept((planes, cy, cx), BF16), (back, *faces), scratch=scratch)
 
 
 def solve_y_near(side, y, u):

time: 155 us -> 154 us (level)
  the two profiles are of different devices: /device:TPU:32 before, /device:TPU:16 now
where the time goes in v4:
time: 154 us; the launch traced here: 153 us
  blocking collectives  64.1 us (42%)
  starting transfers between devices  34.1 us (22%)
  waiting for transfers between devices  23.2 us (15%)
  Pallas kernels  17.5 us (11%)
  between operations  13.5 us (9%)
    all_to_all x1, blocking collectives, local(): mine = lax.all_to_all(updated, 'z', 0, 0, tiled=True).reshape(half, cx)  27.2 us
    all_to_all x1, blocking collectives, local(): out = lax.all_to_all(out, 'z', 0, 0, tiled=True)  25.4 us
    pallas_call x7, Pallas kernels, call(): pl.pallas_call(kernel, out_shape=out_shape, in_specs=[pl.BlockSpec(memory...  17.5 us
    all_to_all x1, waiting for transfers between devices, local(): got = lax.all_to_all(send, GX, 0, 0, tiled=True)  12.7 us
    all_to_all x1, blocking collectives, local(): back = lax.all_to_all(back, ('yl', 'c'), 0, 0, tiled=True)  11.5 us
    ppermute x2, starting transfers between devices, both_ways(): lax.ppermute(to_before, axis, [(j, i) for i, j in up])  10.9 us
    ppermute x1, starting transfers between devices, local(): rows_yl = lax.ppermute(rows, 'yl', swap)  6.25 us
    ppermute x2, starting transfers between devices, both_ways(): lax.ppermute(to_after, axis, up)  5.57 us
  transfers between devices with their start and end apart: 10, of which 5 were waited for; matrix products, arithmetic and copies ran while one was open for 0% of the time, Pallas kernels for 10%

profile of v4, /device:TPU:16, one launch (start us, length us, event | category | flops | bytes accessed | tf_op | source)
XLA Modules:
  0.0 153.3 jit_solution(15035373252837767370)
XLA Ops:
  6.5 0.0 all-gather.2.cloned.1.call-start
  6.5 1.6 %shard_map.46 = (f32[48,128]{1,0:T(8,128)S(1)}, f32[48,128]{1,0:T(8,128)S(1)}, f32[16,64,128]{2,1,0:T(8,128)S(1)}, f32[16,64,128]{2,1,0:T(8,128)S(1)}, bf16[128,...) custom-call(s32[1]{0:T(128)} %bitcast.1.core_ref, f32[16,64,128]{2,1,0:T(8,128)} %p_hbm.1, f32[16,64,128]{2,1,0:T(8,128)} %m_hbm.1, ...), custom_call_target="tpu_custom_call" | custom-call | tf_op jit(solution)/shard_map/pallas_call | solution.py:42
  8.1 0.0 all-gather.2.cloned.1.call-update
  8.2 1.7 %collective-permute-start = (f32[48,128]{1,0:T(8,128)S(1)}, f32[48,128]{1,0:T(8,128)S(1)}, u32[]{:S(2)}, u32[]{:S(2)}) collective-permute-start(f32[48,128]{1,0:T(8,128)S(1)} %get-tuple-element.27.own_r_ref), channel_id=1, source_target_pairs={{0,32},{32,64},{64,96},{96,128},{128,160},{160,192},{192,224},{224... | collective-permute-start | bytes 73736 | tf_op jit(solution)/shard_map/ppermute | solution.py:406
  9.9 1.3 collective-permute-start.1
  11.2 0.0 collective-permute-done.left_ref
  11.2 3.1 %collective-permute-done.1.right_ref = f32[48,128]{1,0:T(8,128)S(1)} collective-permute-done((f32[48,128]{1,0:T(8,128)S(1)}, f32[48,128]{1,0:T(8,128)S(1)}, u32[]{:S(2)}, u32[]{:S(2)}) %collective-permute-start.1) | collective-permute-done | bytes 24608 | tf_op jit(solution)/shard_map/ppermute | solution.py:406
  14.3 1.0 shard_map.47
  15.3 6.3 %collective-permute-start.5 = (bf16[144,2048]{1,0:T(8,128)(2,1)}, bf16[144,2048]{1,0:T(8,128)(2,1)}, u32[]{:S(2)}, u32[]{:S(2)}) collective-permute-start(bf16[144,2048]{1,0:T(8,128)(2,1)} %get-tuple-element.32.x0_hbm), channel_id=1, source_target_pairs={{0,256},{256,0},{1,257},{257,1},{2,258},{258,2},{3,259},{259,3},{4... | collective-permute-start | bytes 1769480 | tf_op jit(solution)/shard_map/ppermute | solution.py:423
  21.5 3.8 %collective-permute-start.2 = (f32[7,16,128]{2,1,0:T(8,128)S(1)}, f32[7,16,128]{2,1,0:T(8,128)S(1)}, u32[]{:S(2)}, u32[]{:S(2)}) collective-permute-start(f32[7,16,128]{2,1,0:T(8,128)S(1)} %get-tuple-element.29), channel_id=1, source_target_pairs={{0,1},{1,2},{2,3},{3,4},{4,5},{5,6},{6,7},{7,8},{8,9},{9,10},{10,1... | collective-permute-start | bytes 172040 | tf_op jit(solution)/shard_map/ppermute | solution.py:406
  25.4 9.6 %collective-permute-start.3 = (f32[7,16,128]{2,1,0:T(8,128)S(1)}, f32[7,16,128]{2,1,0:T(8,128)S(1)}, u32[]{:S(2)}, u32[]{:S(2)}) collective-permute-start(f32[7,16,128]{2,1,0:T(8,128)S(1)} %get-tuple-element.30), channel_id=1, source_target_pairs={{1,0},{2,1},{3,2},{4,3},{5,4},{6,5},{7,6},{8,7},{9,8},{10,9},{11,1... | collective-permute-start | bytes 172040 | tf_op jit(solution)/shard_map/ppermute | solution.py:406
  34.9 1.2 collective-permute-done.2.up_ref
  36.1 1.2 collective-permute-done.3.down_ref
  37.4 6.3 %shard_map.48 = (bf16[16,272,128]{2,1,0:T(8,128)(2,1)}, f32[1360,128]{1,0:T(8,128)S(1)}, f32[1288,128]{1,0:T(8,128)S(1)}, f32[1280,128]{1,0:T(8,128)S(1)}, f32[16,128]{1,0:T(8,128)S(1)}) custom-call(f32[16,64,128]{2,1,0:T(8,128)S(1)} %get-tuple-element.24.p_ref, f32[16,64,128]{2,1,0:T(8,128)S(1)} %get-tuple-element.25.m_ref, ...), custom_call_target="tpu_custom_call" | custom-call | tf_op jit(solution)/shard_map/pallas_call | solution.py:42
  43.7 4.6 %all-to-all-start = ((bf16[16,272,128]{2,1,0:T(8,128)(2,1)}), bf16[16,272,128]{2,1,0:T(8,128)(2,1)S(1)}, u32[]{:S(2)}, u32[]{:S(2)}) async-start(bf16[16,272,128]{2,1,0:T(8,128)(2,1)} %get-tuple-element.31), calls=%async_computation | async-start | bytes 2228224 | tf_op jit(solution)/shard_map/all_to_all | solution.py:427
  48.3 2.3 %collective-permute-start.4 = (bf16[144,2048]{1,0:T(8,128)(2,1)}, bf16[144,2048]{1,0:T(8,128)(2,1)}, u32[]{:S(2)}, u32[]{:S(2)}) collective-permute-start(bf16[144,2048]{1,0:T(8,128)(2,1)} %get-tuple-element.32.x0_hbm), channel_id=1, source_target_pairs={{0,32},{32,0},{1,33},{33,1},{2,34},{34,2},{3,35},{35,3},{4,36},{36... | collective-permute-start | bytes 1769480 | tf_op jit(solution)/shard_map/ppermute | solution.py:424
  50.6 0.0 collective-permute-done.5.x2_hbm
  50.6 2.0 %collective-permute-start.6 = (bf16[144,2048]{1,0:T(8,128)(2,1)}, bf16[144,2048]{1,0:T(8,128)(2,1)}, u32[]{:S(2)}, u32[]{:S(2)}) collective-permute-start(bf16[144,2048]{1,0:T(8,128)(2,1)} %collective-permute-done.5.x2_hbm), channel_id=1, source_target_pairs={{0,32},{32,0},{1,33},{33,1},{2,34},{34,2},{3,35},{35,3},{4,36},{36... | collective-permute-start | bytes 1769480 | tf_op jit(solution)/shard_map/ppermute | solution.py:424
  52.7 0.0 collective-permute-done.4.x1_hbm
  52.7 12.7 %all-to-all-done.got_ref = bf16[16,272,128]{2,1,0:T(8,128)(2,1)S(1)} async-done(((bf16[16,272,128]{2,1,0:T(8,128)(2,1)}), bf16[16,272,128]{2,1,0:T(8,128)(2,1)S(1)}, u32[]{:S(2)}, u32[]{:S(2)}) %all-to-all-start) | async-done | bytes 1114144 | tf_op jit(solution)/shard_map/all_to_all | solution.py:427
  65.5 0.0 collective-permute-done.6.x3_hbm
  65.5 4.0 %shard_map.49 = f32[4,272,128]{2,1,0:T(8,128)S(1)} custom-call(s32[1]{0:T(128)} %bitcast.2.block_ref, bf16[16,272,128]{2,1,0:T(8,128)(2,1)S(1)} %all-to-all-done.got_ref, bf16[144,2048]{1,0:T(8,128)(2,1)} %get-tuple-element.32.x0_hbm, bf16[144,2048]{1,0:T(8,128)(2,1)} %collective-permute-done.4.x1_hbm, bf16[144,2048]{1,0:T(8,128)(2,1)} %collective-permute-done.5.x2_hbm, ...), custom_call_target="tpu_custom_call" | custom-call | tf_op jit(solution)/shard_map/pallas_call | solution.py:42
  69.5 11.5 %all_to_all.20.back_ref = f32[4,272,128]{2,1,0:T(8,128)S(1)} all-to-all(f32[4,272,128]{2,1,0:T(8,128)S(1)} %shard_map.49), channel_id=1, replica_groups=mesh['yl'=2,'x'=4,'c'=2,'yh'=2,'z'=16] {'yl','c'}, dimensions={0} | all-to-all | bytes 1114112 | tf_op jit(solution)/shard_map/all_to_all | solution.py:429
  81.0 1.6 %shard_map.50 = bf16[16,64,128]{2,1,0:T(8,128)(2,1)S(1)} custom-call(f32[4,272,128]{2,1,0:T(8,128)S(1)} %all_to_all.20.back_ref, f32[1360,128]{1,0:T(8,128)S(1)} %get-tuple-element.33.fz_ref, f32[1288,128]{1,0:T(8,128)S(1)} %get-tuple-element.34.fy_ref, f32[1280,128]{1,0:T(8,128)S(1)} %get-tuple-element.35.fx_ref, f32[16,128]{1,0:T(8,128)S(1)} %get-tuple-element.36.edge_ref), custom_call_target="tpu_custom_call" | custom-call | tf_op jit(solution)/shard_map/pallas_call | solution.py:42
  82.6 27.2 %all_to_all.21 = bf16[16,64,128]{2,1,0:T(8,128)(2,1)S(1)} all-to-all(bf16[16,64,128]{2,1,0:T(8,128)(2,1)S(1)} %shard_map.50), channel_id=1, replica_groups=mesh['yl'=2,'x'=4,'c'=2,'yh'=2,'z'=16] {'z'}, dimensions={0} | all-to-all | bytes 524288 | tf_op jit(solution)/shard_map/all_to_all | solution.py:432
  109.8 0.0 all-gather.2.cloned.1.call-done.y_hbm
  109.8 2.5 %collective-permute-start.7 = (bf16[1024,128]{1,0:T(8,128)(2,1)S(1)}, bf16[1024,128]{1,0:T(8,128)(2,1)S(1)}, u32[]{:S(2)}, u32[]{:S(2)}) collective-permute-start(bf16[1024,128]{1,0:T(8,128)(2,1)S(1)} %bitcast.5), channel_id=1, source_target_pairs={{0,16},{16,0},{1,17},{17,1},{2,18},{18,2},{3,19},{19,3},{4,20},{20... | collective-permute-start | bytes 786440 | tf_op jit(solution)/shard_map/ppermute | solution.py:434
  112.3 2.3 %shard_map.51 = (f32[1024,128]{1,0:T(8,128)S(1)}, bf16[1024,1024]{1,0:T(8,128)(2,1)S(1)}) custom-call(s32[1]{0:T(128)} %bitcast.side_ref, bf16[1024,2048]{1,0:T(8,128)(2,1)} %all-gather.2.cloned.1.call-done.y_hbm, bf16[1024,128]{1,0:T(8,128)(2,1)S(1)} %bitcast.6), custom_call_target="tpu_custom_call" | custom-call | tf_op jit(solution)/shard_map/pallas_call | solution.py:42
  114.6 4.9 %collective-permute-done.7.u_ref = bf16[1024,128]{1,0:T(8,128)(2,1)S(1)} collective-permute-done((bf16[1024,128]{1,0:T(8,128)(2,1)S(1)}, bf16[1024,128]{1,0:T(8,128)(2,1)S(1)}, u32[]{:S(2)}, u32[]{:S(2)}) %collective-permute-start.7) | collective-permute-done | bytes 262176 | tf_op jit(solution)/shard_map/ppermute | solution.py:434
  119.5 0.7 shard_map.52
  120.3 25.4 %all_to_all.22 = bf16[16,64,128]{2,1,0:T(8,128)(2,1)S(1)} all-to-all(bf16[16,64,128]{2,1,0:T(8,128)(2,1)S(1)} %bitcast.7), channel_id=1, replica_groups=mesh['yl'=2,'x'=4,'c'=2,'yh'=2,'z'=16] {'z'}, dimensions={0} | all-to-all | bytes 524288 | tf_op jit(solution)/shard_map/all_to_all | solution.py:437
  145.7 0.8 convert_element_type.3
Async XLA Ops:
  6.5 103.2 %all-gather.2.cloned.1.call-start = ((), (), s32[]{:S(2)}) async-start(), calls=%async_computation.4 | async-start | bytes 4325376 | tf_op jit(solution)/shard_map/all_gather | solution.py:419
  8.2 3.1 %collective-permute-start = (f32[48,128]{1,0:T(8,128)S(1)}, f32[48,128]{1,0:T(8,128)S(1)}, u32[]{:S(2)}, u32[]{:S(2)}) collective-permute-start(f32[48,128]{1,0:T(8,128)S(1)} %get-tuple-element.27.own_r_ref), channel_id=1, source_target_pairs={{0,32},{32,64},{64,96},{96,128},{128,160},{160,192},{192,224},{224... | collective-permute-start | bytes 73736 | tf_op jit(solution)/shard_map/ppermute | solution.py:406
  9.9 4.4 %collective-permute-start.1 = (f32[48,128]{1,0:T(8,128)S(1)}, f32[48,128]{1,0:T(8,128)S(1)}, u32[]{:S(2)}, u32[]{:S(2)}) collective-permute-start(f32[48,128]{1,0:T(8,128)S(1)} %get-tuple-element.26.own_l_ref), channel_id=1, source_target_pairs={{32,0},{64,32},{96,64},{128,96},{160,128},{192,160},{224,192},{256... | collective-permute-start | bytes 73736 | tf_op jit(solution)/shard_map/ppermute | solution.py:406
  15.3 35.3 %collective-permute-start.5 = (bf16[144,2048]{1,0:T(8,128)(2,1)}, bf16[144,2048]{1,0:T(8,128)(2,1)}, u32[]{:S(2)}, u32[]{:S(2)}) collective-permute-start(bf16[144,2048]{1,0:T(8,128)(2,1)} %get-tuple-element.32.x0_hbm), channel_id=1, source_target_pairs={{0,256},{256,0},{1,257},{257,1},{2,258},{258,2},{3,259},{259,3},{4... | collective-permute-start | bytes 1769480 | tf_op jit(solution)/shard_map/ppermute | solution.py:423
  21.5 14.6 %collective-permute-start.2 = (f32[7,16,128]{2,1,0:T(8,128)S(1)}, f32[7,16,128]{2,1,0:T(8,128)S(1)}, u32[]{:S(2)}, u32[]{:S(2)}) collective-permute-start(f32[7,16,128]{2,1,0:T(8,128)S(1)} %get-tuple-element.29), channel_id=1, source_target_pairs={{0,1},{1,2},{2,3},{3,4},{4,5},{5,6},{6,7},{7,8},{8,9},{9,10},{10,1... | collective-permute-start | bytes 172040 | tf_op jit(solution)/shard_map/ppermute | solution.py:406
  25.4 12.0 %collective-permute-start.3 = (f32[7,16,128]{2,1,0:T(8,128)S(1)}, f32[7,16,128]{2,1,0:T(8,128)S(1)}, u32[]{:S(2)}, u32[]{:S(2)}) collective-permute-start(f32[7,16,128]{2,1,0:T(8,128)S(1)} %get-tuple-element.30), channel_id=1, source_target_pairs={{1,0},{2,1},{3,2},{4,3},{5,4},{6,5},{7,6},{8,7},{9,8},{10,9},{11,1... | collective-permute-start | bytes 172040 | tf_op jit(solution)/shard_map/ppermute | solution.py:406
  43.7 21.8 %all-to-all-start = ((bf16[16,272,128]{2,1,0:T(8,128)(2,1)}), bf16[16,272,128]{2,1,0:T(8,128)(2,1)S(1)}, u32[]{:S(2)}, u32[]{:S(2)}) async-start(bf16[16,272,128]{2,1,0:T(8,128)(2,1)} %get-tuple-element.31), calls=%async_computation | async-start | bytes 2228224 | tf_op jit(solution)/shard_map/all_to_all | solution.py:427
  48.3 4.4 %collective-permute-start.4 = (bf16[144,2048]{1,0:T(8,128)(2,1)}, bf16[144,2048]{1,0:T(8,128)(2,1)}, u32[]{:S(2)}, u32[]{:S(2)}) collective-permute-start(bf16[144,2048]{1,0:T(8,128)(2,1)} %get-tuple-element.32.x0_hbm), channel_id=1, source_target_pairs={{0,32},{32,0},{1,33},{33,1},{2,34},{34,2},{3,35},{35,3},{4,36},{36... | collective-permute-start | bytes 1769480 | tf_op jit(solution)/shard_map/ppermute | solution.py:424
  50.6 14.8 %collective-permute-start.6 = (bf16[144,2048]{1,0:T(8,128)(2,1)}, bf16[144,2048]{1,0:T(8,128)(2,1)}, u32[]{:S(2)}, u32[]{:S(2)}) collective-permute-start(bf16[144,2048]{1,0:T(8,128)(2,1)} %collective-permute-done.5.x2_hbm), channel_id=1, source_target_pairs={{0,32},{32,0},{1,33},{33,1},{2,34},{34,2},{3,35},{35,3},{4,36},{36... | collective-permute-start | bytes 1769480 | tf_op jit(solution)/shard_map/ppermute | solution.py:424
  109.8 9.8 %collective-permute-start.7 = (bf16[1024,128]{1,0:T(8,128)(2,1)S(1)}, bf16[1024,128]{1,0:T(8,128)(2,1)S(1)}, u32[]{:S(2)}, u32[]{:S(2)}) collective-permute-start(bf16[1024,128]{1,0:T(8,128)(2,1)S(1)} %bitcast.5), channel_id=1, source_target_pairs={{0,16},{16,0},{1,17},{17,1},{2,18},{18,2},{3,19},{19,3},{4,20},{20... | collective-permute-start | bytes 786440 | tf_op jit(solution)/shard_map/ppermute | solution.py:434
Sparse Core Ops, SparseCore 0:
  9.4 78.1 all-gather.1

commit v5 on v4

--- a/solution.py
+++ b/solution.py
@@ -36,7 +36,7 @@
     return pltpu.HBM(shape, dtype)
 
 
-def call(kernel, out_shape, args, scalar=None, scratch=(), far=(), far_out=()):
+def call(kernel, out_shape, args, scalar=None, scratch=(), far=(), far_out=(), aliases=None):
     scalars = [] if scalar is None else [scalar]
     many = isinstance(out_shape, tuple)
     return pl.pallas_call(
@@ -45,6 +45,7 @@
         in_specs=[pl.BlockSpec(memory_space=pltpu.SMEM)] * len(scalars) + [FAR if i in far else VMEM for i in range(len(args))],
         out_specs=tuple(FAR if i in far_out else VMEM for i in range(len(out_shape))) if many else VMEM,
         scratch_shapes=list(scratch),
+        input_output_aliases=aliases or {},
         compiler_params=pltpu.CompilerParams(vmem_limit_bytes=16 << 20),
     )(*scalars, *[away(v) if i in far else near(v) for i, v in enumerate(args)])
 
@@ -61,7 +62,7 @@
     return lax.broadcasted_iota(jnp.int32, shape, axis)
 
 
-def pack_x_kernel(core_ref, p_hbm, m_hbm, x_hbm, y_hbm, left_ref, right_ref, p_ref, m_ref, x_ref, part_hbm, part_ref, sems):
+def pack_x_kernel(core_ref, p_hbm, m_hbm, x_hbm, y_hbm, left_ref, right_ref, p_ref, m_ref, rows_hbm, part_hbm, x_ref, part_ref, sems):
     planes, _, cx = p_ref.shape
     pairs = planes // 2
     rows = part_hbm.shape[0]
@@ -87,12 +88,15 @@
                 right_ref[k : k + 1, :] = t[cx - 2 + j : cx - 1 + j]
     base = 4 * pairs
     copies[3].wait()
+    own = pltpu.make_async_copy(x_ref, rows_hbm.at[pl.ds(0, cx)], sems.at[3])
+    own.start()
     first = x_ref[0:16, :][0:1].astype(F32)
     last = x_ref[cx - 16 : cx, :][15:16].astype(F32)
     for s in range(16):
         left_ref[base + s : base + s + 1, :] = first[:, s * cx : (s + 1) * cx]
         right_ref[base + s : base + s + 1, :] = last[:, s * cx : (s + 1) * cx]
     out.wait()
+    own.wait()
 
 
 def strip(x, cy):
@@ -106,8 +110,18 @@
     return [strip(ref[k * pairs : (k + 1) * pairs, :], cy) for ref, k in refs]
 
 
-def pack_y_kernel(p_ref, m_ref, x_ref, left_ref, right_ref, up_ref, down_ref, rows_ref, row_ref):
+def pack_y_kernel(
+    p_ref, m_ref, own_l_ref, own_r_ref, left_ref, right_ref, _, up_ref, down_ref, rows_hbm, row_ref, cast_ref, sem
+):
     planes, cy, cx = p_ref.shape
+    base = left_ref.shape[0] - 16
+    row_ref[...] = jnp.zeros(row_ref.shape, F32)
+    for j, ref in enumerate((left_ref, own_l_ref, own_r_ref, right_ref)):
+        for s in range(16):
+            row_ref[j : j + 1, s * cx : (s + 1) * cx] = ref[base + s : base + s + 1, :]
+    cast_ref[...] = row_ref[...].astype(BF16)
+    copy = pltpu.make_async_copy(cast_ref, rows_hbm.at[pl.ds(cx, 16)], sem)
+    copy.start()
     for a, ref in enumerate((p_ref, m_ref)):
         for r in range(3):
             up_ref[3 * a + r] = ref[:, cy - 3 + r, :]
@@ -123,21 +137,13 @@
             down = jnp.where(here, turn(s, at - OFF, 1), down)
     up_ref[6] = up
     down_ref[6] = down
-    rows_ref[:cx] = x_ref[...]
-    row_ref[...] = jnp.zeros(row_ref.shape, F32)
-    base = left_ref.shape[0] - 16
-    for s in range(16):
-        row_ref[0:1, s * cx : (s + 1) * cx] = left_ref[base + s : base + s + 1, :]
-        row_ref[3:4, s * cx : (s + 1) * cx] = right_ref[base + s : base + s + 1, :]
-    row_ref[1:2, :] = x_ref[0:16, :][0:1].astype(F32)
-    row_ref[2:3, :] = x_ref[cx - 16 : cx, :][15:16].astype(F32)
-    rows_ref[cx:] = row_ref[...].astype(BF16)
+    copy.wait()
 
 
 def explicit_kernel(
     p_ref, m_ref, own_l_ref, own_r_ref, left_ref, right_ref, up_ref, down_ref,
-    send_ref, fz_ref, fy_ref, fx_ref, edge_ref,
-    v_ref, c_ref, f_ref, side_ref, rim_ref, turned_ref, gy_ref,
+    send_hbm, fz_ref, fy_ref, fx_ref, edge_ref,
+    v_ref, c_ref, f_ref, side_ref, rim_ref, turned_ref, gy_ref, quarter_ref, sems,
 ):
     planes, cy, cx = p_ref.shape
     pairs = planes // 2
@@ -238,28 +244,31 @@
 
     rim_ref[...] = jnp.zeros(rim_ref.shape, F32)
     quarter = planes // 4
-    for h in range(2):
-        before = jnp.zeros((part, cx), F32)
-        for z in range(planes):
+    before = [jnp.zeros((part, cx), F32)] * 2
+    copies = []
+    for z in range(planes):
+        q, row = z // quarter, z % quarter
+        outs = []
+        for h in range(2):
             at = (z + 1) * tall + h * part
             flat = z * tall + h * part
-            out, before = step(
+            out, before[h] = step(
                 f_ref, z, h, fz_ref[at : at + part, :], fy_ref[OFF + flat : OFF + flat + part, :],
-                fx_ref[flat : flat + part, :], before, ends(1, z, h),
+                fx_ref[flat : flat + part, :], before[h], ends(1, z, h),
             )
-            v_ref[at : at + part, :] = out
-    for z in range(planes):
-        out = v_ref[(z + 1) * tall : (z + 2) * tall, :]
-        q, at = z // quarter, z % quarter
-        body = out[OFF : OFF + cy].astype(BF16)
-        for x in range(4):
-            send_ref[(q // 2) * 8 + x * 2 + q % 2, at * cy : (at + 1) * cy, :] = body
-        rim_ref[q, 2 * at : 2 * at + 1, :] = out[OFF - 1 : OFF]
-        rim_ref[q, 2 * at + 1 : 2 * at + 2, :] = out[OFF + cy : OFF + cy + 1]
-    for q in range(4):
-        rims = rim_ref[q].astype(BF16)
-        for x in range(4):
-            send_ref[(q // 2) * 8 + x * 2 + q % 2, quarter * cy :, :] = rims
+            outs.append(out)
+        out = jnp.concatenate(outs, axis=0)
+        quarter_ref[q, row * cy : (row + 1) * cy, :] = out[OFF : OFF + cy].astype(BF16)
+        rim_ref[q, 2 * row : 2 * row + 1, :] = out[OFF - 1 : OFF]
+        rim_ref[q, 2 * row + 1 : 2 * row + 2, :] = out[OFF + cy : OFF + cy + 1]
+        if row == quarter - 1:
+            quarter_ref[q, quarter * cy :, :] = rim_ref[q].astype(BF16)
+            for x in range(4):
+                to = send_hbm.at[(q // 2) * 8 + x * 2 + q % 2]
+                copies.append(pltpu.make_async_copy(quarter_ref.at[q], to, sems.at[q, x]))
+                copies[-1].start()
+    for copy in copies:
+        copy.wait()
 
 
 def solve_x_kernel(block_ref, got_ref, x0_hbm, x1_hbm, x2_hbm, x3_hbm, out_ref, x0_ref, x1_ref, x2_ref, x3_ref, sems):
@@ -345,16 +354,18 @@
     cx = p.shape[2]
     shape = (2 * p.shape[0] + 16, cx)
     cy, order = y_inverse.shape
-    out = (kept(shape, F32),) * 2 + (kept(p.shape, F32),) * 2 + (kept(x_inverse.shape, BF16),)
+    out = (kept(shape, F32),) * 2 + (kept(p.shape, F32),) * 2 + (away_kept((cx + 16, order), BF16),)
     out += (away_kept((cy // 2, order), BF16),)
-    scratch = (pltpu.VMEM((cy // 2, order), BF16), pltpu.SemaphoreType.DMA((4,)))
-    return call(pack_x_kernel, out, (p, m, x_inverse, y_inverse), core, scratch, range(4), (5,))
-
-
-def pack_y(p, m, x_inverse, left, right):
-    cx, order = x_inverse.shape
-    out = (kept((7, p.shape[0], cx), F32),) * 2 + (kept((cx + 16, order), BF16),)
-    return call(pack_y_kernel, out, (p, m, x_inverse, left, right), scratch=(pltpu.VMEM((16, order), F32),))
+    scratch = (pltpu.VMEM((cx, order), BF16), pltpu.VMEM((cy // 2, order), BF16), pltpu.SemaphoreType.DMA((4,)))
+    return call(pack_x_kernel, out, (p, m, x_inverse, y_inverse), core, scratch, range(4), (4, 5))
+
+
+def pack_y(p, m, own_l, own_r, left, right, rows):
+    order = rows.shape[1]
+    out = (kept((7, p.shape[0], p.shape[2]), F32),) * 2 + (away_kept(rows.shape, BF16),)
+    scratch = (pltpu.VMEM((16, order), F32), pltpu.VMEM((16, order), BF16), pltpu.SemaphoreType.DMA(()))
+    args = (p, m, own_l, own_r, left, right, rows)
+    return call(pack_y_kernel, out, args, scratch=scratch, far=(6,), far_out=(2,), aliases={6: 2})
 
 
 def explicit(*args):
@@ -363,7 +374,7 @@
     lines = planes // 4 * cy + 16
     field = pltpu.VMEM(((planes + 2) * tall, cx), F32)
     out = (
-        kept((16, lines, cx), BF16),
+        away_kept((16, lines, cx), BF16),
         kept(((planes + 1) * tall, cx), F32),
         kept((planes * tall + OFF, cx), F32),
         kept((planes * tall, cx), F32),
@@ -371,8 +382,8 @@
     )
     scratch = (field, field, field, pltpu.VMEM((planes, cx), F32))
     scratch += (pltpu.VMEM((4, 16, cx), F32), pltpu.VMEM((cx, cx), F32))
-    scratch += (pltpu.VMEM((planes * tall + OFF, cx), F32),)
-    return call(explicit_kernel, out, args, scratch=scratch)
+    scratch += (pltpu.VMEM((planes * tall + OFF, cx), F32), pltpu.VMEM((4, lines, cx), BF16), pltpu.SemaphoreType.DMA((4, 4)))
+    return call(explicit_kernel, out, args, scratch=scratch, far_out=(0,))
 
 
 def solve_x(block, got, x_blocks):
@@ -415,10 +426,10 @@
 
     one = lambda v: v.reshape(1).astype(jnp.int32)
 
-    own_l, own_r, phase_field, mobility, x_own, y_part = pack_x(one(core), phase_field, mobility, x_inverse, y_inverse)
+    own_l, own_r, phase_field, mobility, rows, y_part = pack_x(one(core), phase_field, mobility, x_inverse, y_inverse)
     y_rows = lax.all_gather(y_part, ("z", "c"), axis=0, tiled=True)
     left, right = both_ways(own_l, own_r, GX)
-    to_up, to_down, rows = pack_y(phase_field, mobility, x_own, left, right)
+    to_up, to_down, rows = pack_y(phase_field, mobility, own_l, own_r, left, right, rows)
     up, down = both_ways(to_down, to_up, GY)
     rows_yl = lax.ppermute(rows, "yl", swap)
     x_blocks = (rows, lax.ppermute(rows, "c", swap), rows_yl, lax.ppermute(rows_yl, "c", swap))

time: 154 us -> 154 us (level)
  no operation moved by 1% of the time
where the time goes in v5:
time: 154 us
  blocking collectives  64.4 us (42%)
  starting transfers between devices  34 us (22%)
  waiting for transfers between devices  23.2 us (15%)
  Pallas kernels  17.9 us (12%)
  between operations  13.5 us (9%)
    all_to_all x1, blocking collectives, local(): mine = lax.all_to_all(updated, 'z', 0, 0, tiled=True).reshape(half, cx)  27.5 us
    all_to_all x1, blocking collectives, local(): out = lax.all_to_all(out, 'z', 0, 0, tiled=True)  25.4 us
    pallas_call x7, Pallas kernels, call(): pl.pallas_call(kernel, out_shape=out_shape, in_specs=[pl.BlockSpec(memory...  17.9 us
    all_to_all x1, waiting for transfers between devices, local(): got = lax.all_to_all(send, GX, 0, 0, tiled=True)  12.7 us
    all_to_all x1, blocking collectives, local(): back = lax.all_to_all(back, ('yl', 'c'), 0, 0, tiled=True)  11.5 us
    ppermute x2, starting transfers between devices, both_ways(): lax.ppermute(to_before, axis, [(j, i) for i, j in up])  10.9 us
    ppermute x1, starting transfers between devices, local(): rows_yl = lax.ppermute(rows, 'yl', swap)  6.26 us
    ppermute x2, starting transfers between devices, both_ways(): lax.ppermute(to_after, axis, up)  5.57 us
  transfers between devices with their start and end apart: 10, of which 5 were waited for; matrix products, arithmetic and copies ran while one was open for 0% of the time, Pallas kernels for 10%

profile of v5, /device:TPU:16, one launch (start us, length us, event | category | flops | bytes accessed | tf_op | source)
XLA Modules:
  0.0 154.0 jit_solution(3749234755884882983)
XLA Ops:
  6.5 0.0 all-gather.2.cloned.1.call-start
  6.5 2.3 %shard_map.46 = (f32[48,128]{1,0:T(8,128)S(1)}, f32[48,128]{1,0:T(8,128)S(1)}, f32[16,64,128]{2,1,0:T(8,128)S(1)}, f32[16,64,128]{2,1,0:T(8,128)S(1)}, bf16[144,...) custom-call(s32[1]{0:T(128)} %bitcast.1.core_ref, f32[16,64,128]{2,1,0:T(8,128)} %p_hbm.1, f32[16,64,128]{2,1,0:T(8,128)} %m_hbm.1, ...), custom_call_target="tpu_custom_call" | custom-call | tf_op jit(solution)/shard_map/pallas_call | solution.py:42
  8.9 0.0 all-gather.2.cloned.1.call-update
  8.9 1.7 %collective-permute-start = (f32[48,128]{1,0:T(8,128)S(1)}, f32[48,128]{1,0:T(8,128)S(1)}, u32[]{:S(2)}, u32[]{:S(2)}) collective-permute-start(f32[48,128]{1,0:T(8,128)S(1)} %get-tuple-element.27.own_r_ref), channel_id=1, source_target_pairs={{0,32},{32,64},{64,96},{96,128},{128,160},{160,192},{192,224},{224... | collective-permute-start | bytes 73736 | tf_op jit(solution)/shard_map/ppermute | solution.py:417
  10.7 1.3 collective-permute-start.1
  12.0 0.0 collective-permute-done.left_ref
  12.0 3.1 %collective-permute-done.1.right_ref = f32[48,128]{1,0:T(8,128)S(1)} collective-permute-done((f32[48,128]{1,0:T(8,128)S(1)}, f32[48,128]{1,0:T(8,128)S(1)}, u32[]{:S(2)}, u32[]{:S(2)}) %collective-permute-start.1) | collective-permute-done | bytes 24608 | tf_op jit(solution)/shard_map/ppermute | solution.py:417
  15.0 0.8 shard_map.47
  15.8 6.3 %collective-permute-start.5 = (bf16[144,2048]{1,0:T(8,128)(2,1)}, bf16[144,2048]{1,0:T(8,128)(2,1)}, u32[]{:S(2)}, u32[]{:S(2)}) collective-permute-start(bf16[144,2048]{1,0:T(8,128)(2,1)} %get-tuple-element.32.x0_hbm), channel_id=1, source_target_pairs={{0,256},{256,0},{1,257},{257,1},{2,258},{258,2},{3,259},{259,3},{4... | collective-permute-start | bytes 1769480 | tf_op jit(solution)/shard_map/ppermute | solution.py:434
  22.1 3.8 %collective-permute-start.2 = (f32[7,16,128]{2,1,0:T(8,128)S(1)}, f32[7,16,128]{2,1,0:T(8,128)S(1)}, u32[]{:S(2)}, u32[]{:S(2)}) collective-permute-start(f32[7,16,128]{2,1,0:T(8,128)S(1)} %get-tuple-element.29), channel_id=1, source_target_pairs={{0,1},{1,2},{2,3},{3,4},{4,5},{5,6},{6,7},{7,8},{8,9},{9,10},{10,1... | collective-permute-start | bytes 172040 | tf_op jit(solution)/shard_map/ppermute | solution.py:417
  25.9 9.6 %collective-permute-start.3 = (f32[7,16,128]{2,1,0:T(8,128)S(1)}, f32[7,16,128]{2,1,0:T(8,128)S(1)}, u32[]{:S(2)}, u32[]{:S(2)}) collective-permute-start(f32[7,16,128]{2,1,0:T(8,128)S(1)} %get-tuple-element.30), channel_id=1, source_target_pairs={{1,0},{2,1},{3,2},{4,3},{5,4},{6,5},{7,6},{8,7},{9,8},{10,9},{11,1... | collective-permute-start | bytes 172040 | tf_op jit(solution)/shard_map/ppermute | solution.py:417
  35.5 0.9 collective-permute-done.2.up_ref
  36.4 1.4 collective-permute-done.3.down_ref
  37.8 6.2 %shard_map.48 = (bf16[16,272,128]{2,1,0:T(8,128)(2,1)}, f32[1360,128]{1,0:T(8,128)S(1)}, f32[1288,128]{1,0:T(8,128)S(1)}, f32[1280,128]{1,0:T(8,128)S(1)}, f32[16,128]{1,0:T(8,128)S(1)}) custom-call(f32[16,64,128]{2,1,0:T(8,128)S(1)} %get-tuple-element.24.p_ref, f32[16,64,128]{2,1,0:T(8,128)S(1)} %get-tuple-element.25.m_ref, ...), custom_call_target="tpu_custom_call" | custom-call | tf_op jit(solution)/shard_map/pallas_call | solution.py:42
  44.0 4.6 %all-to-all-start = ((bf16[16,272,128]{2,1,0:T(8,128)(2,1)}), bf16[16,272,128]{2,1,0:T(8,128)(2,1)S(1)}, u32[]{:S(2)}, u32[]{:S(2)}) async-start(bf16[16,272,128]{2,1,0:T(8,128)(2,1)} %get-tuple-element.31), calls=%async_computation | async-start | bytes 2228224 | tf_op jit(solution)/shard_map/all_to_all | solution.py:438
  48.6 2.3 %collective-permute-start.4 = (bf16[144,2048]{1,0:T(8,128)(2,1)}, bf16[144,2048]{1,0:T(8,128)(2,1)}, u32[]{:S(2)}, u32[]{:S(2)}) collective-permute-start(bf16[144,2048]{1,0:T(8,128)(2,1)} %get-tuple-element.32.x0_hbm), channel_id=1, source_target_pairs={{0,32},{32,0},{1,33},{33,1},{2,34},{34,2},{3,35},{35,3},{4,36},{36... | collective-permute-start | bytes 1769480 | tf_op jit(solution)/shard_map/ppermute | solution.py:435
  50.9 0.0 collective-permute-done.5.x2_hbm
  51.0 2.0 %collective-permute-start.6 = (bf16[144,2048]{1,0:T(8,128)(2,1)}, bf16[144,2048]{1,0:T(8,128)(2,1)}, u32[]{:S(2)}, u32[]{:S(2)}) collective-permute-start(bf16[144,2048]{1,0:T(8,128)(2,1)} %collective-permute-done.5.x2_hbm), channel_id=1, source_target_pairs={{0,32},{32,0},{1,33},{33,1},{2,34},{34,2},{3,35},{35,3},{4,36},{36... | collective-permute-start | bytes 1769480 | tf_op jit(solution)/shard_map/ppermute | solution.py:435
  53.0 0.0 collective-permute-done.4.x1_hbm
  53.0 12.7 %all-to-all-done.got_ref = bf16[16,272,128]{2,1,0:T(8,128)(2,1)S(1)} async-done(((bf16[16,272,128]{2,1,0:T(8,128)(2,1)}), bf16[16,272,128]{2,1,0:T(8,128)(2,1)S(1)}, u32[]{:S(2)}, u32[]{:S(2)}) %all-to-all-start) | async-done | bytes 1114144 | tf_op jit(solution)/shard_map/all_to_all | solution.py:438
  65.8 0.0 collective-permute-done.6.x3_hbm
  65.8 4.0 %shard_map.49 = f32[4,272,128]{2,1,0:T(8,128)S(1)} custom-call(s32[1]{0:T(128)} %bitcast.2.block_ref, bf16[16,272,128]{2,1,0:T(8,128)(2,1)S(1)} %all-to-all-done.got_ref, bf16[144,2048]{1,0:T(8,128)(2,1)} %get-tuple-element.32.x0_hbm, bf16[144,2048]{1,0:T(8,128)(2,1)} %collective-permute-done.4.x1_hbm, bf16[144,2048]{1,0:T(8,128)(2,1)} %collective-permute-done.5.x2_hbm, ...), custom_call_target="tpu_custom_call" | custom-call | tf_op jit(solution)/shard_map/pallas_call | solution.py:42
  69.8 11.5 %all_to_all.20.back_ref = f32[4,272,128]{2,1,0:T(8,128)S(1)} all-to-all(f32[4,272,128]{2,1,0:T(8,128)S(1)} %shard_map.49), channel_id=1, replica_groups=mesh['yl'=2,'x'=4,'c'=2,'yh'=2,'z'=16] {'yl','c'}, dimensions={0} | all-to-all | bytes 1114112 | tf_op jit(solution)/shard_map/all_to_all | solution.py:440
  81.3 1.6 %shard_map.50 = bf16[16,64,128]{2,1,0:T(8,128)(2,1)S(1)} custom-call(f32[4,272,128]{2,1,0:T(8,128)S(1)} %all_to_all.20.back_ref, f32[1360,128]{1,0:T(8,128)S(1)} %get-tuple-element.33.fz_ref, f32[1288,128]{1,0:T(8,128)S(1)} %get-tuple-element.34.fy_ref, f32[1280,128]{1,0:T(8,128)S(1)} %get-tuple-element.35.fx_ref, f32[16,128]{1,0:T(8,128)S(1)} %get-tuple-element.36.edge_ref), custom_call_target="tpu_custom_call" | custom-call | tf_op jit(solution)/shard_map/pallas_call | solution.py:42
  82.9 27.5 %all_to_all.21 = bf16[16,64,128]{2,1,0:T(8,128)(2,1)S(1)} all-to-all(bf16[16,64,128]{2,1,0:T(8,128)(2,1)S(1)} %shard_map.50), channel_id=1, replica_groups=mesh['yl'=2,'x'=4,'c'=2,'yh'=2,'z'=16] {'z'}, dimensions={0} | all-to-all | bytes 524288 | tf_op jit(solution)/shard_map/all_to_all | solution.py:443
  110.4 0.0 all-gather.2.cloned.1.call-done.y_hbm
  110.4 2.4 %collective-permute-start.7 = (bf16[1024,128]{1,0:T(8,128)(2,1)S(1)}, bf16[1024,128]{1,0:T(8,128)(2,1)S(1)}, u32[]{:S(2)}, u32[]{:S(2)}) collective-permute-start(bf16[1024,128]{1,0:T(8,128)(2,1)S(1)} %bitcast.5), channel_id=1, source_target_pairs={{0,16},{16,0},{1,17},{17,1},{2,18},{18,2},{3,19},{19,3},{4,20},{20... | collective-permute-start | bytes 786440 | tf_op jit(solution)/shard_map/ppermute | solution.py:445
  112.8 2.3 %shard_map.51 = (f32[1024,128]{1,0:T(8,128)S(1)}, bf16[1024,1024]{1,0:T(8,128)(2,1)S(1)}) custom-call(s32[1]{0:T(128)} %bitcast.side_ref, bf16[1024,2048]{1,0:T(8,128)(2,1)} %all-gather.2.cloned.1.call-done.y_hbm, bf16[1024,128]{1,0:T(8,128)(2,1)S(1)} %bitcast.6), custom_call_target="tpu_custom_call" | custom-call | tf_op jit(solution)/shard_map/pallas_call | solution.py:42
  115.1 5.1 %collective-permute-done.7.u_ref = bf16[1024,128]{1,0:T(8,128)(2,1)S(1)} collective-permute-done((bf16[1024,128]{1,0:T(8,128)(2,1)S(1)}, bf16[1024,128]{1,0:T(8,128)(2,1)S(1)}, u32[]{:S(2)}, u32[]{:S(2)}) %collective-permute-start.7) | collective-permute-done | bytes 262176 | tf_op jit(solution)/shard_map/ppermute | solution.py:445
  120.2 0.7 shard_map.52
  120.9 25.4 %all_to_all.22 = bf16[16,64,128]{2,1,0:T(8,128)(2,1)S(1)} all-to-all(bf16[16,64,128]{2,1,0:T(8,128)(2,1)S(1)} %bitcast.7), channel_id=1, replica_groups=mesh['yl'=2,'x'=4,'c'=2,'yh'=2,'z'=16] {'z'}, dimensions={0} | all-to-all | bytes 524288 | tf_op jit(solution)/shard_map/all_to_all | solution.py:448
  146.3 0.8 convert_element_type.3
Async XLA Ops:
  6.5 103.9 %all-gather.2.cloned.1.call-start = ((), (), s32[]{:S(2)}) async-start(), calls=%async_computation.4 | async-start | bytes 4325376 | tf_op jit(solution)/shard_map/all_gather | solution.py:430
  8.9 3.1 %collective-permute-start = (f32[48,128]{1,0:T(8,128)S(1)}, f32[48,128]{1,0:T(8,128)S(1)}, u32[]{:S(2)}, u32[]{:S(2)}) collective-permute-start(f32[48,128]{1,0:T(8,128)S(1)} %get-tuple-element.27.own_r_ref), channel_id=1, source_target_pairs={{0,32},{32,64},{64,96},{96,128},{128,160},{160,192},{192,224},{224... | collective-permute-start | bytes 73736 | tf_op jit(solution)/shard_map/ppermute | solution.py:417
  10.7 4.4 %collective-permute-start.1 = (f32[48,128]{1,0:T(8,128)S(1)}, f32[48,128]{1,0:T(8,128)S(1)}, u32[]{:S(2)}, u32[]{:S(2)}) collective-permute-start(f32[48,128]{1,0:T(8,128)S(1)} %get-tuple-element.26.own_l_ref), channel_id=1, source_target_pairs={{32,0},{64,32},{96,64},{128,96},{160,128},{192,160},{224,192},{256... | collective-permute-start | bytes 73736 | tf_op jit(solution)/shard_map/ppermute | solution.py:417
  15.8 35.1 %collective-permute-start.5 = (bf16[144,2048]{1,0:T(8,128)(2,1)}, bf16[144,2048]{1,0:T(8,128)(2,1)}, u32[]{:S(2)}, u32[]{:S(2)}) collective-permute-start(bf16[144,2048]{1,0:T(8,128)(2,1)} %get-tuple-element.32.x0_hbm), channel_id=1, source_target_pairs={{0,256},{256,0},{1,257},{257,1},{2,258},{258,2},{3,259},{259,3},{4... | collective-permute-start | bytes 1769480 | tf_op jit(solution)/shard_map/ppermute | solution.py:434
  22.1 14.3 %collective-permute-start.2 = (f32[7,16,128]{2,1,0:T(8,128)S(1)}, f32[7,16,128]{2,1,0:T(8,128)S(1)}, u32[]{:S(2)}, u32[]{:S(2)}) collective-permute-start(f32[7,16,128]{2,1,0:T(8,128)S(1)} %get-tuple-element.29), channel_id=1, source_target_pairs={{0,1},{1,2},{2,3},{3,4},{4,5},{5,6},{6,7},{7,8},{8,9},{9,10},{10,1... | collective-permute-start | bytes 172040 | tf_op jit(solution)/shard_map/ppermute | solution.py:417
  25.9 11.8 %collective-permute-start.3 = (f32[7,16,128]{2,1,0:T(8,128)S(1)}, f32[7,16,128]{2,1,0:T(8,128)S(1)}, u32[]{:S(2)}, u32[]{:S(2)}) collective-permute-start(f32[7,16,128]{2,1,0:T(8,128)S(1)} %get-tuple-element.30), channel_id=1, source_target_pairs={{1,0},{2,1},{3,2},{4,3},{5,4},{6,5},{7,6},{8,7},{9,8},{10,9},{11,1... | collective-permute-start | bytes 172040 | tf_op jit(solution)/shard_map/ppermute | solution.py:417
  44.0 21.8 %all-to-all-start = ((bf16[16,272,128]{2,1,0:T(8,128)(2,1)}), bf16[16,272,128]{2,1,0:T(8,128)(2,1)S(1)}, u32[]{:S(2)}, u32[]{:S(2)}) async-start(bf16[16,272,128]{2,1,0:T(8,128)(2,1)} %get-tuple-element.31), calls=%async_computation | async-start | bytes 2228224 | tf_op jit(solution)/shard_map/all_to_all | solution.py:438
  48.6 4.4 %collective-permute-start.4 = (bf16[144,2048]{1,0:T(8,128)(2,1)}, bf16[144,2048]{1,0:T(8,128)(2,1)}, u32[]{:S(2)}, u32[]{:S(2)}) collective-permute-start(bf16[144,2048]{1,0:T(8,128)(2,1)} %get-tuple-element.32.x0_hbm), channel_id=1, source_target_pairs={{0,32},{32,0},{1,33},{33,1},{2,34},{34,2},{3,35},{35,3},{4,36},{36... | collective-permute-start | bytes 1769480 | tf_op jit(solution)/shard_map/ppermute | solution.py:435
  51.0 14.8 %collective-permute-start.6 = (bf16[144,2048]{1,0:T(8,128)(2,1)}, bf16[144,2048]{1,0:T(8,128)(2,1)}, u32[]{:S(2)}, u32[]{:S(2)}) collective-permute-start(bf16[144,2048]{1,0:T(8,128)(2,1)} %collective-permute-done.5.x2_hbm), channel_id=1, source_target_pairs={{0,32},{32,0},{1,33},{33,1},{2,34},{34,2},{3,35},{35,3},{4,36},{36... | collective-permute-start | bytes 1769480 | tf_op jit(solution)/shard_map/ppermute | solution.py:435
  110.4 9.8 %collective-permute-start.7 = (bf16[1024,128]{1,0:T(8,128)(2,1)S(1)}, bf16[1024,128]{1,0:T(8,128)(2,1)S(1)}, u32[]{:S(2)}, u32[]{:S(2)}) collective-permute-start(bf16[1024,128]{1,0:T(8,128)(2,1)S(1)} %bitcast.5), channel_id=1, source_target_pairs={{0,16},{16,0},{1,17},{17,1},{2,18},{18,2},{3,19},{19,3},{4,20},{20... | collective-permute-start | bytes 786440 | tf_op jit(solution)/shard_map/ppermute | solution.py:445
Sparse Core Ops, SparseCore 0:
  9.4 77.8 all-gather.1
